TPU v7x, 32 devices: a whole 2x2x4 slice. The times are simulated.
32 devices in a mesh: section: 2 (over x), dp: 8 (over z, y), tensor: 2 (over core).
Axes of the slice: x: 2, y: 2, z: 4, core: 2. Of those that a mesh axis runs over, the one named last changes fastest.
Arguments:
- images_in: bfloat16 [256, 32, 1152], P('tensor', 'dp'), may hold values from -6 to 6
- timesteps: int32 [32], P('dp'), may hold values from 0 to 999
- labels: int32 [32], P('dp'), may hold values from 0 to 1000
- counts: int32 [8], P('dp'), may hold values from 1 to 4, 21 in all
- label_table: bfloat16 [1001, 1152], replicated, may hold values from -6 to 6
- ada_weight: bfloat16 [2, 1152, 6912], P('section', None, 'tensor'), may hold values from -0.1875 to 0.1875
- ada_bias: bfloat16 [2, 6912], P('section', 'tensor'), may hold values from -3 to 3
- qkv_weight: bfloat16 [2, 1152, 3, 1152], P('section', None, None, 'tensor'), may hold values from -0.1875 to 0.1875
- qkv_bias: bfloat16 [2, 2, 1152], P('section', None, 'tensor'), may hold values from -3 to 3
- out_weight: bfloat16 [2, 1152, 1152], P('section', 'tensor'), may hold values from -1.5 to 1.5
- out_bias: bfloat16 [2, 1152], P('section'), may hold values from -6 to 6
- up_weight: bfloat16 [2, 1152, 4608], P('section', None, 'tensor'), may hold values from -0.1875 to 0.1875
- up_bias: bfloat16 [2, 4608], P('section', 'tensor'), may hold values from -3 to 3
- down_weight: bfloat16 [2, 4608, 1152], P('section', 'tensor'), may hold values from -0.09375 to 0.09375
- down_bias: bfloat16 [2, 1152], P('section'), may hold values from -6 to 6
- out_cotangent: bfloat16 [256, 32, 1152], P('tensor', 'dp'), may hold values from -6 to 6
Outputs:
- layer_out: bfloat16 [2, 256, 32, 1152], P('section', 'tensor', 'dp')
- in_grad: bfloat16 [2, 256, 32, 1152], P('section', 'tensor', 'dp')
- cond_grad: float32 [32, 1152], P('dp')
- table_grad: float32 [1001, 1152], replicated
- grad_ada_weight: float32 [2, 1152, 6912], P('section', None, 'tensor')
- grad_ada_bias: float32 [2, 6912], P('section', 'tensor')
- grad_qkv_weight: float32 [2, 1152, 3, 1152], P('section', None, None, 'tensor')
- grad_qkv_bias: float32 [2, 2, 1152], P('section', None, 'tensor')
- grad_out_weight: float32 [2, 1152, 1152], P('section', 'tensor')
- grad_out_bias: float32 [2, 1152], P('section')
- grad_up_weight: float32 [2, 1152, 4608], P('section', None, 'tensor')
- grad_up_bias: float32 [2, 4608], P('section', 'tensor')
- grad_down_weight: float32 [2, 4608, 1152], P('section', 'tensor')
- grad_down_bias: float32 [2, 1152], P('section')
Inputs may be any that keep to these rules, and one draw needn't show every extreme that they name: `counts`: the groups hold 21 images in all, and some group holds 4; a group's images fill its first slots.
All inputs are finite; a program needn't handle non-finite values.
Results may differ from a plain program's by a relative error of at most 0.035.
Values may be sent and summed in bfloat16 or wider, within the bound.
No kernel may reach another device: no remote copies, remote signals or barrier semaphores. Data moves between devices by JAX's collectives and lax.ppermute only.
A program may use at most 320 MiB of HBM per device.

v0:
```python
import math

import jax
import jax.numpy as jnp
from jax import lax
from jax.sharding import PartitionSpec as P

D = 1152
HEADS = 16
MICRO = 4


eps_norm = 1e-06


def from_behind(array, axis, by):
    peers = lax.axis_size(axis)
    pairs = [(i, i + by) for i in range(peers) if 0 <= i + by < peers]
    return lax.ppermute(array, axis, pairs)


def time_embed(timesteps, width_all):
    half_width = width_all // 2
    frequencies = jnp.exp(
        -math.log(10000.0) * jnp.arange(half_width, dtype=jnp.float32) / half_width
    )
    angles = timesteps.astype(jnp.float32)[:, None] * frequencies[None, :]
    return jnp.concatenate([jnp.cos(angles), jnp.sin(angles)], axis=1)


def modulate(row_block, shift_rows, scale_rows):
    centered = row_block - jnp.mean(row_block, axis=-1, keepdims=True)
    variance = jnp.mean(centered * centered, axis=-1, keepdims=True)
    return centered * lax.rsqrt(variance + eps_norm) * (1.0 + scale_rows[None]) + shift_rows[None]


def gelu_tanh(values):
    return jax.nn.gelu(values, approximate=True)


def widen(row_block):
    return lax.all_gather(row_block, "tensor", axis=0, tiled=True)


def narrow(left_rows, weight):

    def term_rows(start_row, row_count):
        return jnp.einsum("nbk,kd->nbd", left_rows, weight, preferred_element_type=jnp.float32)

    return lax.psum_scatter(
        term_rows(
            jnp.int32(0), left_rows.shape[0] // lax.axis_size("tensor") * lax.axis_size("tensor")
        ),
        "tensor",
        scatter_dimension=0,
        tiled=True,
    )


def narrow_back(grad_block, weight):

    def term_rows(start_row, row_count):
        return jnp.einsum("nbk,dk->nbd", grad_block, weight, preferred_element_type=jnp.float32)

    return lax.psum_scatter(
        term_rows(
            jnp.int32(0), grad_block.shape[0] // lax.axis_size("tensor") * lax.axis_size("tensor")
        ).astype(jnp.bfloat16),
        "tensor",
        scatter_dimension=0,
        tiled=True,
    ).astype(jnp.float32)


def fold_back(grad_rows, left_rows, weight):
    piece_rows = lax.all_gather(grad_rows, "tensor", axis=0, tiled=True)
    weight_grad = jnp.einsum(
        "nbk,nbd->kd", left_rows, piece_rows, preferred_element_type=jnp.float32
    )
    back_rows = jnp.einsum("nbd,kd->nbk", piece_rows, weight, preferred_element_type=jnp.float32)
    return (weight_grad, back_rows)


def project_qkv(full_one, qkv_w, qkv_b):
    width_local = qkv_w.shape[-1]
    flat_weight = qkv_w.reshape(qkv_w.shape[0], 3 * width_local)
    mixed_rows = jnp.einsum(
        "nbd,dk->nbk", full_one, flat_weight, preferred_element_type=jnp.float32
    )
    bias_full = jnp.stack([qkv_b[0], jnp.zeros_like(qkv_b[0]), qkv_b[1]]).astype(jnp.float32)
    return (
        mixed_rows.reshape(full_one.shape[0], full_one.shape[1], 3, width_local)
        + bias_full[None, None]
    )


def attend(mixed_qkv):
    seq_len, batch_len, width_local = (mixed_qkv.shape[0], mixed_qkv.shape[1], mixed_qkv.shape[3])
    head_size = D // HEADS
    heads_here = width_local // head_size
    shaped = mixed_qkv.astype(jnp.bfloat16).reshape(seq_len, batch_len, 3, heads_here, head_size)
    queries, keys_b, values_b = (shaped[:, :, 0], shaped[:, :, 1], shaped[:, :, 2])
    scores = jnp.einsum(
        "nbhe,mbhe->bhnm", queries, keys_b, preferred_element_type=jnp.float32
    ) * head_size ** (-0.5)
    attn_probs = jax.nn.softmax(scores, axis=-1)
    attn_probs_b = attn_probs.astype(jnp.bfloat16)
    mixed_rows = jnp.einsum(
        "bhnm,mbhe->nbhe", attn_probs_b, values_b, preferred_element_type=jnp.float32
    )
    attended = mixed_rows.astype(jnp.bfloat16).reshape(seq_len, batch_len, width_local)
    return ((queries, keys_b, values_b, attn_probs, attn_probs_b), attended)


def layer_forward(rows_in, mod_rows, valid_rows, params):
    qkv_w, qkv_b, out_w, out_b, up_w, up_b, down_w, down_b = params
    shift_one, scale_one, gate_one, shift_two, scale_two, gate_two = jnp.split(mod_rows, 6, axis=1)
    full_one = widen(modulate(rows_in, shift_one, scale_one).astype(jnp.bfloat16))
    attn_parts, attended = attend(project_qkv(full_one, qkv_w, qkv_b))
    attn_out = narrow(attended, out_w) + out_b.astype(jnp.float32)[None, None]
    middle = rows_in + gate_one[None] * attn_out
    full_two = widen(modulate(middle, shift_two, scale_two).astype(jnp.bfloat16))
    pre_act = (
        jnp.einsum("nbd,df->nbf", full_two, up_w, preferred_element_type=jnp.float32)
        + up_b.astype(jnp.float32)[None, None]
    )
    act_b = gelu_tanh(pre_act).astype(jnp.bfloat16)
    mlp_out = narrow(act_b, down_w) + down_b.astype(jnp.float32)[None, None]
    result = (middle + gate_two[None] * mlp_out) * valid_rows[None, :, None]
    return (result, (full_one, full_two, attn_out, mlp_out, pre_act, attn_parts, attended))


def mlp_backward(rows_in, mod_rows, valid_rows, grad_rows, saved_rows, params):
    qkv_w, qkv_b, out_w, out_b, up_w, up_b, down_w, down_b = params
    full_one, full_two, attn_out, mlp_out, pre_act, attn_parts, attended = saved_rows
    shift_one, scale_one, gate_one, shift_two, scale_two, gate_two = jnp.split(mod_rows, 6, axis=1)
    out_grad = grad_rows * valid_rows[None, :, None]
    middle = rows_in + gate_one[None] * attn_out
    act_rows, gelu_back = jax.vjp(gelu_tanh, pre_act)
    act_b = act_rows.astype(jnp.bfloat16)
    gate_two_grad = jnp.sum(out_grad * mlp_out, axis=0)
    down_in = (out_grad * gate_two[None]).astype(jnp.bfloat16)
    down_b_part = jnp.sum(down_in, axis=(0, 1), dtype=jnp.float32)
    down_w_grad, act_grad = fold_back(down_in, act_b, down_w)
    pre_grad = gelu_back(act_grad)[0].astype(jnp.bfloat16)
    up_w_grad = jnp.einsum("nbd,nbf->df", full_two, pre_grad, preferred_element_type=jnp.float32)
    up_b_grad = jnp.sum(pre_grad, axis=(0, 1), dtype=jnp.float32)
    normed_grad = narrow_back(pre_grad, up_w)
    _, norm_back = jax.vjp(modulate, middle, shift_two, scale_two)
    middle_norm, shift_two_grad, scale_two_grad = norm_back(normed_grad)
    middle_grad = out_grad + middle_norm
    return (
        middle_grad,
        (up_w_grad, up_b_grad, down_w_grad),
        down_b_part,
        (shift_two_grad, scale_two_grad, gate_two_grad),
    )


def attention_backward(rows_in, mod_rows, middle_grad, saved_rows, params):
    qkv_w, qkv_b, out_w, out_b, up_w, up_b, down_w, down_b = params
    full_one, full_two, attn_out, mlp_out, pre_act, attn_parts, attended = saved_rows
    queries, keys_b, values_b, attn_probs, attn_probs_b = attn_parts
    shift_one, scale_one, gate_one, shift_two, scale_two, gate_two = jnp.split(mod_rows, 6, axis=1)
    gate_one_grad = jnp.sum(middle_grad * attn_out, axis=0)
    out_in = (middle_grad * gate_one[None]).astype(jnp.bfloat16)
    out_b_part = jnp.sum(out_in, axis=(0, 1), dtype=jnp.float32)
    out_w_grad, attended_grad = fold_back(out_in, attended, out_w)
    seq_len, batch_len, width_local = attended.shape
    head_size = D // HEADS
    mixed_grad = attended_grad.astype(jnp.bfloat16).reshape(
        seq_len, batch_len, width_local // head_size, head_size
    )
    values_grad = jnp.einsum(
        "bhnm,nbhe->mbhe", attn_probs_b, mixed_grad, preferred_element_type=jnp.float32
    )
    probs_grad = jnp.einsum(
        "nbhe,mbhe->bhnm", mixed_grad, values_b, preferred_element_type=jnp.float32
    )
    scores_grad = attn_probs * (
        probs_grad - jnp.sum(probs_grad * attn_probs, axis=-1, keepdims=True)
    )
    scores_grad = scores_grad.astype(jnp.bfloat16)
    queries_grad = jnp.einsum(
        "bhnm,mbhe->nbhe", scores_grad, keys_b, preferred_element_type=jnp.float32
    ) * head_size ** (-0.5)
    keys_grad = jnp.einsum(
        "bhnm,nbhe->mbhe", scores_grad, queries, preferred_element_type=jnp.float32
    ) * head_size ** (-0.5)
    qkv_grad = jnp.stack(
        [
            queries_grad.reshape(seq_len, batch_len, width_local),
            keys_grad.reshape(seq_len, batch_len, width_local),
            values_grad.reshape(seq_len, batch_len, width_local),
        ],
        axis=2,
    ).astype(jnp.bfloat16)
    qkv_sums = jnp.sum(qkv_grad, axis=(0, 1), dtype=jnp.float32)
    qkv_b_grad = jnp.stack([qkv_sums[0], qkv_sums[2]])
    qkv_flat = qkv_grad.reshape(seq_len, batch_len, 3 * width_local)
    qkv_w_grad = jnp.einsum(
        "nbd,nbk->dk", full_one, qkv_flat, preferred_element_type=jnp.float32
    ).reshape(qkv_w.shape)
    normed_grad = narrow_back(qkv_flat, qkv_w.reshape(qkv_w.shape[0], 3 * width_local))
    _, norm_back = jax.vjp(modulate, rows_in, shift_one, scale_one)
    rows_norm, shift_one_grad, scale_one_grad = norm_back(normed_grad)
    return (
        middle_grad + rows_norm,
        (qkv_w_grad, qkv_b_grad, out_w_grad),
        out_b_part,
        (shift_one_grad, scale_one_grad, gate_one_grad),
    )


def shards(
    images_in,
    timesteps,
    labels,
    counts,
    label_table,
    ada_weight,
    ada_bias,
    qkv_weight,
    qkv_bias,
    out_weight,
    out_bias,
    up_weight,
    up_bias,
    down_weight,
    down_bias,
    out_cotangent,
):
    section_no = lax.axis_index("section")
    is_first = section_no == 0
    slot_count = images_in.shape[1]
    per_micro = slot_count // MICRO
    local_len = images_in.shape[0]
    params = (
        qkv_weight[0],
        qkv_bias[0],
        out_weight[0],
        out_bias[0],
        up_weight[0],
        up_bias[0],
        down_weight[0],
        down_bias[0],
    )

    def by_section(first_val, later_val):
        return jnp.where(is_first, first_val, later_val)

    def micro_rows(table_rows, micro_no):
        return lax.dynamic_slice_in_dim(table_rows, micro_no * per_micro, per_micro, 0)

    condition = jnp.take(label_table, labels, axis=0).astype(jnp.float32) + time_embed(timesteps, D)
    silu_cond, silu_back = jax.vjp(jax.nn.silu, condition)
    silu_b = silu_cond.astype(jnp.bfloat16)
    mod_local = (
        jnp.dot(silu_b, ada_weight[0], preferred_element_type=jnp.float32)
        + ada_bias[0].astype(jnp.float32)[None]
    )
    mod_all = lax.all_gather(mod_local, "tensor", axis=1, tiled=True)
    valid_all = (jnp.arange(slot_count, dtype=jnp.int32) < counts[0]).astype(jnp.float32)
    received = jnp.zeros((local_len, per_micro, images_in.shape[2]), jnp.bfloat16)
    kept_inputs, kept_saved, outputs = ([], [], [])
    for turn_no in range(MICRO + 1):
        micro_no = jnp.clip(jnp.where(is_first, turn_no, turn_no - 1), 0, MICRO - 1)
        mod_rows = micro_rows(mod_all, micro_no)
        valid_rows = micro_rows(valid_all, micro_no)
        if turn_no < MICRO:
            own_rows = images_in[:, turn_no * per_micro : (turn_no + 1) * per_micro]
        else:
            own_rows = jnp.zeros_like(received)
        layer_in = jnp.where(is_first, own_rows, received)
        result, saved_rows = layer_forward(
            layer_in.astype(jnp.float32), mod_rows, valid_rows, params
        )
        result_b = result.astype(jnp.bfloat16)
        kept_inputs.append(layer_in)
        kept_saved.append(saved_rows)
        outputs.append(result_b)
        if turn_no < MICRO:
            received = from_behind(result_b, "section", 1)
    layer_out = jnp.concatenate(
        [by_section(outputs[position], outputs[position + 1]) for position in range(MICRO)], axis=1
    )[None]
    attn_acc = (
        jnp.zeros(params[0].shape, jnp.float32),
        jnp.zeros(params[1].shape, jnp.float32),
        jnp.zeros(params[2].shape, jnp.float32),
    )
    mlp_acc = (
        jnp.zeros(params[4].shape, jnp.float32),
        jnp.zeros(params[5].shape, jnp.float32),
        jnp.zeros(params[6].shape, jnp.float32),
    )
    out_b_acc = jnp.zeros((D,), jnp.float32)
    down_b_acc = jnp.zeros((D,), jnp.float32)
    mod_grad_all = jnp.zeros(mod_all.shape, jnp.float32)
    received_grad = jnp.zeros((local_len, per_micro, images_in.shape[2]), jnp.float32)
    input_grads = []
    for turn_no in range(MICRO + 1):
        micro_no = jnp.clip(jnp.where(is_first, turn_no - 1, turn_no), 0, MICRO - 1)
        mod_rows = micro_rows(mod_all, micro_no)
        valid_rows = micro_rows(valid_all, micro_no)
        if turn_no < MICRO:
            own_grad = out_cotangent[:, turn_no * per_micro : (turn_no + 1) * per_micro].astype(
                jnp.float32
            )
        else:
            own_grad = jnp.zeros_like(received_grad)
        grad_rows = jnp.where(is_first, received_grad, own_grad)
        early_turn = max(turn_no - 1, 0)
        later_turn = min(turn_no + 1, MICRO)
        layer_in = by_section(kept_inputs[early_turn], kept_inputs[later_turn]).astype(jnp.float32)
        _, saved_rows = layer_forward(layer_in, mod_rows, valid_rows, params)
        middle_grad, mlp_grads, down_b_part, mlp_mod = mlp_backward(
            layer_in, mod_rows, valid_rows, grad_rows, saved_rows, params
        )
        mlp_acc = jax.tree.map(
            lambda first_item, later_item: first_item + later_item, mlp_acc, mlp_grads
        )
        down_b_acc = down_b_acc + down_b_part
        rows_grad, attn_grads, out_b_part, attn_mod = attention_backward(
            layer_in, mod_rows, middle_grad, saved_rows, params
        )
        attn_acc = jax.tree.map(
            lambda first_item, later_item: first_item + later_item, attn_acc, attn_grads
        )
        out_b_acc = out_b_acc + out_b_part
        mod_part = jnp.concatenate(
            [attn_mod[0], attn_mod[1], attn_mod[2], mlp_mod[0], mlp_mod[1], mlp_mod[2]], axis=1
        )
        current = micro_rows(mod_grad_all, micro_no)
        mod_grad_all = lax.dynamic_update_slice_in_dim(
            mod_grad_all, current + mod_part, micro_no * per_micro, 0
        )
        input_grads.append(rows_grad.astype(jnp.bfloat16))
        if turn_no < MICRO:
            received_grad = from_behind(rows_grad.astype(jnp.bfloat16), "section", -1).astype(
                rows_grad.dtype
            )
    in_grad = jnp.concatenate(
        [by_section(input_grads[position + 1], input_grads[position]) for position in range(MICRO)],
        axis=1,
    )[None]
    mod_grad_cols = lax.psum_scatter(
        mod_grad_all.astype(jnp.bfloat16), "tensor", scatter_dimension=1, tiled=True
    )
    ada_w_grad = jnp.einsum("sd,sk->dk", silu_b, mod_grad_cols, preferred_element_type=jnp.float32)
    ada_b_grad = jnp.sum(mod_grad_cols, axis=0, dtype=jnp.float32)
    silu_grad = jnp.einsum(
        "sk,dk->sd", mod_grad_cols, ada_weight[0], preferred_element_type=jnp.float32
    )
    cond_part = silu_back(silu_grad)[0]
    cond_grad = lax.psum(cond_part, ("section", "tensor"))
    onehot = (labels[:, None] == jnp.arange(label_table.shape[0], dtype=jnp.int32)[None]).astype(
        jnp.float32
    )
    table_part = jnp.dot(
        onehot.T, cond_grad, precision=lax.Precision.HIGHEST, preferred_element_type=jnp.float32
    )
    out_b_sum, down_b_sum = lax.psum((out_b_acc, down_b_acc), ("dp", "tensor"))
    (
        qkv_w_sum,
        qkv_b_sum,
        out_w_sum,
        up_w_sum,
        up_b_sum,
        down_w_sum,
        ada_w_sum,
        ada_b_sum,
        table_grad,
    ) = (
        lax.psum(attn_acc[0].astype(jnp.bfloat16), "dp").astype(jnp.float32),
        lax.psum(attn_acc[1].astype(jnp.bfloat16), "dp").astype(jnp.float32),
        lax.psum(attn_acc[2].astype(jnp.bfloat16), "dp").astype(jnp.float32),
        lax.psum(mlp_acc[0].astype(jnp.bfloat16), "dp").astype(jnp.float32),
        lax.psum(mlp_acc[1].astype(jnp.bfloat16), "dp").astype(jnp.float32),
        lax.psum(mlp_acc[2].astype(jnp.bfloat16), "dp").astype(jnp.float32),
        lax.psum(ada_w_grad.astype(jnp.bfloat16), "dp").astype(jnp.float32),
        lax.psum(ada_b_grad.astype(jnp.bfloat16), "dp").astype(jnp.float32),
        lax.psum(table_part.astype(jnp.bfloat16), "dp").astype(jnp.float32),
    )
    return (
        layer_out,
        in_grad,
        cond_grad,
        table_grad,
        ada_w_sum[None],
        ada_b_sum[None],
        qkv_w_sum[None],
        qkv_b_sum[None],
        out_w_sum[None],
        out_b_sum[None],
        up_w_sum[None],
        up_b_sum[None],
        down_w_sum[None],
        down_b_sum[None],
    )


def solution(mesh):
    placed = (
        P("tensor", "dp", None),
        P("dp"),
        P("dp"),
        P("dp"),
        P(),
        P("section", None, "tensor"),
        P("section", "tensor"),
        P("section", None, None, "tensor"),
        P("section", None, "tensor"),
        P("section", "tensor", None),
        P("section", None),
        P("section", None, "tensor"),
        P("section", "tensor"),
        P("section", "tensor", None),
        P("section", None),
        P("tensor", "dp", None),
    )
    return jax.shard_map(
        shards,
        mesh=mesh,
        in_specs=placed,
        out_specs=(
            P("section", "tensor", "dp", None),
            P("section", "tensor", "dp", None),
            P("dp", None),
            P(),
            P("section", None, "tensor"),
            P("section", "tensor"),
            P("section", None, None, "tensor"),
            P("section", None, "tensor"),
            P("section", "tensor", None),
            P("section", None),
            P("section", None, "tensor"),
            P("section", "tensor"),
            P("section", "tensor", None),
            P("section", None),
        ),
        check_vma=False,
    )
```

profile of v0, /device:TPU:0, one launch (start us, length us, event | category | flops | bytes accessed | tf_op | source)
XLA Modules:
  0.0 1655.8 jit_solution(8306120888916237872)
XLA Ops:
  33.8 10.7 reduce-scatter.34.cloned.1.call-done
  50.5 8.5 fusion.145
  60.5 8.5 reduce-scatter.36.cloned.1.call-done
  92.9 10.7 reduce-scatter.38.cloned.1.call-done
  109.8 8.6 fusion.148
  118.5 10.0 reduce-scatter.40.cloned.1.call-done
  135.4 6.7 collective-permute-done.1
  154.9 10.3 reduce-scatter.42.cloned.1.call-done
  171.4 8.6 fusion.151
  180.1 10.0 reduce-scatter.44.cloned.1.call-done
  196.9 6.7 collective-permute-done.2
  214.9 10.7 reduce-scatter.46.cloned.1.call-done
  231.8 8.6 fusion.154
  240.5 10.0 reduce-scatter.48.cloned.1.call-done
  373.7 9.3 reduce-scatter.56.cloned.1.call-done
  401.9 6.5 reduce-scatter.58.cloned.1.call-done
  434.3 8.5 reduce-scatter.62.cloned.1.call-done
  495.0 8.5 reduce-scatter.68.cloned.1.call-done
  567.2 9.6 reduce-scatter.90.cloned.1.call-done
  617.3 6.8 fusion.616
  645.8 10.4 convolution_add_fusion.7
  684.2 7.0 convolution_add_fusion.5
  704.3 9.8 collective-permute-done.7
  732.4 8.4 fusion.14
  740.8 8.7 fusion.13
  776.2 8.5 fusion.157
  794.8 15.2 fusion.142
  816.3 10.7 psum.84
  842.7 38.4 %all-reduce = (f32[1,1152]{1,0:T(1,128)}, f32[1,1152]{1,0:T(1,128)}) all-reduce(f32[1,1152]{1,0:T(1,128)S(1)} %broadcast_in_dim.198, f32[1,1152]{1,0:T(1,128)S(1)} %broadcast_in_dim.205), channel_id=1, replica_groups=mesh['section'=2,'dp'=8,'tensor'=2] {'dp','tensor'}, use_global_device_ids=true, to_apply=%region_164.165 | all-reduce | flops 2304 | bytes 18432 | tf_op jit(solution)/shard_map/psum | solution.py:363
  886.8 36.4 %all-reduce.1 = (bf16[1,3456]{1,0:T(2,128)(2,1)S(1)}, bf16[1,2,576]{2,1,0:T(2,128)(2,1)S(1)}, bf16[1,2304]{1,0:T(2,128)(2,1)S(1)}) all-reduce(bf16[1,3456]{1,0:T(2,128)(2,1)S(1)} %broadcast_in_dim.190, bf16[1,2,576]{2,1,0:T(2,128)(2,1)S(1)} %fusion.732, ...), channel_id=1, replica_groups=mesh['section'=2,'dp'=8,'tensor'=2] {'dp'}, use_global_device_ids=true, to_apply=%region_150.151 | all-reduce | flops 6912 | bytes 27648 | tf_op jit(solution)/shard_map/psum | solution.py:382
  929.0 691.3 %all-reduce.5.cloned.1.call-done = (bf16[1001,1152]{1,0:T(8,128)(2,1)}, bf16[1,1152,3456]{2,1,0:T(8,128)(2,1)}, bf16[1,1152,3,576]{1,3,2,0:T(8,128)(2,1)}, bf16[...) async-done(((bf16[1001,1152]{1,0:T(8,128)(2,1)}, bf16[1,1152,3456]{2,1,0:T(8,128)(2,1)}, ...) | async-done | bytes 26194192 | tf_op jit(solution)/shard_map/psum | solution.py:383
  1620.3 10.3 broadcast_in_dim.189
  (1153 shorter events, 603.4 us)
Async XLA Ops:
  7.2 37.3 %reduce-scatter.34.cloned.1.call-start = ((), (), s32[]{:S(2)}) async-start(), calls=%async_computation.31 | async-start | bytes 1769472 | tf_op jit(solution)/shard_map/reduce_scatter | solution.py:50
  33.0 36.0 %reduce-scatter.36.cloned.1.call-start = ((), (), s32[]{:S(2)}) async-start(), calls=%async_computation.32 | async-start | bytes 1769472 | tf_op jit(solution)/shard_map/reduce_scatter | solution.py:50
  59.1 44.5 %reduce-scatter.38.cloned.1.call-start = ((), (), s32[]{:S(2)}) async-start(), calls=%async_computation.33 | async-start | bytes 1769472 | tf_op jit(solution)/shard_map/reduce_scatter | solution.py:50
  92.8 35.6 %reduce-scatter.40.cloned.1.call-start = ((), (), s32[]{:S(2)}) async-start(), calls=%async_computation.34 | async-start | bytes 1769472 | tf_op jit(solution)/shard_map/reduce_scatter | solution.py:50
  118.4 46.8 %reduce-scatter.42.cloned.1.call-start = ((), (), s32[]{:S(2)}) async-start(), calls=%async_computation.35 | async-start | bytes 1769472 | tf_op jit(solution)/shard_map/reduce_scatter | solution.py:50
  154.4 35.6 %reduce-scatter.44.cloned.1.call-start = ((), (), s32[]{:S(2)}) async-start(), calls=%async_computation.36 | async-start | bytes 1769472 | tf_op jit(solution)/shard_map/reduce_scatter | solution.py:50
  180.0 45.6 %reduce-scatter.46.cloned.1.call-start = ((), (), s32[]{:S(2)}) async-start(), calls=%async_computation.37 | async-start | bytes 1769472 | tf_op jit(solution)/shard_map/reduce_scatter | solution.py:50
  214.9 35.6 %reduce-scatter.48.cloned.1.call-start = ((), (), s32[]{:S(2)}) async-start(), calls=%async_computation.38 | async-start | bytes 1769472 | tf_op jit(solution)/shard_map/reduce_scatter | solution.py:50
  240.5 88.8 %reduce-scatter.50.cloned.1.call-start = ((), (), s32[]{:S(2)}) async-start(), calls=%async_computation.39 | async-start | bytes 1769472 | tf_op jit(solution)/shard_map/reduce_scatter | solution.py:50
  275.0 75.1 %reduce-scatter.54.cloned.1.call-start = ((), (), s32[]{:S(2)}) async-start(), calls=%async_computation.41 | async-start | bytes 1769472 | tf_op jit(solution)/shard_map/reduce_scatter | solution.py:50
  289.5 60.6 %reduce-scatter.60.cloned.1.call-start = ((), (), s32[]{:S(2)}) async-start(), calls=%async_computation.44 | async-start | bytes 1769472 | tf_op jit(solution)/shard_map/reduce_scatter | solution.py:50
  304.0 46.1 %reduce-scatter.66.cloned.1.call-start = ((), (), s32[]{:S(2)}) async-start(), calls=%async_computation.47 | async-start | bytes 1769472 | tf_op jit(solution)/shard_map/reduce_scatter | solution.py:50
  316.7 33.4 %reduce-scatter.78.cloned.1.call-start = ((), (), s32[]{:S(2)}) async-start(), calls=%async_computation.53 | async-start | bytes 1769472 | tf_op jit(solution)/shard_map/reduce_scatter | solution.py:50
  329.2 25.0 %reduce-scatter.72.cloned.1.call-start = ((), (), s32[]{:S(2)}) async-start(), calls=%async_computation.50 | async-start | bytes 1769472 | tf_op jit(solution)/shard_map/reduce_scatter | solution.py:50
  343.6 39.4 %reduce-scatter.56.cloned.1.call-start = ((), (), s32[]{:S(2)}) async-start(), calls=%async_computation.42 | async-start | bytes 884736 | tf_op jit(solution)/shard_map/reduce_scatter | solution.py:65
  373.7 34.7 %reduce-scatter.58.cloned.1.call-start = ((), (), s32[]{:S(2)}) async-start(), calls=%async_computation.43 | async-start | bytes 884736 | tf_op jit(solution)/shard_map/reduce_scatter | solution.py:65
  399.0 43.8 %reduce-scatter.62.cloned.1.call-start = ((), (), s32[]{:S(2)}) async-start(), calls=%async_computation.45 | async-start | bytes 884736 | tf_op jit(solution)/shard_map/reduce_scatter | solution.py:65
  434.3 34.0 %reduce-scatter.64.cloned.1.call-start = ((), (), s32[]{:S(2)}) async-start(), calls=%async_computation.46 | async-start | bytes 884736 | tf_op jit(solution)/shard_map/reduce_scatter | solution.py:65
  458.9 44.6 %reduce-scatter.68.cloned.1.call-start = ((), (), s32[]{:S(2)}) async-start(), calls=%async_computation.48 | async-start | bytes 884736 | tf_op jit(solution)/shard_map/reduce_scatter | solution.py:65
  494.9 33.9 %reduce-scatter.70.cloned.1.call-start = ((), (), s32[]{:S(2)}) async-start(), calls=%async_computation.49 | async-start | bytes 884736 | tf_op jit(solution)/shard_map/reduce_scatter | solution.py:65
  519.5 44.5 %reduce-scatter.74.cloned.1.call-start = ((), (), s32[]{:S(2)}) async-start(), calls=%async_computation.51 | async-start | bytes 884736 | tf_op jit(solution)/shard_map/reduce_scatter | solution.py:65
  555.5 21.3 %reduce-scatter.90.cloned.1.call-start = ((), (), s32[]{:S(2)}) async-start(), calls=%async_computation.59 | async-start | bytes 1769472 | tf_op jit(solution)/shard_map/reduce_scatter | solution.py:50
  561.6 136.4 %reduce-scatter.76.cloned.1.call-start = ((), (), s32[]{:S(2)}) async-start(), calls=%async_computation.52 | async-start | bytes 884736 | tf_op jit(solution)/shard_map/reduce_scatter | solution.py:65
  589.8 114.5 %reduce-scatter.88.cloned.1.call-start = ((), (), s32[]{:S(2)}) async-start(), calls=%async_computation.58 | async-start | bytes 1769472 | tf_op jit(solution)/shard_map/reduce_scatter | solution.py:50
  596.2 108.1 %reduce-scatter.86.cloned.1.call-start = ((), (), s32[]{:S(2)}) async-start(), calls=%async_computation.57 | async-start | bytes 1769472 | tf_op jit(solution)/shard_map/reduce_scatter | solution.py:50
  602.6 101.7 %reduce-scatter.84.cloned.1.call-start = ((), (), s32[]{:S(2)}) async-start(), calls=%async_computation.56 | async-start | bytes 1769472 | tf_op jit(solution)/shard_map/reduce_scatter | solution.py:50
  609.6 94.8 %reduce-scatter.92.cloned.1.call-start = ((), (), s32[]{:S(2)}) async-start(), calls=%async_computation.60 | async-start | bytes 1769472 | tf_op jit(solution)/shard_map/reduce_scatter | solution.py:50
  633.2 116.2 %reduce-scatter.80.cloned.1.call-start = ((), (), s32[]{:S(2)}) async-start(), calls=%async_computation.54 | async-start | bytes 884736 | tf_op jit(solution)/shard_map/reduce_scatter | solution.py:65
  732.1 52.5 %reduce-scatter.82.cloned.1.call-start = ((), (), s32[]{:S(2)}) async-start(), calls=%async_computation.55 | async-start | bytes 884736 | tf_op jit(solution)/shard_map/reduce_scatter | solution.py:65
  764.7 45.3 %reduce-scatter.94.cloned.1.call-start = ((), (), s32[]{:S(2)}) async-start(), calls=%async_computation.61 | async-start | bytes 2654208
  791.2 133.8 %reduce-scatter.52.cloned.1.call-start = ((), (), s32[]{:S(2)}) async-start(), calls=%async_computation.40 | async-start | bytes 1769472 | tf_op jit(solution)/shard_map/reduce_scatter | solution.py:50
  794.7 825.6 %all-reduce.5.cloned.1.call-start = ((), (), s32[]{:S(2)}) async-start(), calls=%async_computation.62 | async-start | bytes 52420608 | tf_op jit(solution)/shard_map/psum | solution.py:383
  (339 other events, 4760.4 us)
Sparse Core Ops, SparseCore 0:
  33.1 11.2 reduce-scatter.33
  59.2 9.8 reduce-scatter.35
  93.0 10.5 reduce-scatter.37
  118.6 9.8 reduce-scatter.39
  154.5 10.5 reduce-scatter.41
  180.2 9.8 reduce-scatter.43
  215.0 10.5 reduce-scatter.45
  240.6 9.8 reduce-scatter.47
  275.1 10.5 reduce-scatter.49
  289.6 10.5 reduce-scatter.53
  304.1 10.4 reduce-scatter.59
  317.4 9.9 reduce-scatter.65
  329.6 10.2 reduce-scatter.77
  343.7 10.5 reduce-scatter.71
  373.8 9.1 reduce-scatter.55
  399.1 9.2 reduce-scatter.57
  434.4 8.4 reduce-scatter.61
  459.0 9.1 reduce-scatter.63
  495.1 8.3 reduce-scatter.67
  519.7 9.1 reduce-scatter.69
  555.6 8.3 reduce-scatter.73
  567.0 9.8 reduce-scatter.89
  589.9 9.2 reduce-scatter.75
  601.4 9.8 reduce-scatter.87
  613.5 9.8 reduce-scatter.85
  626.1 9.8 reduce-scatter.83
  638.7 9.8 reduce-scatter.91
  732.2 8.3 reduce-scatter.79
  764.8 8.3 reduce-scatter.81
  791.3 9.5 reduce-scatter.93
  803.7 9.8 reduce-scatter.51
  836.5 783.6 all-reduce.4
where the time goes:
time: 1670 us; the launch traced here: 1660 us
  waiting for transfers between devices  886 us (53%)
  matrix products  369 us (22%)
  other arithmetic  162 us (10%)
  blocking collectives  156 us (9%)
  local copies, waits for them, and re-layouts  40.4 us (2%)
  starting transfers between devices  23.8 us (1%)
  between operations  19.4 us (1%)
    psum x1, waiting for transfers between devices, shards(): lax.psum(table_part.astype(jnp.bfloat16), 'dp').astype(jnp.float32)  691 us
    reduce_scatter x20, waiting for transfers between devices, narrow(): lax.psum_scatter(term_rows(jnp.int32(0), left_rows.shape[0] // lax.axis_s...  94.7 us
    dot_general x20, matrix products, term_rows(): jnp.einsum('nbk,kd->nbd', left_rows, weight, preferred_element_type=jnp.f...  87.4 us
    ppermute x8, waiting for transfers between devices, from_behind(): return lax.ppermute(array, axis, pairs)  51.4 us
    reduce_scatter x10, waiting for transfers between devices, narrow_back(): lax.psum_scatter(term_rows(jnp.int32(0), grad_block.shape[0] // lax.axis_...  48.3 us
    all_gather x20, blocking collectives, widen(): return lax.all_gather(row_block, 'tensor', axis=0, tiled=True)  46 us
    dot_general x5, matrix products, mlp_backward(): jnp.einsum('nbd,nbf->df', full_two, pre_grad, preferred_element_type=jnp....  38.7 us
    psum x1, blocking collectives, shards(): out_b_sum, down_b_sum = lax.psum((out_b_acc, down_b_acc), ('dp', 'tensor'))  38.4 us
  transfers between devices with their start and end apart: 40, of which 26 were waited for; matrix products, arithmetic and copies ran while one was open for 17% of the time, Pallas kernels for 0%

commit v1 on v0

v1 whole, which is shorter than its diff:
```python
import functools
import math
import jax
import jax.numpy as jnp
from jax import lax
from jax.experimental import pallas as pl
from jax.experimental.pallas import tpu as pltpu
from jax.sharding import PartitionSpec as P

HEADS = 16
eps_norm = 1e-06
BF, F32 = jnp.bfloat16, jnp.float32
ANY = pl.BlockSpec(memory_space=pl.ANY)
VM = pl.BlockSpec(memory_space=pltpu.VMEM)
LIMIT = 60 * 1024 * 1024
ROOT = math.sqrt(2.0 / math.pi)
CUBE = 0.044715


def nt(left, right):
    return lax.dot_general(left, right, (((1,), (1,)), ((), ())), preferred_element_type=F32)


def tn(left, right):
    return lax.dot_general(left, right, (((0,), (0,)), ((), ())), preferred_element_type=F32)


def nn(left, right):
    return jnp.dot(left, right, preferred_element_type=F32)


def norm_parts(rows):
    centered = rows - jnp.mean(rows, axis=-1, keepdims=True)
    inverse = lax.rsqrt(jnp.mean(centered * centered, axis=-1, keepdims=True) + eps_norm)
    return centered * inverse, inverse


def windows(width, size):
    spans = []
    for head in range(width // size):
        low, high = head * size, (head + 1) * size
        spans.append((low, high, low // 128 * 128, min(width, (high + 127) // 128 * 128)))
    return spans


def head_mask(span):
    low, high, start, stop = span
    lanes = lax.broadcasted_iota(jnp.int32, (1, stop - start), 1) + start
    return (lanes >= low) & (lanes < high)


class Copies:
    def __init__(self, sems):
        self.sems, self.used = sems, 0

    def start(self, source, target):
        copy = pltpu.make_async_copy(source, target, self.sems.at[self.used])
        self.used += 1
        copy.start()
        return copy


def soft(scores, scale):
    top = jnp.max(scores, axis=-1, keepdims=True)
    powers = jnp.exp2((scores - top) * (scale * math.log2(math.e)))
    return powers * (1.0 / jnp.sum(powers, axis=-1, keepdims=True))


def layer_kernel(chunks, index_ref, x_ref, mod_ref, bqv_ref, bup_ref, bod_ref,
                 wqo, wqt, woo, wot, wuo, wut, wdo, wdt, *rest):
    extra = len(rest) - 28
    rest = rest[extra:]
    (y_ref, xs, h1s, qkvo, qkvt, atts, aos, h2s, preo, pret, acto, actt, mos,
     wq, wo, wu, wd, h1, qkv, att, attf, ao, h2, pre, act, mo, mid, sems) = rest
    copies = Copies(sems)
    img = index_ref[0]
    qkv_in = [copies.start(wqo, wq.at[0]), copies.start(wqt, wq.at[1])]
    out_in = [copies.start(woo, wo.at[0]), copies.start(wot, wo.at[1])]
    up_in = [copies.start(wuo, wu.at[0]), copies.start(wut, wu.at[1])]
    down_in = [copies.start(wdo, wd.at[0]), copies.start(wdt, wd.at[1])]
    pending = [copies.start(x_ref, xs.at[img])]
    half = att.shape[2]
    size = 2 * half // HEADS
    scale = size ** (-0.5)
    mods = mod_ref[img]
    rows = x_ref[...].astype(F32)
    normed, _ = norm_parts(rows)
    h1[...] = (normed * (1.0 + mods[1:2]) + mods[0:1]).astype(BF)
    pending.append(copies.start(h1, h1s.at[img]))
    for copy in qkv_in:
        copy.wait()

    def project(part, carry):
        side, kind = part // 3, part % 3
        mixed = nn(h1[...], wq[side, kind])
        qkv[side, kind] = (mixed + bqv_ref[pl.ds(part, 1)]).astype(BF)
        return carry

    lax.fori_loop(0, 6, project, 0)
    pending += [copies.start(qkv.at[0], qkvo.at[img]), copies.start(qkv.at[1], qkvt.at[img])]

    def attend(side, carry):
        attf[...] = jnp.zeros_like(attf)
        for span in windows(half, size):
            part = slice(span[2], span[3])
            mask = head_mask(span)
            zero = jnp.zeros((), BF)
            queries = jnp.where(mask, qkv[side, 0, :, part], zero)
            scores = nt(queries, qkv[side, 1, :, part])
            probs = soft(scores, scale).astype(BF)
            attf[:, part] += nn(probs, jnp.where(mask, qkv[side, 2, :, part], zero))
        att[side] = attf[...].astype(BF)
        return carry

    lax.fori_loop(0, 2, attend, 0)
    pending.append(copies.start(att, atts.at[img]))
    for copy in out_in:
        copy.wait()
    ao[...] = nn(att[0], wo[0]) + nn(att[1], wo[1]) + bod_ref[0:1]
    pending.append(copies.start(ao, aos.at[img]))
    mid[...] = rows + mods[2:3] * ao[...]
    normed, _ = norm_parts(mid[...])
    h2[...] = (normed * (1.0 + mods[4:5]) + mods[3:4]).astype(BF)
    pending.append(copies.start(h2, h2s.at[img]))
    mo[...] = jnp.broadcast_to(bod_ref[1:2], mo.shape)
    for copy in up_in:
        copy.wait()
    for copy in down_in:
        copy.wait()
    step = bup_ref.shape[1] // chunks

    def mlp(part, carry):
        side, place = part // chunks, part % chunks
        spot = pl.ds(pl.multiple_of(place * step, 128), step)
        values = nn(h2[...], wu[side, :, spot]) + bup_ref[pl.ds(side, 1), spot]
        pre[side, :, spot] = values.astype(BF)
        inner = jnp.tanh(values * (ROOT + ROOT * CUBE * values * values))
        acted = (0.5 * values * (1.0 + inner)).astype(BF)
        act[side, :, spot] = acted
        mo[...] += nn(acted, wd[side, spot, :])
        return carry

    lax.fori_loop(0, 2 * chunks, mlp, 0)
    pending += [copies.start(pre.at[0], preo.at[img]), copies.start(pre.at[1], pret.at[img]),
                copies.start(act.at[0], acto.at[img]), copies.start(act.at[1], actt.at[img]),
                copies.start(mo, mos.at[img])]
    y_ref[...] = (mods[6:7] * (mid[...] + mods[5:6] * mo[...])).astype(BF)
    for copy in pending:
        copy.wait()


def layer_call(index, x, mods, bqv, bup, bod, weights, saved, images):
    tokens, width = x.shape
    half, hidden = width // 2, bup.shape[1]
    chunks = 3 if hidden % 384 == 0 else 1
    sd = jax.ShapeDtypeStruct
    outs = (
        sd((tokens, width), BF),
        sd((images, tokens, width), BF),
        sd((images, tokens, width), BF),
        sd((images, 3, tokens, half), BF),
        sd((images, 3, tokens, half), BF),
        sd((images, 2, tokens, half), BF),
        sd((images, tokens, width), F32),
        sd((images, tokens, width), BF),
        sd((images, tokens, hidden), BF),
        sd((images, tokens, hidden), BF),
        sd((images, tokens, hidden), BF),
        sd((images, tokens, hidden), BF),
        sd((images, tokens, width), F32),
    )
    saved = tuple(saved) if saved is not None else ()
    aliases = {14 + i: 1 + i for i in range(len(saved))}
    scratch = [
        pltpu.VMEM((2, 3, width, half), BF),
        pltpu.VMEM((2, half, width), BF),
        pltpu.VMEM((2, width, hidden), BF),
        pltpu.VMEM((2, hidden, width), BF),
        pltpu.VMEM((tokens, width), BF),
        pltpu.VMEM((2, 3, tokens, half), BF),
        pltpu.VMEM((2, tokens, half), BF),
        pltpu.VMEM((tokens, half), F32),
        pltpu.VMEM((tokens, width), F32),
        pltpu.VMEM((tokens, width), BF),
        pltpu.VMEM((2, tokens, hidden), BF),
        pltpu.VMEM((2, tokens, hidden), BF),
        pltpu.VMEM((tokens, width), F32),
        pltpu.VMEM((tokens, width), F32),
        pltpu.SemaphoreType.DMA((32,)),
    ]
    return pl.pallas_call(
        functools.partial(layer_kernel, chunks),
        out_shape=outs,
        in_specs=[pl.BlockSpec(memory_space=pltpu.SMEM)] + [VM] * 5 + [ANY] * (8 + len(saved)),
        out_specs=[VM] + [ANY] * 12,
        scratch_shapes=scratch,
        input_output_aliases=aliases,
        compiler_params=pltpu.CompilerParams(vmem_limit_bytes=LIMIT),
        cost_estimate=pl.CostEstimate(flops=2 * tokens * width * (6 * half * 2 + 4 * hidden), bytes_accessed=4 * width * (4 * half + 2 * hidden), transcendentals=0),
        name="layer",
    )(index, x, mods, bqv, bup, bod, *weights, *saved)


def mlp_back_kernel(chunks, index_ref, g_ref, mod_ref, xs, aos, mos, preo, pret, wuo, wut, wdo, wdt, *rest):
    rest = rest[len(rest) - 18:]
    (mg_ref, sum_ref, bu_ref, dis, pgo, pgt, wu, wd, x, ao, mo, pre, di, pg, ng, og, sems, _) = rest
    copies = Copies(sems)
    img = index_ref[0]
    first = [copies.start(mos.at[img], mo)]
    second = [copies.start(preo.at[img], pre.at[0]), copies.start(pret.at[img], pre.at[1]),
              copies.start(wdo, wd.at[0]), copies.start(wdt, wd.at[1]),
              copies.start(wuo, wu.at[0]), copies.start(wut, wu.at[1])]
    third = [copies.start(xs.at[img], x), copies.start(aos.at[img], ao)]
    mods = mod_ref[img]
    og[...] = g_ref[...].astype(F32) * mods[6:7]
    di[...] = (og[...] * mods[5:6]).astype(BF)
    pending = [copies.start(di, dis.at[img])]
    for copy in first:
        copy.wait()
    sum_ref[2:3] = jnp.sum(og[...] * mo[...], axis=0, keepdims=True)
    sum_ref[3:4] = jnp.sum(di[...].astype(F32), axis=0, keepdims=True)
    ng[...] = jnp.zeros_like(ng)
    for copy in second:
        copy.wait()
    step = pre.shape[2] // chunks

    def mlp(part, carry):
        side, place = part // chunks, part % chunks
        spot = pl.ds(pl.multiple_of(place * step, 128), step)
        values = pre[side, :, spot].astype(F32)
        grad = nt(di[...], wd[side, spot, :])
        square = values * values
        inner = jnp.tanh(values * (ROOT + ROOT * CUBE * square))
        slope = 0.5 * (1.0 + inner) + 0.5 * values * (1.0 - inner * inner) * (ROOT + 3.0 * ROOT * CUBE * square)
        graded = (grad * slope).astype(BF)
        pg[side, :, spot] = graded
        bu_ref[pl.ds(side, 1), spot] = jnp.sum(graded.astype(F32), axis=0, keepdims=True)
        ng[...] += nt(graded, wu[side, :, spot])
        return carry

    lax.fori_loop(0, 2 * chunks, mlp, 0)
    pending += [copies.start(pg.at[0], pgo.at[img]), copies.start(pg.at[1], pgt.at[img])]
    for copy in third:
        copy.wait()
    normed, inverse = norm_parts(x[...].astype(F32) + mods[2:3] * ao[...])
    sum_ref[0:1] = jnp.sum(ng[...], axis=0, keepdims=True)
    sum_ref[1:2] = jnp.sum(ng[...] * normed, axis=0, keepdims=True)
    dn = ng[...] * (1.0 + mods[4:5])
    mg_ref[...] = og[...] + inverse * (
        dn - jnp.mean(dn, axis=-1, keepdims=True) - normed * jnp.mean(dn * normed, axis=-1, keepdims=True))
    for copy in pending:
        copy.wait()


def mlp_back_call(index, grad, mods, saved, weights, kept, images):
    xs, aos, mos, preo, pret = saved
    tokens, width = grad.shape
    hidden = preo.shape[2]
    chunks = 3 if hidden % 384 == 0 else 1
    sd = jax.ShapeDtypeStruct
    kept = tuple(kept) if kept is not None else ()
    aliases = {12 + i: 3 + i for i in range(len(kept))}
    scratch = [
        pltpu.VMEM((2, width, hidden), BF),
        pltpu.VMEM((2, hidden, width), BF),
        pltpu.VMEM((tokens, width), BF),
        pltpu.VMEM((tokens, width), F32),
        pltpu.VMEM((tokens, width), F32),
        pltpu.VMEM((2, tokens, hidden), BF),
        pltpu.VMEM((tokens, width), BF),
        pltpu.VMEM((2, tokens, hidden), BF),
        pltpu.VMEM((tokens, width), F32),
        pltpu.VMEM((tokens, width), F32),
        pltpu.SemaphoreType.DMA((16,)),
        pltpu.VMEM((8, 128), F32),
    ]
    return pl.pallas_call(
        functools.partial(mlp_back_kernel, chunks),
        out_shape=(
            sd((tokens, width), F32), sd((8, width), F32), sd((2, hidden), F32),
            sd((images, tokens, width), BF), sd((images, tokens, hidden), BF), sd((images, tokens, hidden), BF)),
        in_specs=[pl.BlockSpec(memory_space=pltpu.SMEM)] + [VM] * 2 + [ANY] * (9 + len(kept)),
        out_specs=[VM] * 3 + [ANY] * 3,
        scratch_shapes=scratch,
        input_output_aliases=aliases,
        compiler_params=pltpu.CompilerParams(vmem_limit_bytes=LIMIT),
        cost_estimate=pl.CostEstimate(flops=2 * tokens * width * 4 * hidden, bytes_accessed=4 * width * 2 * hidden, transcendentals=0),
        name="mlp_back",
    )(index, grad, mods, xs, aos, mos, preo, pret, *weights, *kept)


def attn_back_kernel(index_ref, mg_ref, mod_ref, xs, aos, qkvo, qkvt, wqo, wqt, woo, wot, *rest):
    rest = rest[len(rest) - 17:]
    (rg_ref, sum_ref, bqv_ref, ois, qgo, qgt, wq, wo, x, ao, qkv, oi, qg, da, acc, ng, sems) = rest
    copies = Copies(sems)
    img = index_ref[0]
    first = [copies.start(aos.at[img], ao)]
    second = [copies.start(woo, wo.at[0]), copies.start(wot, wo.at[1])]
    third = [copies.start(qkvo.at[img], qkv.at[0]), copies.start(qkvt.at[img], qkv.at[1])]
    fourth = [copies.start(wqo, wq.at[0]), copies.start(wqt, wq.at[1])]
    fifth = [copies.start(xs.at[img], x)]
    half = wo.shape[1]
    size = 2 * half // HEADS
    scale = size ** (-0.5)
    mods = mod_ref[img]
    oi[...] = (mg_ref[...] * mods[2:3]).astype(BF)
    pending = [copies.start(oi, ois.at[img])]
    sum_ref[3:4] = jnp.sum(oi[...].astype(F32), axis=0, keepdims=True)
    for copy in first + second + third:
        copy.wait()
    sum_ref[2:3] = jnp.sum(mg_ref[...] * ao[...], axis=0, keepdims=True)

    def attend(side, carry):
        da[...] = nt(oi[...], wo[side]).astype(BF)
        for kind in range(3):
            acc[kind] = jnp.zeros_like(acc[kind])
        for span in windows(half, size):
            part = slice(span[2], span[3])
            mask = head_mask(span)
            zero = jnp.zeros((), BF)
            queries = jnp.where(mask, qkv[side, 0, :, part], zero)
            keys = jnp.where(mask, qkv[side, 1, :, part], zero)
            outer = jnp.where(mask, da[:, part], zero)
            probs = soft(nt(queries, keys), scale)
            grads = nt(outer, qkv[side, 2, :, part])
            inner = jnp.sum(grads * probs, axis=-1, keepdims=True)
            spread = (probs * (grads - inner)).astype(BF)
            acc[2, :, part] += tn(probs.astype(BF), outer)
            acc[0, :, part] += nn(spread, keys)
            acc[1, :, part] += tn(spread, queries)
        for kind in range(3):
            factor = 1.0 if kind == 2 else scale
            qg[side, kind] = (acc[kind] * factor).astype(BF)
        return carry

    lax.fori_loop(0, 2, attend, 0)
    pending += [copies.start(qg.at[0, 0], qgo.at[0, img]), copies.start(qg.at[0, 1], qgo.at[1, img]),
                copies.start(qg.at[0, 2], qgo.at[2, img]), copies.start(qg.at[1, 0], qgt.at[0, img]),
                copies.start(qg.at[1, 1], qgt.at[1, img]), copies.start(qg.at[1, 2], qgt.at[2, img])]
    ng[...] = jnp.zeros_like(ng)
    for copy in fourth:
        copy.wait()

    def project(part, carry):
        side, kind = part // 3, part % 3
        graded = qg[side, kind]
        bqv_ref[pl.ds(part, 1)] = jnp.sum(graded.astype(F32), axis=0, keepdims=True)
        ng[...] += nt(graded, wq[side, kind])
        return carry

    lax.fori_loop(0, 6, project, 0)
    for copy in fifth:
        copy.wait()
    normed, inverse = norm_parts(x[...].astype(F32))
    sum_ref[0:1] = jnp.sum(ng[...], axis=0, keepdims=True)
    sum_ref[1:2] = jnp.sum(ng[...] * normed, axis=0, keepdims=True)
    dn = ng[...] * (1.0 + mods[1:2])
    rg_ref[...] = (mg_ref[...] + inverse * (
        dn - jnp.mean(dn, axis=-1, keepdims=True) - normed * jnp.mean(dn * normed, axis=-1, keepdims=True))).astype(BF)
    for copy in pending:
        copy.wait()


def attn_back_call(index, grad, mods, saved, weights, kept, images):
    xs, aos, qkvo, qkvt = saved
    tokens, width = grad.shape
    half = width // 2
    sd = jax.ShapeDtypeStruct
    kept = tuple(kept) if kept is not None else ()
    aliases = {11 + i: 3 + i for i in range(len(kept))}
    scratch = [
        pltpu.VMEM((2, 3, width, half), BF),
        pltpu.VMEM((2, half, width), BF),
        pltpu.VMEM((tokens, width), BF),
        pltpu.VMEM((tokens, width), F32),
        pltpu.VMEM((2, 3, tokens, half), BF),
        pltpu.VMEM((tokens, width), BF),
        pltpu.VMEM((2, 3, tokens, half), BF),
        pltpu.VMEM((tokens, half), BF),
        pltpu.VMEM((3, tokens, half), F32),
        pltpu.VMEM((tokens, width), F32),
        pltpu.SemaphoreType.DMA((16,)),
    ]
    return pl.pallas_call(
        attn_back_kernel,
        out_shape=(
            sd((tokens, width), BF), sd((8, width), F32), sd((8, half), F32),
            sd((images, tokens, width), BF), sd((3, images, tokens, half), BF), sd((3, images, tokens, half), BF)),
        in_specs=[pl.BlockSpec(memory_space=pltpu.SMEM)] + [VM] * 2 + [ANY] * (8 + len(kept)),
        out_specs=[VM] * 3 + [ANY] * 3,
        scratch_shapes=scratch,
        input_output_aliases=aliases,
        compiler_params=pltpu.CompilerParams(vmem_limit_bytes=LIMIT),
        cost_estimate=pl.CostEstimate(flops=2 * tokens * width * 12 * half, bytes_accessed=4 * width * 4 * half, transcendentals=0),
        name="attn_back",
    )(index, grad, mods, xs, aos, qkvo, qkvt, *weights, *kept)


def time_embed(timesteps, width_all):
    half_width = width_all // 2
    frequencies = jnp.exp(-math.log(10000.0) * jnp.arange(half_width, dtype=F32) / half_width)
    angles = timesteps.astype(F32)[:, None] * frequencies[None, :]
    return jnp.concatenate([jnp.cos(angles), jnp.sin(angles)], axis=1)


def swap(array):
    return lax.ppermute(array, "tensor", [(0, 1), (1, 0)])


def ring_order(peers):
    order = list(range(0, peers, 2)) + list(range(1, peers, 2))[::-1]
    place = [order.index(peer) for peer in range(peers)]
    ahead = [(order[i], order[(i + 1) % peers]) for i in range(peers)]
    return place, ahead, [(b, a) for a, b in ahead]


def ring_sum(terms):
    peers = lax.axis_size("dp")
    place, ahead, behind = ring_order(peers)
    here = jnp.asarray(place, jnp.int32)[lax.axis_index("dp")]
    count, width = terms.shape
    part = count // (2 * peers)
    blocks = terms.reshape(2, peers, part, width)
    total = jnp.zeros((2, peers, part, width), F32)
    lanes = ((ahead, 1), (behind, -1))

    def block(side, number):
        return lax.dynamic_slice(blocks, (side, number % peers, 0, 0), (1, 1, part, width))

    moving = [block(side, here) for side in range(2)]
    for step in range(1, peers):
        for side, (pairs, sign) in enumerate(lanes):
            came = lax.ppermute(moving[side], "dp", pairs)
            mine = block(side, here - sign * step)
            moving[side] = (came.astype(F32) + mine.astype(F32)).astype(BF)
    for step in range(peers):
        for side, (pairs, sign) in enumerate(lanes):
            owner = (here - sign * (peers - 1 + step)) % peers
            total = lax.dynamic_update_slice(total, moving[side].astype(F32), (side, owner, 0, 0))
            if step < peers - 1:
                moving[side] = lax.ppermute(moving[side], "dp", pairs)
    return total.reshape(count, width)


def folded(other, own):
    came = swap(other.astype(BF))
    return (own + came.astype(F32)).astype(BF)


def outer(left, right):
    return jnp.einsum("btk,btd->kd", left, right, preferred_element_type=F32)


def outers(left, right):
    return jnp.einsum("jbtk,btd->jkd", left, right, preferred_element_type=F32)


def shards(images_in, timesteps, labels, counts, label_table, ada_weight, ada_bias, qkv_weight,
           qkv_bias, out_weight, out_bias, up_weight, up_bias, down_weight, down_bias, out_cotangent):
    is_first = lax.axis_index("section") == 0
    core = lax.axis_index("tensor")
    slots = images_in.shape[1]
    images = slots // 2
    width = images_in.shape[2]
    hidden = up_weight.shape[2]
    half = out_weight.shape[1]

    def by_section(first_val, later_val):
        return jnp.where(is_first, first_val, later_val)

    def by_core(first_val, later_val):
        return jnp.where(core == 0, first_val, later_val)

    def mine(array, axis):
        return lax.dynamic_slice_in_dim(array, core * images, images, axis)

    def others(array, axis):
        return lax.dynamic_slice_in_dim(array, (1 - core) * images, images, axis)

    def in_order(own, came, axis):
        return by_core(jnp.concatenate([own, came], axis), jnp.concatenate([came, own], axis))

    def whole_images(rows):
        came = swap(others(rows, 1))
        return jnp.moveaxis(jnp.concatenate([mine(rows, 1), came], axis=0), 1, 0)

    def split_images(rows):
        local = rows.shape[1] // 2
        came = swap(rows[:, local:])
        return jnp.moveaxis(in_order(rows[:, :local], came, 0), 0, 1)[None]

    qkv_own = jnp.moveaxis(qkv_weight[0], 1, 0)
    w_qkv = (qkv_own, swap(qkv_own))
    w_out = (out_weight[0], swap(out_weight[0]))
    w_up = (up_weight[0], swap(up_weight[0]))
    w_down = (down_weight[0], swap(down_weight[0]))
    weights = (*w_qkv, *w_out, *w_up, *w_down)

    condition = jnp.take(label_table, labels, axis=0).astype(F32) + time_embed(timesteps, width)
    silu_cond, silu_back = jax.vjp(jax.nn.silu, condition)
    silu_b = silu_cond.astype(BF)
    mod_local = (
        jnp.dot(silu_b, ada_weight[0], preferred_element_type=F32) + ada_bias[0].astype(F32)[None]
    )
    modulation = in_order(mine(mod_local, 0), swap(others(mod_local, 0)), 1).reshape(images, 6, width)
    slot_no = core * images + jnp.arange(images, dtype=jnp.int32)
    valid = (slot_no < counts[0]).astype(F32)
    mods = jnp.concatenate(
        [modulation, jnp.broadcast_to(valid[:, None, None], (images, 2, width))], axis=1
    )
    pair_bias = jnp.concatenate([qkv_bias[0, 0], qkv_bias[0, 1], up_bias[0]])[None]
    pair_bias = jnp.concatenate([pair_bias, swap(pair_bias)], axis=0).astype(F32)
    zero_row = jnp.zeros((half,), F32)
    bqv = jnp.stack([
        pair_bias[0, :half], zero_row, pair_bias[0, half : 2 * half],
        pair_bias[1, :half], zero_row, pair_bias[1, half : 2 * half], zero_row, zero_row])
    bup = pair_bias[:, 2 * half :]
    bod = jnp.concatenate([out_bias, down_bias], axis=0).astype(F32)

    rows_in = whole_images(images_in)
    cotangent = whole_images(out_cotangent)

    saved, received, results = (None, None, [])
    for turn in range(images + 1):
        early, later = min(turn, images - 1), max(turn - 1, 0)
        index = by_section(jnp.int32(early), jnp.int32(later)).reshape(1)
        layer_in = rows_in[early] if received is None else by_section(rows_in[early], received)
        answer = layer_call(index, layer_in, mods, bqv, bup, bod, weights, saved, images)
        result, saved = answer[0], answer[1:]
        results.append(result)
        if turn < images:
            received = lax.ppermute(result, "section", [(0, 1)])
    layer_out = split_images(
        jnp.stack([by_section(results[i], results[i + 1]) for i in range(images)])
    )
    xs, h1s, qkvo, qkvt, atts, aos, h2s, preo, pret, acto, actt, mos = saved

    mlp_kept, attn_kept, received, turns = (None, None, None, [])
    for turn in range(images + 1):
        early, later = min(turn, images - 1), max(turn - 1, 0)
        index = by_section(jnp.int32(later), jnp.int32(early)).reshape(1)
        grad = cotangent[early] if received is None else by_section(received, cotangent[early])
        answer = mlp_back_call(
            index, grad, mods, (xs, aos, mos, preo, pret), (*w_up, *w_down), mlp_kept, images
        )
        middle_grad, mlp_sums, up_sums, mlp_kept = answer[0], answer[1], answer[2], answer[3:]
        answer = attn_back_call(
            index, middle_grad, mods, (xs, aos, qkvo, qkvt), (*w_qkv, *w_out), attn_kept, images
        )
        row_grad, attn_sums, qkv_sums, attn_kept = answer[0], answer[1], answer[2], answer[3:]
        turns.append((row_grad, mlp_sums, up_sums, attn_sums, qkv_sums))
        if turn < images:
            received = lax.ppermute(row_grad, "section", [(1, 0)])
    by_image = [
        jax.tree.map(by_section, turns[i + 1], turns[i]) if i < images - 1 else turns[i + 1]
        for i in range(images)
    ]
    in_grad = split_images(jnp.stack([item[0] for item in by_image]))
    down_ins, pre_grads_o, pre_grads_t = mlp_kept
    out_ins, qkv_grads_o, qkv_grads_t = attn_kept

    down_w = folded(outer(actt, down_ins), outer(acto, down_ins))
    up_w = folded(outer(h2s, pre_grads_t), outer(h2s, pre_grads_o))
    stacked = 3 * half
    attn_w = folded(
        jnp.concatenate([outers(qkv_grads_t, h1s).reshape(stacked, width), outer(atts[:, 1], out_ins)]),
        jnp.concatenate([outers(qkv_grads_o, h1s).reshape(stacked, width), outer(atts[:, 0], out_ins)]),
    )
    down_w_sum, up_w_sum, attn_w_sum = ring_sum(down_w), ring_sum(up_w), ring_sum(attn_w)
    qkv_w_sum = jnp.moveaxis(attn_w_sum[:stacked].reshape(3, half, width), 2, 0)
    out_w_sum = attn_w_sum[stacked:]

    mod_grad = jnp.stack([
        jnp.concatenate([item[3][0], item[3][1], item[3][2], item[1][0], item[1][1], item[1][2]])
        for item in by_image
    ]).astype(BF)
    columns = mod_grad.reshape(images, 2, 3 * width)
    own_cols = lax.dynamic_index_in_dim(columns, core, 1, keepdims=False)
    other_cols = lax.dynamic_index_in_dim(columns, 1 - core, 1, keepdims=False)
    mod_cols = in_order(own_cols, swap(other_cols), 0)
    silu_grad = jnp.einsum("sk,dk->sd", mod_cols, ada_weight[0], preferred_element_type=F32)
    silu_grad = silu_grad + swap(silu_grad)
    silu_grad = silu_grad + lax.ppermute(silu_grad, "section", [(0, 1), (1, 0)])
    cond_grad = silu_back(silu_grad)[0]

    def spread(array):
        return lax.all_gather(array, "dp", axis=0, tiled=True)

    silu_all, mod_all, cond_all = spread(silu_b), spread(mod_cols), spread(cond_grad)
    ada_w_sum = jnp.einsum("sd,sk->dk", silu_all, mod_all, preferred_element_type=F32)
    ada_b_sum = jnp.sum(mod_all, axis=0, dtype=F32)

    total = jax.tree.map(lambda *items: sum(items), *by_image)
    own_bias = jnp.concatenate([total[4][0], total[4][2], total[2][0]])
    other_bias = jnp.concatenate([total[4][3], total[4][5], total[2][1]])
    both_bias = jnp.concatenate([total[3][3], total[1][3]])
    own_bias = own_bias + swap(other_bias)
    both_bias = both_bias + swap(both_bias)
    gathered = spread(jnp.concatenate([own_bias, both_bias, labels.astype(F32)])[None])
    biases = jnp.sum(gathered, axis=0)
    labels_all = gathered[:, -slots:].reshape(-1)
    onehot = (labels_all[None] == jnp.arange(label_table.shape[0], dtype=F32)[:, None]).astype(F32)
    table_grad = jnp.dot(onehot, cond_all, precision=lax.Precision.HIGHEST, preferred_element_type=F32)
    qkv_b_sum = biases[: 2 * half].reshape(2, half)
    up_b_sum = biases[2 * half : 2 * half + hidden]
    out_b_sum = biases[2 * half + hidden : 2 * half + hidden + width]
    down_b_sum = biases[2 * half + hidden + width : 2 * half + hidden + 2 * width]
    return (
        layer_out,
        in_grad,
        cond_grad,
        table_grad,
        ada_w_sum[None],
        ada_b_sum[None],
        qkv_w_sum[None],
        qkv_b_sum[None],
        out_w_sum[None],
        out_b_sum[None],
        up_w_sum[None],
        up_b_sum[None],
        down_w_sum[None],
        down_b_sum[None],
    )


def solution(mesh):
    placed = (
        P("tensor", "dp", None),
        P("dp"),
        P("dp"),
        P("dp"),
        P(),
        P("section", None, "tensor"),
        P("section", "tensor"),
        P("section", None, None, "tensor"),
        P("section", None, "tensor"),
        P("section", "tensor", None),
        P("section", None),
        P("section", None, "tensor"),
        P("section", "tensor"),
        P("section", "tensor", None),
        P("section", None),
        P("tensor", "dp", None),
    )
    return jax.shard_map(
        shards,
        mesh=mesh,
        in_specs=placed,
        out_specs=(
            P("section", "tensor", "dp", None),
            P("section", "tensor", "dp", None),
            P("dp", None),
            P(),
            P("section", None, "tensor"),
            P("section", "tensor"),
            P("section", None, None, "tensor"),
            P("section", None, "tensor"),
            P("section", "tensor", None),
            P("section", None),
            P("section", None, "tensor"),
            P("section", "tensor"),
            P("section", "tensor", None),
            P("section", None),
        ),
        check_vma=False,
    )
```

time: 1670 us -> 859 us (0.51)
  waiting for transfers between devices: 886 us -> 257 us
  matrix products: 369 us -> 61.8 us
  Pallas kernels: 0 us -> 201 us
  other arithmetic: 162 us -> 50.2 us
  starting transfers between devices: 23.8 us -> 100 us
  blocking collectives: 156 us -> 92.8 us
  between operations: 19.4 us -> 38.1 us
    psum x1 -> x0, waiting for transfers between devices: 691 us -> none  [shards(): lax.psum(table_part.astype(jnp.bfloat16), 'dp').astype(jnp.float32)]
    dot_general x109 -> x12, matrix products: 346 us -> 61.8 us  [the longest x6 29.7 us: outer(): return jnp.einsum('btk,btd->kd', left, right, preferred_element_type=F32)]
    pallas_call x0 -> x9, Pallas kernels: none -> 201 us  [the longest x3 78.9 us: layer_call(): pl.pallas_call(functools.partial(layer_kernel, chunks), out_shape=outs, i...]
    ppermute x8 -> x106, waiting for transfers between devices: 51.4 us -> 219 us  [the longest x42 103 us: ring_sum(): came = lax.ppermute(moving[side], 'dp', pairs)]
    reduce_scatter x30 -> x0, waiting for transfers between devices: 143 us -> none  [the longest x20 94.7 us: narrow(): lax.psum_scatter(term_rows(jnp.int32(0), left_rows.shape[0] // lax.axis_s...]
    reduce_sum x71 -> x2, other arithmetic: 91.1 us -> 0.11 us  [the longest x1 0.06 us: shards(): ada_b_sum = jnp.sum(mod_all, axis=0, dtype=F32)]
    psum x3 -> x0, blocking collectives: 85.5 us -> none  [the longest x1 38.4 us: shards(): out_b_sum, down_b_sum = lax.psum((out_b_acc, down_b_acc), ('dp', 'tensor'))]
    ppermute x8 -> x106, starting transfers between devices: 21.5 us -> 100 us  [the longest x42 44.3 us: ring_sum(): came = lax.ppermute(moving[side], 'dp', pairs)]
  transfers between devices with their start and end apart: 40 -> 107, of which waited for: 26 -> 49; matrix products, arithmetic and copies ran while one was open for 17% -> 17% of each run, Pallas kernels for 0% -> 10%
where the time goes in v1:
time: 859 us; the launch traced here: 849 us
  waiting for transfers between devices  257 us (30%)
  Pallas kernels  201 us (23%)
  starting transfers between devices  100 us (12%)
  blocking collectives  92.8 us (11%)
  matrix products  61.8 us (7%)
  other arithmetic  50.2 us (6%)
  local copies, waits for them, and re-layouts  48 us (6%)
  between operations  38.1 us (4%)
    ppermute x42, waiting for transfers between devices, ring_sum(): came = lax.ppermute(moving[side], 'dp', pairs)  103 us
    ppermute x42, waiting for transfers between devices, ring_sum(): moving[side] = lax.ppermute(moving[side], 'dp', pairs)  93 us
    all_gather x3, blocking collectives, spread(): return lax.all_gather(array, 'dp', axis=0, tiled=True)  92.8 us
    pallas_call x3, Pallas kernels, layer_call(): pl.pallas_call(functools.partial(layer_kernel, chunks), out_shape=outs, i...  78.9 us
    pallas_call x3, Pallas kernels, mlp_back_call(): pl.pallas_call(functools.partial(mlp_back_kernel, chunks), out_shape=(sd(...  62 us
    pallas_call x3, Pallas kernels, attn_back_call(): pl.pallas_call(attn_back_kernel, out_shape=(sd((tokens, width), BF), sd((...  60.4 us
    ppermute x42, starting transfers between devices, ring_sum(): came = lax.ppermute(moving[side], 'dp', pairs)  44.3 us
    ppermute x42, starting transfers between devices, ring_sum(): moving[side] = lax.ppermute(moving[side], 'dp', pairs)  42 us
  transfers between devices with their start and end apart: 107, of which 49 were waited for; matrix products, arithmetic and copies ran while one was open for 17% of the time, Pallas kernels for 10%

profile of v1, /device:TPU:0, one launch (start us, length us, event | category | flops | bytes accessed | tf_op | source)
XLA Modules:
  0.0 849.4 jit_solution(9791657569625328758)
XLA Ops:
  24.1 6.7 copy.116
  37.5 6.5 copy.118.wqt
  44.0 26.4 %layer.3 = (bf16[256,1152]{1,0:T(8,128)(2,1)}, bf16[2,256,1152]{2,1,0:T(8,128)(2,1)}, bf16[2,256,1152]{2,1,0:T(8,128)(2,1)}, bf16[2,3,256,576]{3,2,1,0:T(8,128)(...) custom-call(s32[1]{0:T(128)} %constant.530.clone.1.index_ref, ...), custom_call_target="tpu_custom_call" | custom-call | flops 9512681472 | bytes 31850496 | tf_op jit(solution)/shard_map/layer/pallas_call | solution.py:191
  98.1 31.2 %all-gather.2 = bf16[8,4,1152]{2,1,0:T(4,128)(2,1)S(1)} all-gather(bf16[1,4,1152]{2,1,0:T(4,128)(2,1)S(1)} %bitcast.206), channel_id=1, replica_groups=mesh['section'=2,'dp'=8,'tensor'=2] {'dp'}, dimensions={0}, use_global_device_ids=true | all-gather | bytes 82944 | tf_op jit(solution)/shard_map/all_gather | solution.py:587
  131.8 26.3 %layer.4 = (bf16[256,1152]{1,0:T(8,128)(2,1)}, bf16[2,256,1152]{2,1,0:T(8,128)(2,1)}, bf16[2,256,1152]{2,1,0:T(8,128)(2,1)}, bf16[2,3,256,576]{3,2,1,0:T(8,128)(...) custom-call(s32[1]{0:T(128)} %bitcast.11.index_ref, ...), custom_call_target="tpu_custom_call", output_to_operand_aliasing={{1}: (14, {}), {2}: (15, {}), {3}: (16, {}), {4}: (17, {}),... | custom-call | flops 9512681472 | bytes 31850496 | tf_op jit(solution)/shard_map/layer/pallas_call | solution.py:191
  162.1 5.6 collective-permute-done.8
  168.5 26.3 %layer.5 = (bf16[256,1152]{1,0:T(8,128)(2,1)}, bf16[2,256,1152]{2,1,0:T(8,128)(2,1)}, bf16[2,256,1152]{2,1,0:T(8,128)(2,1)}, bf16[2,3,256,576]{3,2,1,0:T(8,128)(...) custom-call(s32[1]{0:T(128)} %constant.540.clone.1.index_ref, ...), custom_call_target="tpu_custom_call", output_to_operand_aliasing={{1}: (14, {}), {2}: (15, {}), {3}: (16, {}), {4}: (17, {}),... | custom-call | flops 9512681472 | bytes 31850496 | tf_op jit(solution)/shard_map/layer/pallas_call | solution.py:191
  194.8 20.7 %mlp_back.3 = (f32[256,1152]{1,0:T(8,128)}, f32[8,1152]{1,0:T(8,128)}, f32[2,2304]{1,0:T(2,128)}, bf16[2,256,1152]{2,1,0:T(8,128)(2,1)}, bf16[2,256,2304]{2,1,0:T(8,128)(2,1)}, /*index=5*/bf16[2,256,2304]{2,1,0:T(8,128)(2,1)}) custom-call(s32[1]{0:T(128)} %constant.530.clone.1.index_ref, bf16[256,1152]{1,0:T(8,128)(2,1)} %slice_bitcast_fusion.2.g_ref, ...), custom_call_target="tpu_custom_call" | custom-call | flops 5435817984 | bytes 21233664 | tf_op jit(solution)/shard_map/mlp_back/pallas_call | solution.py:277
  215.5 20.2 %attn_back.3 = (bf16[256,1152]{1,0:T(8,128)(2,1)}, f32[8,1152]{1,0:T(8,128)}, f32[8,576]{1,0:T(8,128)}, bf16[2,256,1152]{2,1,0:T(8,128)(2,1)}, bf16[3,2,256,576]...) custom-call(s32[1]{0:T(128)} %constant.530.clone.1.index_ref, f32[256,1152]{1,0:T(8,128)} %get-tuple-element.121.mg_ref, ...), custom_call_target="tpu_custom_call" | custom-call | flops 4076863488 | bytes 10616832 | tf_op jit(solution)/shard_map/attn_back/pallas_call | solution.py:384
  238.1 9.6 %collective-permute-done.11 = bf16[256,1152]{1,0:T(8,128)(2,1)S(1)} collective-permute-done((bf16[256,1152]{1,0:T(8,128)(2,1)}, bf16[256,1152]{1,0:T(8,128)(2,1)S(1)}, u32[]{:S(2)}, u32[]{:S(2)}) %collective-permute-start.11) | collective-permute-done | bytes 589856 | tf_op jit(solution)/shard_map/ppermute | solution.py:553
  248.6 20.6 %mlp_back.4 = (f32[256,1152]{1,0:T(8,128)}, f32[8,1152]{1,0:T(8,128)}, f32[2,2304]{1,0:T(2,128)}, bf16[2,256,1152]{2,1,0:T(8,128)(2,1)}, bf16[2,256,2304]{2,1,0:T(8,128)(2,1)}, /*index=5*/bf16[2,256,2304]{2,1,0:T(8,128)(2,1)}) custom-call(s32[1]{0:T(128)} %bitcast.17.index_ref, ...), custom_call_target="tpu_custom_call", output_to_operand_aliasing={{3}: (12, {}), {4}: (13, {}), {5}: (14, {})} | custom-call | flops 5435817984 | bytes 21233664 | tf_op jit(solution)/shard_map/mlp_back/pallas_call | solution.py:277
  269.3 19.9 %attn_back.4 = (bf16[256,1152]{1,0:T(8,128)(2,1)}, f32[8,1152]{1,0:T(8,128)}, f32[8,576]{1,0:T(8,128)}, bf16[2,256,1152]{2,1,0:T(8,128)(2,1)}, bf16[3,2,256,576]...) custom-call(s32[1]{0:T(128)} %bitcast.17.index_ref, ...), custom_call_target="tpu_custom_call", output_to_operand_aliasing={{3}: (11, {}), {4}: (12, {}), {5}: (13, {})} | custom-call | flops 4076863488 | bytes 10616832 | tf_op jit(solution)/shard_map/attn_back/pallas_call | solution.py:384
  303.3 20.7 %mlp_back.5 = (f32[256,1152]{1,0:T(8,128)}, f32[8,1152]{1,0:T(8,128)}, f32[2,2304]{1,0:T(2,128)}, bf16[2,256,1152]{2,1,0:T(8,128)(2,1)}, bf16[2,256,2304]{2,1,0:T(8,128)(2,1)}, /*index=5*/bf16[2,256,2304]{2,1,0:T(8,128)(2,1)}) custom-call(s32[1]{0:T(128)} %constant.540.clone.1.index_ref, ...), custom_call_target="tpu_custom_call", output_to_operand_aliasing={{3}: (12, {}), {4}: (13, {}), {5}: (14, {})} | custom-call | flops 5435817984 | bytes 21233664 | tf_op jit(solution)/shard_map/mlp_back/pallas_call | solution.py:277
  324.1 7.7 fusion.5
  337.3 20.3 %attn_back.5 = (bf16[256,1152]{1,0:T(8,128)(2,1)}, f32[8,1152]{1,0:T(8,128)}, f32[8,576]{1,0:T(8,128)}, bf16[2,256,1152]{2,1,0:T(8,128)(2,1)}, bf16[3,2,256,576]...) custom-call(s32[1]{0:T(128)} %constant.540.clone.1.index_ref, ...), custom_call_target="tpu_custom_call", output_to_operand_aliasing={{3}: (11, {}), {4}: (12, {}), {5}: (13, {})} | custom-call | flops 4076863488 | bytes 10616832 | tf_op jit(solution)/shard_map/attn_back/pallas_call | solution.py:384
  373.6 5.8 fusion.18
  380.8 30.7 %all-gather.3 = bf16[8,4,3456]{2,1,0:T(4,128)(2,1)S(1)} all-gather(bf16[1,4,3456]{2,1,0:T(4,128)(2,1)S(1)} %fusion.33), channel_id=1, replica_groups=mesh['section'=2,'dp'=8,'tensor'=2] {'dp'}, dimensions={0}, use_global_device_ids=true | all-gather | bytes 248832 | tf_op jit(solution)/shard_map/all_gather | solution.py:587
  411.6 5.4 fusion.7
  417.0 8.2 convolution_bitcast_fusion
  429.8 30.8 %all-gather.1 = f32[8,4,1152]{2,1,0:T(4,128)S(1)} all-gather(f32[1,4,1152]{2,1,0:T(4,128)S(1)} %bitcast.209), channel_id=1, replica_groups=mesh['section'=2,'dp'=8,'tensor'=2] {'dp'}, dimensions={0}, use_global_device_ids=true | all-gather | bytes 165888 | tf_op jit(solution)/shard_map/all_gather | solution.py:587
  460.7 37.7 %all-reduce.3.cloned.1.call-done = f32[46112]{0:T(1024)} async-done(((f32[46112]{0:T(1024)}), f32[46112]{0:T(1024)}) %all-reduce.3.cloned.1.call-update) | async-done | bytes 184464
  508.4 6.6 fusion.4
  517.2 5.4 fusion.2
  532.4 7.1 collective-permute-done.20
  561.8 6.1 collective-permute-done.80
  693.2 6.3 collective-permute-done.64
  714.8 6.0 collective-permute-done.66
  736.1 6.0 collective-permute-done.68
  757.5 6.0 collective-permute-done.70
  778.8 6.0 collective-permute-done.72
  800.1 6.1 collective-permute-done.74
  815.1 16.1 %collective-permute-done.47 = bf16[1,1,144,1152]{3,2,1,0:T(8,128)(2,1)S(1)} collective-permute-done((bf16[1,1,144,1152]{3,2,1,0:T(8,128)(2,1)S(1)}, bf16[1,1,144,1152]{3,2,1,0:T(8,128)(2,1)S(1)}, u32[]{:S(2)}, u32[]{:S(2)}) %collective-permute-start.47) | collective-permute-done | bytes 331808 | tf_op jit(solution)/shard_map/ppermute | solution.py:441
  (493 shorter events, 346.3 us)
Async XLA Ops:
  7.2 491.2 %all-reduce.3.cloned.1.call-start = ((), (), s32[]{:S(2)}) async-start(), calls=%async_computation | async-start | bytes 376832
  7.2 36.8 %collective-permute-start.5 = (bf16[1152,2304]{1,0:T(8,128)(2,1)}, bf16[1152,2304]{1,0:T(8,128)(2,1)}, u32[]{:S(2)}, u32[]{:S(2)}) collective-permute-start(bf16[1152,2304]{1,0:T(8,128)(2,1)} %bitcast.147), channel_id=1, source_target_pairs={{0,1},{1,0},{2,3},{3,2},{4,5},{5,4},{6,7},{7,6},{8,9},{9,8},{10,11... | collective-permute-start | bytes 15925256 | tf_op jit(solution)/shard_map/ppermute | solution.py:407
  7.8 36.2 %collective-permute-start.6 = (bf16[2304,1152]{1,0:T(8,128)(2,1)}, bf16[2304,1152]{1,0:T(8,128)(2,1)}, u32[]{:S(2)}, u32[]{:S(2)}) collective-permute-start(bf16[2304,1152]{1,0:T(8,128)(2,1)} %bitcast.154), channel_id=1, source_target_pairs={{0,1},{1,0},{2,3},{3,2},{4,5},{5,4},{6,7},{7,6},{8,9},{9,8},{10,11... | collective-permute-start | bytes 15925256 | tf_op jit(solution)/shard_map/ppermute | solution.py:407
  7.8 29.6 %collective-permute-start.3 = (bf16[3,1152,576]{1,2,0:T(8,128)(2,1)}, bf16[3,1152,576]{1,2,0:T(8,128)(2,1)}, u32[]{:S(2)}, u32[]{:S(2)}) collective-permute-start(bf16[3,1152,576]{1,2,0:T(8,128)(2,1)} %bitcast.203), channel_id=1, source_target_pairs={{0,1},{1,0},{2,3},{3,2},{4,5},{5,4},{6,7},{7,6},{8,9},{9,8},{10,11... | collective-permute-start | bytes 11943944 | tf_op jit(solution)/shard_map/ppermute | solution.py:407
  70.5 60.3 %collective-permute-start.7 = (bf16[256,1152]{1,0:T(8,128)(2,1)}, bf16[256,1152]{1,0:T(8,128)(2,1)}, u32[]{:S(2)}, u32[]{:S(2)}) collective-permute-start(bf16[256,1152]{1,0:T(8,128)(2,1)} %get-tuple-element.89), channel_id=1, source_target_pairs={{0,16},{1,17},{2,18},{3,19},{4,20},{5,21},{6,22},{7,23},{8,24},{9,... | collective-permute-start | bytes 1769480 | tf_op jit(solution)/shard_map/ppermute | solution.py:532
  75.8 84.2 %collective-permute-start.10 = (bf16[128,2,1152]{2,0,1:T(8,128)(2,1)S(1)}, bf16[128,2,1152]{2,0,1:T(8,128)(2,1)}, u32[]{:S(2)}, u32[]{:S(2)}) collective-permute-start(bf16[128,2,1152]{2,0,1:T(8,128)(2,1)S(1)} %copy.150), channel_id=1, source_target_pairs={{0,1},{1,0},{2,3},{3,2},{4,5},{5,4},{6,7},{7,6},{8,9},{9,8},{10,11... | collective-permute-start | bytes 1769480 | tf_op jit(solution)/shard_map/ppermute | solution.py:407
  238.1 55.3 %collective-permute-start.9 = (bf16[2,128,1152]{2,1,0:T(8,128)(2,1)}, bf16[2,128,1152]{2,1,0:T(8,128)(2,1)S(1)}, u32[]{:S(2)}, u32[]{:S(2)}) collective-permute-start(bf16[2,128,1152]{2,1,0:T(8,128)(2,1)} %get-tuple-element.300), channel_id=1, source_target_pairs={{0,1},{1,0},{2,3},{3,2},{4,5},{5,4},{6,7},{7,6},{8,9},{9,8},{10,11... | collective-permute-start | bytes 1769480 | tf_op jit(solution)/shard_map/ppermute | solution.py:407
  331.7 176.6 %collective-permute-start.77 = (bf16[2304,1152]{1,0:T(8,128)(2,1)}, bf16[2304,1152]{1,0:T(8,128)(2,1)}, u32[]{:S(2)}, u32[]{:S(2)}) collective-permute-start(bf16[2304,1152]{1,0:T(8,128)(2,1)} %fusion.5), channel_id=1, source_target_pairs={{0,1},{1,0},{2,3},{3,2},{4,5},{5,4},{6,7},{7,6},{8,9},{9,8},{10,11... | collective-permute-start | bytes 15925256 | tf_op jit(solution)/shard_map/ppermute | solution.py:407
  336.8 180.4 %collective-permute-start.48 = (bf16[1152,2304]{1,0:T(8,128)(2,1)}, bf16[1152,2304]{1,0:T(8,128)(2,1)}, u32[]{:S(2)}, u32[]{:S(2)}) collective-permute-start(bf16[1152,2304]{1,0:T(8,128)(2,1)} %fusion.3), channel_id=1, source_target_pairs={{0,1},{1,0},{2,3},{3,2},{4,5},{5,4},{6,7},{7,6},{8,9},{9,8},{10,11... | collective-permute-start | bytes 15925256 | tf_op jit(solution)/shard_map/ppermute | solution.py:407
  365.6 159.1 %collective-permute-start.19 = (bf16[2304,1152]{1,0:T(8,128)(2,1)}, bf16[2304,1152]{1,0:T(8,128)(2,1)}, u32[]{:S(2)}, u32[]{:S(2)}) collective-permute-start(bf16[2304,1152]{1,0:T(8,128)(2,1)} %pad_maximum_fusion), channel_id=1, source_target_pairs={{0,1},{1,0},{2,3},{3,2},{4,5},{5,4},{6,7},{7,6},{8,9},{9,8},{10,11... | collective-permute-start | bytes 15925256 | tf_op jit(solution)/shard_map/ppermute | solution.py:407
  380.6 44.7 %collective-permute-start.17 = (f32[3456]{0:T(1024)S(1)}, f32[3456]{0:T(1024)S(1)}, u32[]{:S(2)}, u32[]{:S(2)}) collective-permute-start(f32[3456]{0:T(1024)S(1)} %concatenate.100), channel_id=1, source_target_pairs={{0,1},{1,0},{2,3},{3,2},{4,5},{5,4},{6,7},{7,6},{8,9},{9,8},{10,11... | collective-permute-start | bytes 41480 | tf_op jit(solution)/shard_map/ppermute | solution.py:407
  425.3 81.0 %collective-permute-start.13 = (bf16[2,128,1152]{2,1,0:T(8,128)(2,1)S(1)}, bf16[2,128,1152]{2,1,0:T(8,128)(2,1)S(1)}, u32[]{:S(2)}, u32[]{:S(2)}) collective-permute-start(bf16[2,128,1152]{2,1,0:T(8,128)(2,1)S(1)} %get-tuple-element.296), channel_id=1, source_target_pairs={{0,1},{1,0},{2,3},{3,2},{4,5},{5,4},{6,7},{7,6},{8,9},{9,8},{10,11... | collective-permute-start | bytes 1769480 | tf_op jit(solution)/shard_map/ppermute | solution.py:407
  516.0 24.4 %collective-permute-start.85 = (bf16[1,1,144,1152]{3,2,1,0:T(8,128)(2,1)S(1)}, bf16[1,1,144,1152]{3,2,1,0:T(8,128)(2,1)S(1)}, u32[]{:S(2)}, u32[]{:S(2)}) collective-permute-start(bf16[1,1,144,1152]{3,2,1,0:T(8,128)(2,1)S(1)} %get-tuple-element.267), channel_id=1, source_target_pairs={{4,0},{8,4},{12,8},{14,12},{10,14},{6,10},{2,6},{0,2},{5,1},{9,5},... | collective-permute-start | bytes 995336 | tf_op jit(solution)/shard_map/ppermute | solution.py:433
  523.6 24.1 %collective-permute-start.56 = (bf16[1,1,72,2304]{3,2,1,0:T(8,128)(2,1)S(1)}, bf16[1,1,72,2304]{3,2,1,0:T(8,128)(2,1)S(1)}, u32[]{:S(2)}, u32[]{:S(2)}) collective-permute-start(bf16[1,1,72,2304]{3,2,1,0:T(8,128)(2,1)S(1)} %get-tuple-element.280), channel_id=1, source_target_pairs={{4,0},{8,4},{12,8},{14,12},{10,14},{6,10},{2,6},{0,2},{5,1},{9,5},... | collective-permute-start | bytes 995336 | tf_op jit(solution)/shard_map/ppermute | solution.py:433
  529.5 25.2 %collective-permute-start.27 = (bf16[1,1,144,1152]{3,2,1,0:T(8,128)(2,1)S(1)}, bf16[1,1,144,1152]{3,2,1,0:T(8,128)(2,1)S(1)}, u32[]{:S(2)}, u32[]{:S(2)}) collective-permute-start(bf16[1,1,144,1152]{3,2,1,0:T(8,128)(2,1)S(1)} %get-tuple-element.293), channel_id=1, source_target_pairs={{4,0},{8,4},{12,8},{14,12},{10,14},{6,10},{2,6},{0,2},{5,1},{9,5},... | collective-permute-start | bytes 995336 | tf_op jit(solution)/shard_map/ppermute | solution.py:433
  540.4 20.4 %collective-permute-start.21 = (bf16[1,1,144,1152]{3,2,1,0:T(8,128)(2,1)S(1)}, bf16[1,1,144,1152]{3,2,1,0:T(8,128)(2,1)S(1)}, u32[]{:S(2)}, u32[]{:S(2)}) collective-permute-start(bf16[1,1,144,1152]{3,2,1,0:T(8,128)(2,1)S(1)} %add_convert_fusion.41), channel_id=1, source_target_pairs={{0,4},{4,8},{8,12},{12,14},{14,10},{10,6},{6,2},{2,0},{1,5},{5,9},... | collective-permute-start | bytes 995336 | tf_op jit(solution)/shard_map/ppermute | solution.py:433
  546.8 21.1 %collective-permute-start.80 = (bf16[1,1,144,1152]{3,2,1,0:T(8,128)(2,1)S(1)}, bf16[1,1,144,1152]{3,2,1,0:T(8,128)(2,1)S(1)}, u32[]{:S(2)}, u32[]{:S(2)}) collective-permute-start(bf16[1,1,144,1152]{3,2,1,0:T(8,128)(2,1)S(1)} %get-tuple-element.266), channel_id=1, source_target_pairs={{0,4},{4,8},{8,12},{12,14},{14,10},{10,6},{6,2},{2,0},{1,5},{5,9},... | collective-permute-start | bytes 995336 | tf_op jit(solution)/shard_map/ppermute | solution.py:433
  547.6 21.0 %collective-permute-start.86 = (bf16[1,1,144,1152]{3,2,1,0:T(8,128)(2,1)S(1)}, bf16[1,1,144,1152]{3,2,1,0:T(8,128)(2,1)S(1)}, u32[]{:S(2)}, u32[]{:S(2)}) collective-permute-start(bf16[1,1,144,1152]{3,2,1,0:T(8,128)(2,1)S(1)} %get-tuple-element.265), channel_id=1, source_target_pairs={{4,0},{8,4},{12,8},{14,12},{10,14},{6,10},{2,6},{0,2},{5,1},{9,5},... | collective-permute-start | bytes 995336 | tf_op jit(solution)/shard_map/ppermute | solution.py:433
  553.9 21.1 %collective-permute-start.51 = (bf16[1,1,72,2304]{3,2,1,0:T(8,128)(2,1)S(1)}, bf16[1,1,72,2304]{3,2,1,0:T(8,128)(2,1)S(1)}, u32[]{:S(2)}, u32[]{:S(2)}) collective-permute-start(bf16[1,1,72,2304]{3,2,1,0:T(8,128)(2,1)S(1)} %get-tuple-element.279), channel_id=1, source_target_pairs={{0,4},{4,8},{8,12},{12,14},{14,10},{10,6},{6,2},{2,0},{1,5},{5,9},... | collective-permute-start | bytes 995336 | tf_op jit(solution)/shard_map/ppermute | solution.py:433
  554.7 21.3 %collective-permute-start.57 = (bf16[1,1,72,2304]{3,2,1,0:T(8,128)(2,1)S(1)}, bf16[1,1,72,2304]{3,2,1,0:T(8,128)(2,1)S(1)}, u32[]{:S(2)}, u32[]{:S(2)}) collective-permute-start(bf16[1,1,72,2304]{3,2,1,0:T(8,128)(2,1)S(1)} %get-tuple-element.278), channel_id=1, source_target_pairs={{4,0},{8,4},{12,8},{14,12},{10,14},{6,10},{2,6},{0,2},{5,1},{9,5},... | collective-permute-start | bytes 995336 | tf_op jit(solution)/shard_map/ppermute | solution.py:433
  561.0 21.1 %collective-permute-start.22 = (bf16[1,1,144,1152]{3,2,1,0:T(8,128)(2,1)S(1)}, bf16[1,1,144,1152]{3,2,1,0:T(8,128)(2,1)S(1)}, u32[]{:S(2)}, u32[]{:S(2)}) collective-permute-start(bf16[1,1,144,1152]{3,2,1,0:T(8,128)(2,1)S(1)} %get-tuple-element.292), channel_id=1, source_target_pairs={{0,4},{4,8},{8,12},{12,14},{14,10},{10,6},{6,2},{2,0},{1,5},{5,9},... | collective-permute-start | bytes 995336 | tf_op jit(solution)/shard_map/ppermute | solution.py:433
  568.8 20.4 %collective-permute-start.81 = (bf16[1,1,144,1152]{3,2,1,0:T(8,128)(2,1)S(1)}, bf16[1,1,144,1152]{3,2,1,0:T(8,128)(2,1)S(1)}, u32[]{:S(2)}, u32[]{:S(2)}) collective-permute-start(bf16[1,1,144,1152]{3,2,1,0:T(8,128)(2,1)S(1)} %get-tuple-element.264), channel_id=1, source_target_pairs={{0,4},{4,8},{8,12},{12,14},{14,10},{10,6},{6,2},{2,0},{1,5},{5,9},... | collective-permute-start | bytes 995336 | tf_op jit(solution)/shard_map/ppermute | solution.py:433
  597.3 20.4 %collective-permute-start.53 = (bf16[1,1,72,2304]{3,2,1,0:T(8,128)(2,1)S(1)}, bf16[1,1,72,2304]{3,2,1,0:T(8,128)(2,1)S(1)}, u32[]{:S(2)}, u32[]{:S(2)}) collective-permute-start(bf16[1,1,72,2304]{3,2,1,0:T(8,128)(2,1)S(1)} %get-tuple-element.275), channel_id=1, source_target_pairs={{0,4},{4,8},{8,12},{12,14},{14,10},{10,6},{6,2},{2,0},{1,5},{5,9},... | collective-permute-start | bytes 995336 | tf_op jit(solution)/shard_map/ppermute | solution.py:433
  611.5 20.4 %collective-permute-start.83 = (bf16[1,1,144,1152]{3,2,1,0:T(8,128)(2,1)S(1)}, bf16[1,1,144,1152]{3,2,1,0:T(8,128)(2,1)S(1)}, u32[]{:S(2)}, u32[]{:S(2)}) collective-permute-start(bf16[1,1,144,1152]{3,2,1,0:T(8,128)(2,1)S(1)} %get-tuple-element.260), channel_id=1, source_target_pairs={{0,4},{4,8},{8,12},{12,14},{14,10},{10,6},{6,2},{2,0},{1,5},{5,9},... | collective-permute-start | bytes 995336 | tf_op jit(solution)/shard_map/ppermute | solution.py:433
  618.6 20.4 %collective-permute-start.54 = (bf16[1,1,72,2304]{3,2,1,0:T(8,128)(2,1)S(1)}, bf16[1,1,72,2304]{3,2,1,0:T(8,128)(2,1)S(1)}, u32[]{:S(2)}, u32[]{:S(2)}) collective-permute-start(bf16[1,1,72,2304]{3,2,1,0:T(8,128)(2,1)S(1)} %get-tuple-element.273), channel_id=1, source_target_pairs={{0,4},{4,8},{8,12},{12,14},{14,10},{10,6},{6,2},{2,0},{1,5},{5,9},... | collective-permute-start | bytes 995336 | tf_op jit(solution)/shard_map/ppermute | solution.py:433
  625.7 20.4 %collective-permute-start.25 = (bf16[1,1,144,1152]{3,2,1,0:T(8,128)(2,1)S(1)}, bf16[1,1,144,1152]{3,2,1,0:T(8,128)(2,1)S(1)}, u32[]{:S(2)}, u32[]{:S(2)}) collective-permute-start(bf16[1,1,144,1152]{3,2,1,0:T(8,128)(2,1)S(1)} %get-tuple-element.286), channel_id=1, source_target_pairs={{0,4},{4,8},{8,12},{12,14},{14,10},{10,6},{6,2},{2,0},{1,5},{5,9},... | collective-permute-start | bytes 995336 | tf_op jit(solution)/shard_map/ppermute | solution.py:433
  639.9 20.4 %collective-permute-start.55 = (bf16[1,1,72,2304]{3,2,1,0:T(8,128)(2,1)S(1)}, bf16[1,1,72,2304]{3,2,1,0:T(8,128)(2,1)S(1)}, u32[]{:S(2)}, u32[]{:S(2)}) collective-permute-start(bf16[1,1,72,2304]{3,2,1,0:T(8,128)(2,1)S(1)} %get-tuple-element.271), channel_id=1, source_target_pairs={{0,4},{4,8},{8,12},{12,14},{14,10},{10,6},{6,2},{2,0},{1,5},{5,9},... | collective-permute-start | bytes 995336 | tf_op jit(solution)/shard_map/ppermute | solution.py:433
  660.3 25.8 %collective-permute-start.92 = (bf16[1,1,144,1152]{3,2,1,0:T(8,128)(2,1)S(1)}, bf16[1,1,144,1152]{3,2,1,0:T(8,128)(2,1)S(1)}, u32[]{:S(2)}, u32[]{:S(2)}) collective-permute-start(bf16[1,1,144,1152]{3,2,1,0:T(8,128)(2,1)S(1)} %get-tuple-element.243), channel_id=1, source_target_pairs={{0,4},{4,8},{8,12},{12,14},{14,10},{10,6},{6,2},{2,0},{1,5},{5,9},... | collective-permute-start | bytes 995336 | tf_op jit(solution)/shard_map/ppermute | solution.py:441
  686.1 20.9 %collective-permute-start.35 = (bf16[1,1,144,1152]{3,2,1,0:T(8,128)(2,1)S(1)}, bf16[1,1,144,1152]{3,2,1,0:T(8,128)(2,1)S(1)}, u32[]{:S(2)}, u32[]{:S(2)}) collective-permute-start(bf16[1,1,144,1152]{3,2,1,0:T(8,128)(2,1)S(1)} %get-tuple-element.249), channel_id=1, source_target_pairs={{4,0},{8,4},{12,8},{14,12},{10,14},{6,10},{2,6},{0,2},{5,1},{9,5},... | collective-permute-start | bytes 995336 | tf_op jit(solution)/shard_map/ppermute | solution.py:441
  790.9 24.1 %collective-permute-start.104 = (bf16[1,1,144,1152]{3,2,1,0:T(8,128)(2,1)S(1)}, bf16[1,1,144,1152]{3,2,1,0:T(8,128)(2,1)S(1)}, u32[]{:S(2)}, u32[]{:S(2)}) collective-permute-start(bf16[1,1,144,1152]{3,2,1,0:T(8,128)(2,1)S(1)} %collective-permute-done.102), channel_id=1, source_target_pairs={{0,4},{4,8},{8,12},{12,14},{14,10},{10,6},{6,2},{2,0},{1,5},{5,9},... | collective-permute-start | bytes 995336 | tf_op jit(solution)/shard_map/ppermute | solution.py:441
  806.3 30.4 %collective-permute-start.105 = (bf16[1,1,144,1152]{3,2,1,0:T(8,128)(2,1)S(1)}, bf16[1,1,144,1152]{3,2,1,0:T(8,128)(2,1)}, u32[]{:S(2)}, u32[]{:S(2)}) collective-permute-start(bf16[1,1,144,1152]{3,2,1,0:T(8,128)(2,1)S(1)} %collective-permute-done.103), channel_id=1, source_target_pairs={{4,0},{8,4},{12,8},{14,12},{10,14},{6,10},{2,6},{0,2},{5,1},{9,5},... | collective-permute-start | bytes 995336 | tf_op jit(solution)/shard_map/ppermute | solution.py:441
  810.8 26.9 %collective-permute-start.76 = (bf16[1,1,72,2304]{3,2,1,0:T(8,128)(2,1)}, bf16[1,1,72,2304]{3,2,1,0:T(8,128)(2,1)}, u32[]{:S(2)}, u32[]{:S(2)}) collective-permute-start(bf16[1,1,72,2304]{3,2,1,0:T(8,128)(2,1)} %collective-permute-done.74), channel_id=1, source_target_pairs={{4,0},{8,4},{12,8},{14,12},{10,14},{6,10},{2,6},{0,2},{5,1},{9,5},... | collective-permute-start | bytes 995336 | tf_op jit(solution)/shard_map/ppermute | solution.py:441
  (124 other events, 2053.5 us)
Sparse Core Ops, SparseCore 0:
  427.0 71.3 all-reduce.2

commit v2 on v1

v2 whole, which is shorter than its diff:
```python
import functools
import math
import jax
import jax.numpy as jnp
from jax import lax
from jax.experimental import pallas as pl
from jax.experimental.pallas import tpu as pltpu
from jax.sharding import PartitionSpec as P

HEADS = 16
eps_norm = 1e-06
BF, F32 = jnp.bfloat16, jnp.float32
ANY = pl.BlockSpec(memory_space=pl.ANY)
VM = pl.BlockSpec(memory_space=pltpu.VMEM)
LIMIT = 60 * 1024 * 1024
DEPTH = 4
ROOT = math.sqrt(2.0 / math.pi)
CUBE = 0.044715


def nt(left, right):
    return lax.dot_general(left, right, (((1,), (1,)), ((), ())), preferred_element_type=F32)


def tn(left, right):
    return lax.dot_general(left, right, (((0,), (0,)), ((), ())), preferred_element_type=F32)


def nn(left, right):
    return jnp.dot(left, right, preferred_element_type=F32)


def norm_parts(rows):
    centered = rows - jnp.mean(rows, axis=-1, keepdims=True)
    inverse = lax.rsqrt(jnp.mean(centered * centered, axis=-1, keepdims=True) + eps_norm)
    return centered * inverse, inverse


def windows(width, size):
    spans = []
    for head in range(width // size):
        low, high = head * size, (head + 1) * size
        spans.append((low, high, low // 128 * 128, min(width, (high + 127) // 128 * 128)))
    return spans


def head_mask(span):
    low, high, start, stop = span
    lanes = lax.broadcasted_iota(jnp.int32, (1, stop - start), 1) + start
    return (lanes >= low) & (lanes < high)


class Copies:
    def __init__(self, sems):
        self.sems, self.used = sems, 0

    def start(self, source, target):
        copy = pltpu.make_async_copy(source, target, self.sems.at[self.used])
        self.used += 1
        copy.start()
        return copy


class Stream:
    def __init__(self, copies, depth, pairs):
        self.copies, self.depth, self.pairs, self.begun, self.taken = copies, depth, pairs, [], 0
        self.fill()

    def fill(self):
        while len(self.begun) < min(len(self.pairs), self.taken + self.depth):
            self.begun.append(self.copies.start(*self.pairs[len(self.begun)]))

    def take(self, count=1):
        for _ in range(count):
            self.begun[self.taken].wait()
            self.taken += 1
            self.fill()


def three_kinds(sources, target):
    return [(source.at[kind], target.at[side, kind]) for side, source in enumerate(sources) for kind in range(3)]


def soft(scores, scale):
    top = jnp.max(scores, axis=-1, keepdims=True)
    powers = jnp.exp2((scores - top) * (scale * math.log2(math.e)))
    return powers * (1.0 / jnp.sum(powers, axis=-1, keepdims=True))


def layer_kernel(chunks, index_ref, mod_ref, bqv_ref, bup_ref, bod_ref, x_in,
                 wqo, wqt, woo, wot, wuo, wut, wdo, wdt, *rest):
    rest = rest[len(rest) - 30:]
    (y_out, ys, xs, h1s, qkvo, qkvt, atts, aos, h2s, preo, pret, acto, actt, mos,
     wq, wo, wu, wd, x, y, h1, qkv, att, attf, ao, h2, pre, act, mo, sems) = rest

    @pl.when(index_ref[1] == 1)
    def _():
        copies = Copies(sems)
        img = index_ref[0]
        step = wu.shape[2] // chunks
        spots = [(side, slice(place * step, (place + 1) * step)) for side in range(2) for place in range(chunks)]
        pairs = [(x_in, x), *three_kinds((wqo, wqt), wq), (woo, wo.at[0]), (wot, wo.at[1])]
        for side, spot in spots:
            up, down = ((wuo, wdo), (wut, wdt))[side]
            pairs += [(up.at[:, spot], wu.at[side, :, spot]), (down.at[spot, :], wd.at[side, spot, :])]
        stream = Stream(copies, DEPTH, pairs)
        half = att.shape[2]
        size = 2 * half // HEADS
        scale = size ** (-0.5)
        mods = mod_ref[img]
        stream.take()
        pending = [copies.start(x, xs.at[img])]
        normed, _ = norm_parts(x[...].astype(F32))
        h1[...] = (normed * (1.0 + mods[1:2]) + mods[0:1]).astype(BF)
        pending.append(copies.start(h1, h1s.at[img]))
        for part in range(6):
            side, kind = part // 3, part % 3
            stream.take()
            mixed = nn(h1[...], wq[side, kind])
            qkv[side, kind] = (mixed + bqv_ref[part : part + 1]).astype(BF)
        pending += [copies.start(qkv.at[0], qkvo.at[img]), copies.start(qkv.at[1], qkvt.at[img])]

        def attend(side, carry):
            attf[...] = jnp.zeros_like(attf)
            for span in windows(half, size):
                part = slice(span[2], span[3])
                mask = head_mask(span)
                zero = jnp.zeros((), BF)
                queries = jnp.where(mask, qkv[side, 0, :, part], zero)
                scores = nt(queries, qkv[side, 1, :, part])
                probs = soft(scores, scale).astype(BF)
                attf[:, part] += nn(probs, jnp.where(mask, qkv[side, 2, :, part], zero))
            att[side] = attf[...].astype(BF)
            return carry

        lax.fori_loop(0, 2, attend, 0)
        pending.append(copies.start(att, atts.at[img]))
        stream.take(2)
        ao[...] = nn(att[0], wo[0]) + nn(att[1], wo[1]) + bod_ref[0:1]
        pending.append(copies.start(ao, aos.at[img]))
        normed, _ = norm_parts(x[...].astype(F32) + mods[2:3] * ao[...])
        h2[...] = (normed * (1.0 + mods[4:5]) + mods[3:4]).astype(BF)
        pending.append(copies.start(h2, h2s.at[img]))
        for number, (side, spot) in enumerate(spots):
            stream.take()
            values = nn(h2[...], wu[side, :, spot]) + bup_ref[side : side + 1, spot]
            pre[side, :, spot] = values.astype(BF)
            inner = jnp.tanh(values * (ROOT + ROOT * CUBE * values * values))
            act[side, :, spot] = (0.5 * values * (1.0 + inner)).astype(BF)
            stream.take()
            term = nn(act[side, :, spot], wd[side, spot, :])
            mo[...] = term + (bod_ref[1:2] if number == 0 else mo[...])
            pre_out, act_out = ((preo, acto), (pret, actt))[side]
            pending += [copies.start(pre.at[side, :, spot], pre_out.at[img, :, spot]),
                        copies.start(act.at[side, :, spot], act_out.at[img, :, spot])]
        pending.append(copies.start(mo, mos.at[img]))
        y[...] = (mods[6:7] * (x[...].astype(F32) + mods[2:3] * ao[...] + mods[5:6] * mo[...])).astype(BF)
        pending += [copies.start(y, y_out), copies.start(y, ys.at[img])]
        for copy in pending:
            copy.wait()


def cost(tokens, weight_count):
    return pl.CostEstimate(
        flops=2 * tokens * weight_count, bytes_accessed=2 * weight_count, transcendentals=0)


def layer_call(index, x, mods, bqv, bup, bod, weights, saved, images):
    tokens, width = x.shape
    half, hidden = width // 2, bup.shape[1]
    chunks = 3 if hidden % 384 == 0 else 1
    sd = jax.ShapeDtypeStruct
    outs = (
        sd((tokens, width), BF),
        sd((images, tokens, width), BF),
        sd((images, tokens, width), BF),
        sd((images, tokens, width), BF),
        sd((images, 3, tokens, half), BF),
        sd((images, 3, tokens, half), BF),
        sd((images, 2, tokens, half), BF),
        sd((images, tokens, width), F32),
        sd((images, tokens, width), BF),
        sd((images, tokens, hidden), BF),
        sd((images, tokens, hidden), BF),
        sd((images, tokens, hidden), BF),
        sd((images, tokens, hidden), BF),
        sd((images, tokens, width), F32),
    )
    saved = tuple(saved) if saved is not None else ()
    aliases = {14 + i: 1 + i for i in range(len(saved))}
    scratch = [
        pltpu.VMEM((2, 3, width, half), BF),
        pltpu.VMEM((2, half, width), BF),
        pltpu.VMEM((2, width, hidden), BF),
        pltpu.VMEM((2, hidden, width), BF),
        pltpu.VMEM((tokens, width), BF),
        pltpu.VMEM((tokens, width), BF),
        pltpu.VMEM((tokens, width), BF),
        pltpu.VMEM((2, 3, tokens, half), BF),
        pltpu.VMEM((2, tokens, half), BF),
        pltpu.VMEM((tokens, half), F32),
        pltpu.VMEM((tokens, width), F32),
        pltpu.VMEM((tokens, width), BF),
        pltpu.VMEM((2, tokens, hidden), BF),
        pltpu.VMEM((2, tokens, hidden), BF),
        pltpu.VMEM((tokens, width), F32),
        pltpu.SemaphoreType.DMA((64,)),
    ]
    return pl.pallas_call(
        functools.partial(layer_kernel, chunks),
        out_shape=outs,
        in_specs=[pl.BlockSpec(memory_space=pltpu.SMEM)] + [VM] * 4 + [ANY] * (9 + len(saved)),
        out_specs=[ANY] * 14,
        scratch_shapes=scratch,
        input_output_aliases=aliases,
        compiler_params=pltpu.CompilerParams(vmem_limit_bytes=LIMIT),
        cost_estimate=cost(tokens, width * (8 * half + 4 * hidden)),
        name="layer",
    )(index, mods, bqv, bup, bod, x, *weights, *saved)


def mlp_back_kernel(chunks, index_ref, mod_ref, g_in, xs, aos, mos, preo, pret, wuo, wut, wdo, wdt, *rest):
    rest = rest[len(rest) - 20:]
    (mg_out, sums, bus, dis, pgo, pgt, wu, wd, g, mg, x, ao, mo, pre, di, pg, ng, total, bu, sems) = rest

    @pl.when(index_ref[1] == 1)
    def _():
        copies = Copies(sems)
        img = index_ref[0]
        step = pre.shape[2] // chunks
        spots = [(side, slice(place * step, (place + 1) * step)) for side in range(2) for place in range(chunks)]
        pairs = [(g_in, g)]
        for side, spot in spots:
            pre_in, up, down = ((preo, wuo, wdo), (pret, wut, wdt))[side]
            pairs += [(down.at[spot, :], wd.at[side, spot, :]), (pre_in.at[img, :, spot], pre.at[side, :, spot]),
                      (up.at[:, spot], wu.at[side, :, spot])]
        stream = Stream(copies, DEPTH, pairs + [(mos.at[img], mo), (xs.at[img], x), (aos.at[img], ao)])
        mods = mod_ref[img]
        stream.take()
        mg[...] = g[...].astype(F32) * mods[6:7]
        di[...] = (mg[...] * mods[5:6]).astype(BF)
        pending = [copies.start(di, dis.at[img])]
        for number, (side, spot) in enumerate(spots):
            stream.take(2)
            values = pre[side, :, spot].astype(F32)
            grad = nt(di[...], wd[side, spot, :])
            square = values * values
            inner = jnp.tanh(values * (ROOT + ROOT * CUBE * square))
            slope = 0.5 * (1.0 + inner) + 0.5 * values * (1.0 - inner * inner) * (ROOT + 3.0 * ROOT * CUBE * square)
            graded = (grad * slope).astype(BF)
            pg[side, :, spot] = graded
            bu[side : side + 1, spot] = jnp.sum(graded.astype(F32), axis=0, keepdims=True)
            stream.take()
            term = nt(pg[side, :, spot], wu[side, :, spot])
            ng[...] = term if number == 0 else ng[...] + term
            pending.append(copies.start(pg.at[side, :, spot], (pgo, pgt)[side].at[img, :, spot]))
        pending.append(copies.start(bu, bus.at[img]))
        stream.take()
        total[2:3] = jnp.sum(mg[...] * mo[...], axis=0, keepdims=True)
        total[3:4] = jnp.sum(di[...].astype(F32), axis=0, keepdims=True)
        stream.take(2)
        normed, inverse = norm_parts(x[...].astype(F32) + mods[2:3] * ao[...])
        total[0:1] = jnp.sum(ng[...], axis=0, keepdims=True)
        total[1:2] = jnp.sum(ng[...] * normed, axis=0, keepdims=True)
        pending.append(copies.start(total, sums.at[img]))
        dn = ng[...] * (1.0 + mods[4:5])
        mg[...] += inverse * (
            dn - jnp.mean(dn, axis=-1, keepdims=True) - normed * jnp.mean(dn * normed, axis=-1, keepdims=True))
        pending.append(copies.start(mg, mg_out))
        for copy in pending:
            copy.wait()


def mlp_back_call(index, grad, mods, saved, weights, kept, images):
    xs, aos, mos, preo, pret = saved
    tokens, width = grad.shape
    hidden = preo.shape[2]
    chunks = 3 if hidden % 384 == 0 else 1
    sd = jax.ShapeDtypeStruct
    kept = tuple(kept) if kept is not None else ()
    aliases = {12 + i: 1 + i for i in range(len(kept))}
    scratch = [
        pltpu.VMEM((2, width, hidden), BF),
        pltpu.VMEM((2, hidden, width), BF),
        pltpu.VMEM((tokens, width), BF),
        pltpu.VMEM((tokens, width), F32),
        pltpu.VMEM((tokens, width), BF),
        pltpu.VMEM((tokens, width), F32),
        pltpu.VMEM((tokens, width), F32),
        pltpu.VMEM((2, tokens, hidden), BF),
        pltpu.VMEM((tokens, width), BF),
        pltpu.VMEM((2, tokens, hidden), BF),
        pltpu.VMEM((tokens, width), F32),
        pltpu.VMEM((8, width), F32),
        pltpu.VMEM((2, hidden), F32),
        pltpu.SemaphoreType.DMA((48,)),
    ]
    return pl.pallas_call(
        functools.partial(mlp_back_kernel, chunks),
        out_shape=(
            sd((tokens, width), F32), sd((images, 8, width), F32), sd((images, 2, hidden), F32),
            sd((images, tokens, width), BF), sd((images, tokens, hidden), BF), sd((images, tokens, hidden), BF)),
        in_specs=[pl.BlockSpec(memory_space=pltpu.SMEM), VM] + [ANY] * (10 + len(kept)),
        out_specs=[ANY] * 6,
        scratch_shapes=scratch,
        input_output_aliases=aliases,
        compiler_params=pltpu.CompilerParams(vmem_limit_bytes=LIMIT),
        cost_estimate=cost(tokens, 4 * width * hidden),
        name="mlp_back",
    )(index, mods, grad, xs, aos, mos, preo, pret, *weights, *kept)


def attn_back_kernel(index_ref, mod_ref, mg_in, xs, aos, qkvo, qkvt, wqo, wqt, woo, wot, *rest):
    rest = rest[len(rest) - 22:]
    (rg_out, rgs, sums, bqvs, ois, qgo, qgt, wq, wo, mg, rg, x, ao, qkv, oi, qg, da, acc, ng, total, bqv, sems) = rest

    @pl.when(index_ref[1] == 1)
    def _():
        copies = Copies(sems)
        img = index_ref[0]
        stream = Stream(copies, DEPTH, [
            (mg_in, mg), (woo, wo.at[0]), (wot, wo.at[1]), (qkvo.at[img], qkv.at[0]), (qkvt.at[img], qkv.at[1]),
            *three_kinds((wqo, wqt), wq), (aos.at[img], ao), (xs.at[img], x)])
        half = wo.shape[1]
        size = 2 * half // HEADS
        scale = size ** (-0.5)
        mods = mod_ref[img]
        stream.take()
        oi[...] = (mg[...] * mods[2:3]).astype(BF)
        pending = [copies.start(oi, ois.at[img])]
        for side in range(2):
            stream.take()
            da[side] = nt(oi[...], wo[side]).astype(BF)
        stream.take(2)

        def attend(side, carry):
            for kind in range(3):
                acc[kind] = jnp.zeros_like(acc[kind])
            for span in windows(half, size):
                part = slice(span[2], span[3])
                mask = head_mask(span)
                zero = jnp.zeros((), BF)
                queries = jnp.where(mask, qkv[side, 0, :, part], zero)
                keys = jnp.where(mask, qkv[side, 1, :, part], zero)
                outer = jnp.where(mask, da[side, :, part], zero)
                probs = soft(nt(queries, keys), scale)
                grads = nt(outer, qkv[side, 2, :, part])
                inner = jnp.sum(grads * probs, axis=-1, keepdims=True)
                spread = (probs * (grads - inner)).astype(BF)
                acc[2, :, part] += tn(probs.astype(BF), outer)
                acc[0, :, part] += nn(spread, keys)
                acc[1, :, part] += tn(spread, queries)
            for kind in range(3):
                factor = 1.0 if kind == 2 else scale
                qg[side, kind] = (acc[kind] * factor).astype(BF)
            return carry

        lax.fori_loop(0, 2, attend, 0)
        for side, target in enumerate((qgo, qgt)):
            pending += [copies.start(qg.at[side, kind], target.at[kind, img]) for kind in range(3)]
        for part in range(6):
            side, kind = part // 3, part % 3
            stream.take()
            term = nt(qg[side, kind], wq[side, kind])
            ng[...] = term if part == 0 else ng[...] + term
            bqv[part : part + 1] = jnp.sum(qg[side, kind].astype(F32), axis=0, keepdims=True)
        pending.append(copies.start(bqv, bqvs.at[img]))
        stream.take()
        total[2:3] = jnp.sum(mg[...] * ao[...], axis=0, keepdims=True)
        total[3:4] = jnp.sum(oi[...].astype(F32), axis=0, keepdims=True)
        stream.take()
        normed, inverse = norm_parts(x[...].astype(F32))
        total[0:1] = jnp.sum(ng[...], axis=0, keepdims=True)
        total[1:2] = jnp.sum(ng[...] * normed, axis=0, keepdims=True)
        pending.append(copies.start(total, sums.at[img]))
        dn = ng[...] * (1.0 + mods[1:2])
        rg[...] = (mg[...] + inverse * (
            dn - jnp.mean(dn, axis=-1, keepdims=True) - normed * jnp.mean(dn * normed, axis=-1, keepdims=True))).astype(BF)
        pending += [copies.start(rg, rg_out), copies.start(rg, rgs.at[img])]
        for copy in pending:
            copy.wait()


def attn_back_call(index, grad, mods, saved, weights, kept, images):
    xs, aos, qkvo, qkvt = saved
    tokens, width = grad.shape
    half = width // 2
    sd = jax.ShapeDtypeStruct
    kept = tuple(kept) if kept is not None else ()
    aliases = {11 + i: 1 + i for i in range(len(kept))}
    scratch = [
        pltpu.VMEM((2, 3, width, half), BF),
        pltpu.VMEM((2, half, width), BF),
        pltpu.VMEM((tokens, width), F32),
        pltpu.VMEM((tokens, width), BF),
        pltpu.VMEM((tokens, width), BF),
        pltpu.VMEM((tokens, width), F32),
        pltpu.VMEM((2, 3, tokens, half), BF),
        pltpu.VMEM((tokens, width), BF),
        pltpu.VMEM((2, 3, tokens, half), BF),
        pltpu.VMEM((2, tokens, half), BF),
        pltpu.VMEM((3, tokens, half), F32),
        pltpu.VMEM((tokens, width), F32),
        pltpu.VMEM((8, width), F32),
        pltpu.VMEM((8, half), F32),
        pltpu.SemaphoreType.DMA((32,)),
    ]
    return pl.pallas_call(
        attn_back_kernel,
        out_shape=(
            sd((tokens, width), BF), sd((images, tokens, width), BF), sd((images, 8, width), F32),
            sd((images, 8, half), F32), sd((images, tokens, width), BF),
            sd((3, images, tokens, half), BF), sd((3, images, tokens, half), BF)),
        in_specs=[pl.BlockSpec(memory_space=pltpu.SMEM), VM] + [ANY] * (9 + len(kept)),
        out_specs=[ANY] * 7,
        scratch_shapes=scratch,
        input_output_aliases=aliases,
        compiler_params=pltpu.CompilerParams(vmem_limit_bytes=LIMIT),
        cost_estimate=cost(tokens, 8 * width * half),
        name="attn_back",
    )(index, mods, grad, xs, aos, qkvo, qkvt, *weights, *kept)


def time_embed(timesteps, width_all):
    half_width = width_all // 2
    frequencies = jnp.exp(-math.log(10000.0) * jnp.arange(half_width, dtype=F32) / half_width)
    angles = timesteps.astype(F32)[:, None] * frequencies[None, :]
    return jnp.concatenate([jnp.cos(angles), jnp.sin(angles)], axis=1)


def swap(array):
    return lax.ppermute(array, "tensor", [(0, 1), (1, 0)])


def partners():
    peers = lax.axis_size("dp")
    place = lax.axis_index("dp")
    bit = 1
    while bit < peers:
        yield [(i, i ^ bit) for i in range(peers)], (place & bit) == 0
        bit *= 2


def gather_all(array):
    for pairs, is_low in partners():
        came = lax.ppermute(array, "dp", pairs)
        array = jnp.where(is_low, jnp.concatenate([array, came]), jnp.concatenate([came, array]))
    return array


def add_all(array):
    for pairs, _ in partners():
        array = array + lax.ppermute(array, "dp", pairs)
    return array


def ring_order(peers):
    order = list(range(0, peers, 2)) + list(range(1, peers, 2))[::-1]
    place = [order.index(peer) for peer in range(peers)]
    ahead = [(order[i], order[(i + 1) % peers]) for i in range(peers)]
    return place, ahead, [(b, a) for a, b in ahead]


def ring_sum(terms):
    peers = lax.axis_size("dp")
    place, ahead, behind = ring_order(peers)
    here = jnp.asarray(place, jnp.int32)[lax.axis_index("dp")]
    count, width = terms.shape
    part = count // (2 * peers)
    blocks = terms.reshape(2, peers, part, width)
    total = jnp.zeros((2, peers, part, width), F32)
    lanes = ((ahead, 1), (behind, -1))

    def block(side, number):
        return lax.dynamic_slice(blocks, (side, number % peers, 0, 0), (1, 1, part, width))

    moving = [block(side, here) for side in range(2)]
    for step in range(1, peers):
        for side, (pairs, sign) in enumerate(lanes):
            came = lax.ppermute(moving[side], "dp", pairs)
            mine = block(side, here - sign * step)
            moving[side] = (came.astype(F32) + mine.astype(F32)).astype(BF)
    for step in range(peers):
        for side, (pairs, sign) in enumerate(lanes):
            owner = (here - sign * (peers - 1 + step)) % peers
            total = lax.dynamic_update_slice(total, moving[side].astype(F32), (side, owner, 0, 0))
            if step < peers - 1:
                moving[side] = lax.ppermute(moving[side], "dp", pairs)
    return total.reshape(count, width)


def folded(other, own):
    came = swap(other.astype(BF))
    return (own + came.astype(F32)).astype(BF)


def outer(left, right):
    return jnp.einsum("btk,btd->kd", left, right, preferred_element_type=F32)


def outers(left, right):
    return jnp.einsum("jbtk,btd->jkd", left, right, preferred_element_type=F32)


def shards(images_in, timesteps, labels, counts, label_table, ada_weight, ada_bias, qkv_weight,
           qkv_bias, out_weight, out_bias, up_weight, up_bias, down_weight, down_bias, out_cotangent):
    is_first = lax.axis_index("section") == 0
    core = lax.axis_index("tensor")
    slots = images_in.shape[1]
    images = slots // 2
    width = images_in.shape[2]
    hidden = up_weight.shape[2]
    half = out_weight.shape[1]

    def by_section(first_val, later_val):
        return jnp.where(is_first, first_val, later_val)

    def by_core(first_val, later_val):
        return jnp.where(core == 0, first_val, later_val)

    def mine(array, axis):
        return lax.dynamic_slice_in_dim(array, core * images, images, axis)

    def others(array, axis):
        return lax.dynamic_slice_in_dim(array, (1 - core) * images, images, axis)

    def in_order(own, came, axis):
        return by_core(jnp.concatenate([own, came], axis), jnp.concatenate([came, own], axis))

    def whole_images(rows):
        came = swap(others(rows, 1))
        return jnp.moveaxis(jnp.concatenate([mine(rows, 1), came], axis=0), 1, 0)

    def split_images(rows):
        local = rows.shape[1] // 2
        came = swap(rows[:, local:])
        return jnp.moveaxis(in_order(rows[:, :local], came, 0), 0, 1)[None]

    qkv_own = lax.optimization_barrier(jnp.moveaxis(qkv_weight[0], 1, 0))
    w_qkv = (qkv_own, swap(qkv_own))
    w_out = (out_weight[0], swap(out_weight[0]))
    w_up = (up_weight[0], swap(up_weight[0]))
    w_down = (down_weight[0], swap(down_weight[0]))
    weights = (*w_qkv, *w_out, *w_up, *w_down)

    condition = jnp.take(label_table, labels, axis=0).astype(F32) + time_embed(timesteps, width)
    silu_cond, silu_back = jax.vjp(jax.nn.silu, condition)
    silu_b = silu_cond.astype(BF)
    mod_local = (
        jnp.dot(silu_b, ada_weight[0], preferred_element_type=F32) + ada_bias[0].astype(F32)[None]
    )
    modulation = in_order(mine(mod_local, 0), swap(others(mod_local, 0)), 1).reshape(images, 6, width)
    slot_no = core * images + jnp.arange(images, dtype=jnp.int32)
    valid = (slot_no < counts[0]).astype(F32)
    mods = jnp.concatenate(
        [modulation, jnp.broadcast_to(valid[:, None, None], (images, 2, width))], axis=1
    )
    pair_bias = jnp.concatenate([qkv_bias[0, 0], qkv_bias[0, 1], up_bias[0]])[None]
    pair_bias = jnp.concatenate([pair_bias, swap(pair_bias)], axis=0).astype(F32)
    zero_row = jnp.zeros((half,), F32)
    bqv = jnp.stack([
        pair_bias[0, :half], zero_row, pair_bias[0, half : 2 * half],
        pair_bias[1, :half], zero_row, pair_bias[1, half : 2 * half], zero_row, zero_row])
    bup = pair_bias[:, 2 * half :]
    bod = jnp.concatenate([out_bias, down_bias], axis=0).astype(F32)

    rows_in = whole_images(images_in)
    cotangent = whole_images(out_cotangent)

    def turn_index(number, is_active):
        return jnp.stack([jnp.int32(number), is_active.astype(jnp.int32)])

    inputs, saved = [rows_in[i] for i in range(images)], None
    for turn in range(2 * images):
        number, is_early = turn % images, turn < images
        answer = layer_call(
            turn_index(number, is_first == is_early), inputs[turn], mods, bqv, bup, bod, weights, saved, images
        )
        saved = answer[1:]
        if is_early:
            inputs.append(lax.ppermute(answer[0], "section", [(0, 1)]))
    ys, xs, h1s, qkvo, qkvt, atts, aos, h2s, preo, pret, acto, actt, mos = saved
    layer_out = split_images(ys)

    inputs, mlp_kept, attn_kept = [cotangent[i] for i in range(images)], None, None
    for turn in range(2 * images):
        number, is_early = turn % images, turn < images
        index = turn_index(number, is_first != is_early)
        answer = mlp_back_call(
            index, inputs[turn], mods, (xs, aos, mos, preo, pret), (*w_up, *w_down), mlp_kept, images
        )
        middle_grad, mlp_kept = answer[0], answer[1:]
        answer = attn_back_call(
            index, middle_grad, mods, (xs, aos, qkvo, qkvt), (*w_qkv, *w_out), attn_kept, images
        )
        attn_kept = answer[1:]
        if is_early:
            inputs.append(lax.ppermute(answer[0], "section", [(1, 0)]))
    mlp_sums, up_sums, down_ins, pre_grads_o, pre_grads_t = mlp_kept
    row_grads, attn_sums, qkv_sums, out_ins, qkv_grads_o, qkv_grads_t = attn_kept
    in_grad = split_images(row_grads)

    down_w = folded(outer(actt, down_ins), outer(acto, down_ins))
    up_w = folded(outer(h2s, pre_grads_t), outer(h2s, pre_grads_o))
    stacked = 3 * half
    attn_w = folded(
        jnp.concatenate([outers(qkv_grads_t, h1s).reshape(stacked, width), outer(atts[:, 1], out_ins)]),
        jnp.concatenate([outers(qkv_grads_o, h1s).reshape(stacked, width), outer(atts[:, 0], out_ins)]),
    )
    down_w_sum, up_w_sum, attn_w_sum = ring_sum(down_w), ring_sum(up_w), ring_sum(attn_w)
    qkv_w_sum = jnp.moveaxis(attn_w_sum[:stacked].reshape(3, half, width), 2, 0)
    out_w_sum = attn_w_sum[stacked:]

    mod_grad = jnp.concatenate([attn_sums[:, :3], mlp_sums[:, :3]], axis=1).astype(BF)
    columns = mod_grad.reshape(images, 2, 3 * width)
    own_cols = lax.dynamic_index_in_dim(columns, core, 1, keepdims=False)
    other_cols = lax.dynamic_index_in_dim(columns, 1 - core, 1, keepdims=False)
    mod_cols = in_order(own_cols, swap(other_cols), 0)
    silu_grad = jnp.einsum("sk,dk->sd", mod_cols, ada_weight[0], preferred_element_type=F32)
    silu_grad = silu_grad + swap(silu_grad)
    silu_grad = silu_grad + lax.ppermute(silu_grad, "section", [(0, 1), (1, 0)])
    cond_grad = silu_back(silu_grad)[0]

    silu_all = gather_all(silu_b)
    mod_all = gather_all(mod_cols)
    kept_rows = jnp.concatenate([cond_grad.reshape(1, -1), labels.astype(F32)[None]], axis=1)
    gathered = gather_all(kept_rows)
    cond_all = gathered[:, : slots * width].reshape(-1, width)
    labels_all = gathered[:, slots * width :].reshape(-1)
    ada_w_sum = jnp.einsum("sd,sk->dk", silu_all, mod_all, preferred_element_type=F32)
    ada_b_sum = jnp.sum(mod_all, axis=0, dtype=F32)
    onehot = (labels_all[None] == jnp.arange(label_table.shape[0], dtype=F32)[:, None]).astype(F32)
    table_grad = jnp.dot(onehot, cond_all, precision=lax.Precision.HIGHEST, preferred_element_type=F32)

    qkv_total, up_total = jnp.sum(qkv_sums, axis=0), jnp.sum(up_sums, axis=0)
    own_bias = jnp.concatenate([qkv_total[0], qkv_total[2], up_total[0]])
    other_bias = jnp.concatenate([qkv_total[3], qkv_total[5], up_total[1]])
    both_bias = jnp.concatenate([jnp.sum(attn_sums[:, 3], axis=0), jnp.sum(mlp_sums[:, 3], axis=0)])
    came_bias = swap(jnp.concatenate([other_bias, both_bias]))
    biases = add_all(jnp.concatenate([own_bias, both_bias]) + came_bias)
    qkv_b_sum = biases[: 2 * half].reshape(2, half)
    up_b_sum = biases[2 * half : 2 * half + hidden]
    out_b_sum = biases[2 * half + hidden : 2 * half + hidden + width]
    down_b_sum = biases[2 * half + hidden + width :]
    return (
        layer_out,
        in_grad,
        cond_grad,
        table_grad,
        ada_w_sum[None],
        ada_b_sum[None],
        qkv_w_sum[None],
        qkv_b_sum[None],
        out_w_sum[None],
        out_b_sum[None],
        up_w_sum[None],
        up_b_sum[None],
        down_w_sum[None],
        down_b_sum[None],
    )


def solution(mesh):
    placed = (
        P("tensor", "dp", None),
        P("dp"),
        P("dp"),
        P("dp"),
        P(),
        P("section", None, "tensor"),
        P("section", "tensor"),
        P("section", None, None, "tensor"),
        P("section", None, "tensor"),
        P("section", "tensor", None),
        P("section", None),
        P("section", None, "tensor"),
        P("section", "tensor"),
        P("section", "tensor", None),
        P("section", None),
        P("tensor", "dp", None),
    )
    return jax.shard_map(
        shards,
        mesh=mesh,
        in_specs=placed,
        out_specs=(
            P("section", "tensor", "dp", None),
            P("section", "tensor", "dp", None),
            P("dp", None),
            P(),
            P("section", None, "tensor"),
            P("section", "tensor"),
            P("section", None, None, "tensor"),
            P("section", None, "tensor"),
            P("section", "tensor", None),
            P("section", None),
            P("section", None, "tensor"),
            P("section", "tensor"),
            P("section", "tensor", None),
            P("section", None),
        ),
        check_vma=False,
    )
```

time: 859 us -> 752 us (0.88)
  blocking collectives: 92.8 us -> 0 us
  Pallas kernels: 201 us -> 155 us
  starting transfers between devices: 100 us -> 130 us
  between operations: 38.1 us -> 24 us
  waiting for transfers between devices: 257 us -> 269 us
  local copies, waits for them, and re-layouts: 48 us -> 58.9 us
    all_gather x3 -> x0, blocking collectives: 92.8 us -> none  [spread(): return lax.all_gather(array, 'dp', axis=0, tiled=True)]
    ppermute x4 -> x16, waiting for transfers between devices: 19 us -> 90 us  [the longest x2 66.4 us: shards(): inputs.append(lax.ppermute(answer[0], 'section', [(1, 0)]))]
    unnamed x2 -> x0, waiting for transfers between devices: 37.7 us -> none
    pallas_call x3 -> x4, Pallas kernels: 62 us -> 39.1 us  [mlp_back_call(): pl.pallas_call(functools.partial(mlp_back_kernel, chunks), out_shape=(sd(...]
    ppermute x4 -> x16, starting transfers between devices: 9.93 us -> 25.3 us  [the longest x9 15.5 us: gather_all(): came = lax.ppermute(array, 'dp', pairs)]
    pallas_call x3 -> x4, Pallas kernels: 78.9 us -> 64.9 us  [layer_call(): pl.pallas_call(functools.partial(layer_kernel, chunks), out_shape=outs, i...]
    ppermute x42, starting transfers between devices: 42 us -> 51.5 us  [ring_sum(): moving[side] = lax.ppermute(moving[side], 'dp', pairs)]
    ppermute x42, waiting for transfers between devices: 93 us -> 83.6 us  [ring_sum(): moving[side] = lax.ppermute(moving[side], 'dp', pairs)]
  transfers between devices with their start and end apart: 107 -> 117, of which waited for: 49 -> 53; matrix products, arithmetic and copies ran while one was open for 17% -> 21% of each run, Pallas kernels for 10% -> 16%
where the time goes in v2:
time: 752 us; the launch traced here: 742 us
  waiting for transfers between devices  269 us (36%)
  Pallas kernels  155 us (21%)
  starting transfers between devices  130 us (17%)
  local copies, waits for them, and re-layouts  58.9 us (8%)
  matrix products  57.3 us (8%)
  other arithmetic  47.7 us (6%)
  between operations  24 us (3%)
    ppermute x42, waiting for transfers between devices, ring_sum(): came = lax.ppermute(moving[side], 'dp', pairs)  95.6 us
    ppermute x42, waiting for transfers between devices, ring_sum(): moving[side] = lax.ppermute(moving[side], 'dp', pairs)  83.6 us
    ppermute x2, waiting for transfers between devices, shards(): inputs.append(lax.ppermute(answer[0], 'section', [(1, 0)]))  66.4 us
    pallas_call x4, Pallas kernels, layer_call(): pl.pallas_call(functools.partial(layer_kernel, chunks), out_shape=outs, i...  64.9 us
    ppermute x42, starting transfers between devices, ring_sum(): moving[side] = lax.ppermute(moving[side], 'dp', pairs)  51.5 us
    pallas_call x4, Pallas kernels, attn_back_call(): pl.pallas_call(attn_back_kernel, out_shape=(sd((tokens, width), BF), sd((...  51.5 us
    ppermute x42, starting transfers between devices, ring_sum(): came = lax.ppermute(moving[side], 'dp', pairs)  48.7 us
    pallas_call x4, Pallas kernels, mlp_back_call(): pl.pallas_call(functools.partial(mlp_back_kernel, chunks), out_shape=(sd(...  39.1 us
  transfers between devices with their start and end apart: 117, of which 53 were waited for; matrix products, arithmetic and copies ran while one was open for 21% of the time, Pallas kernels for 16%

profile of v2, /device:TPU:0, one launch (start us, length us, event | category | flops | bytes accessed | tf_op | source)
XLA Modules:
  0.0 742.3 jit_solution(192175200350089983)
XLA Ops:
  2.9 6.5 copy.137
  9.5 6.5 copy.138
  24.9 5.6 constant_dynamic-slice_fusion.9
  70.7 6.5 copy.140.wqt
  77.3 24.0 %layer.4 = (bf16[256,1152]{1,0:T(8,128)(2,1)}, bf16[2,256,1152]{2,1,0:T(8,128)(2,1)}, bf16[2,256,1152]{2,1,0:T(8,128)(2,1)}, bf16[2,256,1152]{2,1,0:T(8,128)(2,1...) custom-call(s32[2]{0:T(128)} %get-tuple-element.353.index_ref, ...), custom_call_target="tpu_custom_call" | custom-call | flops 8153726976 | bytes 31850496 | tf_op jit(solution)/shard_map/layer/pallas_call | solution.py:209
  102.7 24.2 %layer.5 = (bf16[256,1152]{1,0:T(8,128)(2,1)}, bf16[2,256,1152]{2,1,0:T(8,128)(2,1)}, bf16[2,256,1152]{2,1,0:T(8,128)(2,1)}, bf16[2,256,1152]{2,1,0:T(8,128)(2,1...) custom-call(s32[2]{0:T(128)} %get-tuple-element.352.index_ref, ...), custom_call_target="tpu_custom_call", output_to_operand_aliasing={{1}: (14, {}), {2}: (15, {}), {3}: (16, {}), {4}: (17, {}),... | custom-call | flops 8153726976 | bytes 31850496 | tf_op jit(solution)/shard_map/layer/pallas_call | solution.py:209
  129.1 7.8 %layer.6 = (bf16[256,1152]{1,0:T(8,128)(2,1)}, bf16[2,256,1152]{2,1,0:T(8,128)(2,1)}, bf16[2,256,1152]{2,1,0:T(8,128)(2,1)}, bf16[2,256,1152]{2,1,0:T(8,128)(2,1...) custom-call(s32[2]{0:T(128)} %pad_add_fusion.4.index_ref, ...), custom_call_target="tpu_custom_call", output_to_operand_aliasing={{1}: (14, {}), {2}: (15, {}), {3}: (16, {}), {4}: (17, {}),... | custom-call | flops 8153726976 | bytes 31850496 | tf_op jit(solution)/shard_map/layer/pallas_call | solution.py:209
  142.4 8.8 %layer.7 = (bf16[256,1152]{1,0:T(8,128)(2,1)}, bf16[2,256,1152]{2,1,0:T(8,128)(2,1)}, bf16[2,256,1152]{2,1,0:T(8,128)(2,1)}, bf16[2,256,1152]{2,1,0:T(8,128)(2,1...) custom-call(s32[2]{0:T(128)} %pad_add_fusion.2.index_ref, ...), custom_call_target="tpu_custom_call", output_to_operand_aliasing={{1}: (14, {}), {2}: (15, {}), {3}: (16, {}), {4}: (17, {}),... | custom-call | flops 8153726976 | bytes 31850496 | tf_op jit(solution)/shard_map/layer/pallas_call | solution.py:209
  158.8 5.7 mlp_back.5
  164.5 6.7 attn_back.5
  173.6 45.7 %collective-permute-done.12.g_in = bf16[256,1152]{1,0:T(8,128)(2,1)S(1)} collective-permute-done((bf16[256,1152]{1,0:T(8,128)(2,1)}, bf16[256,1152]{1,0:T(8,128)(2,1)S(1)}, u32[]{:S(2)}, u32[]{:S(2)}) %collective-permute-start.12) | collective-permute-done | bytes 589856 | tf_op jit(solution)/shard_map/ppermute | solution.py:598
  220.1 16.0 %mlp_back.6 = (f32[256,1152]{1,0:T(8,128)}, f32[2,8,1152]{2,1,0:T(8,128)}, f32[2,2,2304]{2,1,0:T(2,128)}, bf16[2,256,1152]{2,1,0:T(8,128)(2,1)}, bf16[2,256,2304...) custom-call(s32[2]{0:T(128)} %get-tuple-element.353.index_ref, ...), custom_call_target="tpu_custom_call", output_to_operand_aliasing={{1}: (12, {}), {2}: (13, {}), {3}: (14, {}), {4}: (15, {}),... | custom-call | flops 5435817984 | bytes 21233664 | tf_op jit(solution)/shard_map/mlp_back/pallas_call | solution.py:298
  236.1 20.8 %collective-permute-done.11.g_in = bf16[256,1152]{1,0:T(8,128)(2,1)S(1)} collective-permute-done((bf16[256,1152]{1,0:T(8,128)(2,1)}, bf16[256,1152]{1,0:T(8,128)(2,1)S(1)}, u32[]{:S(2)}, u32[]{:S(2)}) %collective-permute-start.11) | collective-permute-done | bytes 589856 | tf_op jit(solution)/shard_map/ppermute | solution.py:598
  257.7 16.0 %mlp_back.7 = (f32[256,1152]{1,0:T(8,128)}, f32[2,8,1152]{2,1,0:T(8,128)}, f32[2,2,2304]{2,1,0:T(2,128)}, bf16[2,256,1152]{2,1,0:T(8,128)(2,1)}, bf16[2,256,2304...) custom-call(s32[2]{0:T(128)} %get-tuple-element.352.index_ref, ...), custom_call_target="tpu_custom_call", output_to_operand_aliasing={{1}: (12, {}), {2}: (13, {}), {3}: (14, {}), {4}: (15, {}),... | custom-call | flops 5435817984 | bytes 21233664 | tf_op jit(solution)/shard_map/mlp_back/pallas_call | solution.py:298
  273.7 20.1 %attn_back.6 = (bf16[256,1152]{1,0:T(8,128)(2,1)}, bf16[2,256,1152]{2,1,0:T(8,128)(2,1)}, f32[2,8,1152]{2,1,0:T(8,128)}, f32[2,8,576]{2,1,0:T(8,128)}, bf16[2,25...) custom-call(s32[2]{0:T(128)} %get-tuple-element.353.index_ref, ...), custom_call_target="tpu_custom_call", output_to_operand_aliasing={{1}: (11, {}), {2}: (12, {}), {3}: (13, {}), {4}: (14, {}),... | custom-call | flops 2717908992 | bytes 10616832 | tf_op jit(solution)/shard_map/attn_back/pallas_call | solution.py:408
  293.8 20.0 %attn_back.7 = (bf16[256,1152]{1,0:T(8,128)(2,1)}, bf16[2,256,1152]{2,1,0:T(8,128)(2,1)}, f32[2,8,1152]{2,1,0:T(8,128)}, f32[2,8,576]{2,1,0:T(8,128)}, bf16[2,25...) custom-call(s32[2]{0:T(128)} %get-tuple-element.352.index_ref, ...), custom_call_target="tpu_custom_call", output_to_operand_aliasing={{1}: (11, {}), {2}: (12, {}), {3}: (13, {}), {4}: (14, {}),... | custom-call | flops 2717908992 | bytes 10616832 | tf_op jit(solution)/shard_map/attn_back/pallas_call | solution.py:408
  317.4 7.4 fusion.5
  324.8 5.4 fusion.3
  343.8 5.8 fusion.18
  388.5 5.4 collective-permute-done.25
  399.0 8.2 %convolution_bitcast_fusion = f32[1,1152,3456]{2,1,0:T(8,128)} fusion(bf16[16,1152]{1,0:T(8,128)(2,1)S(1)} %collective-permute-done.22, bf16[16,1152]{1,0:T(8,128)(2,1)S(1)} %copy-done.29, pred[]{:T(512)S(6)} %eq.143, bf16[16,3456]{1,0:T(8,128)(2,1)S(1)} %collective-permute-done.25, bf16[16,3456]{1,0:T(8,128)(2,1)S(1)} %maximum_select_fusion.4), kind=kOutput, calls=%fused_computation.1 | convolution fusion | flops 256131072 | bytes 16220161 | tf_op jit(solution)/shard_map/sd,sk->dk/dot_general | solution.py:630
  411.4 5.4 fusion.4
  419.6 5.4 fusion.2
  438.0 5.0 collective-permute-done.27
  536.7 5.9 collective-permute-done.65
  597.9 5.1 collective-permute-done.75
  619.3 5.1 collective-permute-done.77
  640.6 5.1 collective-permute-done.79
  661.9 5.1 collective-permute-done.81
  683.3 5.1 collective-permute-done.83
  704.6 5.2 collective-permute-done.85
  718.9 12.1 %collective-permute-done.54 = bf16[1,1,144,1152]{3,2,1,0:T(8,128)(2,1)S(1)} collective-permute-done((bf16[1,1,144,1152]{3,2,1,0:T(8,128)(2,1)S(1)}, bf16[1,1,144,1152]{3,2,1,0:T(8,128)(2,1)S(1)}, u32[]{:S(2)}, u32[]{:S(2)}) %collective-permute-start.54) | collective-permute-done | bytes 331808 | tf_op jit(solution)/shard_map/ppermute | solution.py:488
  (496 shorter events, 380.7 us)
Async XLA Ops:
  2.4 57.1 %collective-permute-start.1 = (bf16[1,3456]{1,0:T(2,128)(2,1)S(1)}, bf16[1,3456]{1,0:T(2,128)(2,1)S(1)}, u32[]{:S(2)}, u32[]{:S(2)}) collective-permute-start(bf16[1,3456]{1,0:T(2,128)(2,1)S(1)} %broadcast_in_dim.62), channel_id=1, source_target_pairs={{0,1},{1,0},{2,3},{3,2},{4,5},{5,4},{6,7},{7,6},{8,9},{9,8},{10,11... | collective-permute-start | bytes 20744 | tf_op jit(solution)/shard_map/ppermute | solution.py:432
  16.0 54.7 %collective-permute-start.3 = (bf16[3,1152,576]{1,2,0:T(8,128)(2,1)}, bf16[3,1152,576]{1,2,0:T(8,128)(2,1)}, u32[]{:S(2)}, u32[]{:S(2)}) collective-permute-start(bf16[3,1152,576]{1,2,0:T(8,128)(2,1)} %copy.138), channel_id=1, source_target_pairs={{0,1},{1,0},{2,3},{3,2},{4,5},{5,4},{6,7},{7,6},{8,9},{9,8},{10,11... | collective-permute-start | bytes 11943944 | tf_op jit(solution)/shard_map/ppermute | solution.py:432
  16.1 61.2 %collective-permute-start.5 = (bf16[1152,2304]{1,0:T(8,128)(2,1)}, bf16[1152,2304]{1,0:T(8,128)(2,1)}, u32[]{:S(2)}, u32[]{:S(2)}) collective-permute-start(bf16[1152,2304]{1,0:T(8,128)(2,1)} %bitcast.134), channel_id=1, source_target_pairs={{0,1},{1,0},{2,3},{3,2},{4,5},{5,4},{6,7},{7,6},{8,9},{9,8},{10,11... | collective-permute-start | bytes 15925256 | tf_op jit(solution)/shard_map/ppermute | solution.py:432
  16.5 60.8 %collective-permute-start.6 = (bf16[2304,1152]{1,0:T(8,128)(2,1)}, bf16[2304,1152]{1,0:T(8,128)(2,1)}, u32[]{:S(2)}, u32[]{:S(2)}) collective-permute-start(bf16[2304,1152]{1,0:T(8,128)(2,1)} %bitcast.143), channel_id=1, source_target_pairs={{0,1},{1,0},{2,3},{3,2},{4,5},{5,4},{6,7},{7,6},{8,9},{9,8},{10,11... | collective-permute-start | bytes 15925256 | tf_op jit(solution)/shard_map/ppermute | solution.py:432
  18.0 42.9 %collective-permute-start.20 = (bf16[4,1152]{1,0:T(4,128)(2,1)S(1)}, bf16[4,1152]{1,0:T(4,128)(2,1)S(1)}, u32[]{:S(2)}, u32[]{:S(2)}) collective-permute-start(bf16[4,1152]{1,0:T(4,128)(2,1)S(1)} %multiply_convert_fusion), channel_id=1, source_target_pairs={{0,2},{2,0},{4,6},{6,4},{8,10},{10,8},{12,14},{14,12},{1,3},{3,1},... | collective-permute-start | bytes 27656 | tf_op jit(solution)/shard_map/ppermute | solution.py:446
  101.3 26.9 %collective-permute-start.8 = (bf16[256,1152]{1,0:T(8,128)(2,1)}, bf16[256,1152]{1,0:T(8,128)(2,1)S(1)}, u32[]{:S(2)}, u32[]{:S(2)}) collective-permute-start(bf16[256,1152]{1,0:T(8,128)(2,1)} %get-tuple-element.132), channel_id=1, source_target_pairs={{0,16},{1,17},{2,18},{3,19},{4,20},{5,21},{6,22},{7,23},{8,24},{9,... | collective-permute-start | bytes 1769480 | tf_op jit(solution)/shard_map/ppermute | solution.py:581
  157.5 61.8 %collective-permute-start.12 = (bf16[256,1152]{1,0:T(8,128)(2,1)}, bf16[256,1152]{1,0:T(8,128)(2,1)S(1)}, u32[]{:S(2)}, u32[]{:S(2)}) collective-permute-start(bf16[256,1152]{1,0:T(8,128)(2,1)} %get-tuple-element.181), channel_id=1, source_target_pairs={{16,0},{17,1},{18,2},{19,3},{20,4},{21,5},{22,6},{23,7},{24,8},{25... | collective-permute-start | bytes 1769480 | tf_op jit(solution)/shard_map/ppermute | solution.py:598
  171.2 85.7 %collective-permute-start.11 = (bf16[256,1152]{1,0:T(8,128)(2,1)}, bf16[256,1152]{1,0:T(8,128)(2,1)S(1)}, u32[]{:S(2)}, u32[]{:S(2)}) collective-permute-start(bf16[256,1152]{1,0:T(8,128)(2,1)} %get-tuple-element.180), channel_id=1, source_target_pairs={{16,0},{17,1},{18,2},{19,3},{20,4},{21,5},{22,6},{23,7},{24,8},{25... | collective-permute-start | bytes 1769480 | tf_op jit(solution)/shard_map/ppermute | solution.py:598
  173.6 181.5 %collective-permute-start.9 = (bf16[2,128,1152]{2,1,0:T(8,128)(2,1)}, bf16[2,128,1152]{2,1,0:T(8,128)(2,1)}, u32[]{:S(2)}, u32[]{:S(2)}) collective-permute-start(bf16[2,128,1152]{2,1,0:T(8,128)(2,1)} %get-tuple-element.330), channel_id=1, source_target_pairs={{0,1},{1,0},{2,3},{3,2},{4,5},{5,4},{6,7},{7,6},{8,9},{9,8},{10,11... | collective-permute-start | bytes 1769480 | tf_op jit(solution)/shard_map/ppermute | solution.py:432
  324.8 86.6 %collective-permute-start.88 = (bf16[2304,1152]{1,0:T(8,128)(2,1)}, bf16[2304,1152]{1,0:T(8,128)(2,1)}, u32[]{:S(2)}, u32[]{:S(2)}) collective-permute-start(bf16[2304,1152]{1,0:T(8,128)(2,1)} %fusion.5), channel_id=1, source_target_pairs={{0,1},{1,0},{2,3},{3,2},{4,5},{5,4},{6,7},{7,6},{8,9},{9,8},{10,11... | collective-permute-start | bytes 15925256 | tf_op jit(solution)/shard_map/ppermute | solution.py:432
  330.2 89.3 %collective-permute-start.59 = (bf16[1152,2304]{1,0:T(8,128)(2,1)}, bf16[1152,2304]{1,0:T(8,128)(2,1)}, u32[]{:S(2)}, u32[]{:S(2)}) collective-permute-start(bf16[1152,2304]{1,0:T(8,128)(2,1)} %fusion.3), channel_id=1, source_target_pairs={{0,1},{1,0},{2,3},{3,2},{4,5},{5,4},{6,7},{7,6},{8,9},{9,8},{10,11... | collective-permute-start | bytes 15925256 | tf_op jit(solution)/shard_map/ppermute | solution.py:432
  331.0 23.5 %collective-permute-start.55 = (f32[5760]{0:T(1024)S(1)}, f32[5760]{0:T(1024)S(1)}, u32[]{:S(2)}, u32[]{:S(2)}) collective-permute-start(f32[5760]{0:T(1024)S(1)} %concatenate.168), channel_id=1, source_target_pairs={{0,1},{1,0},{2,3},{3,2},{4,5},{5,4},{6,7},{7,6},{8,9},{9,8},{10,11... | collective-permute-start | bytes 69128 | tf_op jit(solution)/shard_map/ppermute | solution.py:432
  354.5 72.7 %collective-permute-start.26 = (bf16[2304,1152]{1,0:T(8,128)(2,1)}, bf16[2304,1152]{1,0:T(8,128)(2,1)}, u32[]{:S(2)}, u32[]{:S(2)}) collective-permute-start(bf16[2304,1152]{1,0:T(8,128)(2,1)} %pad_maximum_fusion), channel_id=1, source_target_pairs={{0,1},{1,0},{2,3},{3,2},{4,5},{5,4},{6,7},{7,6},{8,9},{9,8},{10,11... | collective-permute-start | bytes 15925256 | tf_op jit(solution)/shard_map/ppermute | solution.py:432
  364.5 42.7 %collective-permute-start.13 = (bf16[2,128,1152]{2,1,0:T(8,128)(2,1)}, bf16[2,128,1152]{2,1,0:T(8,128)(2,1)S(1)}, u32[]{:S(2)}, u32[]{:S(2)}) collective-permute-start(bf16[2,128,1152]{2,1,0:T(8,128)(2,1)} %get-tuple-element.324), channel_id=1, source_target_pairs={{0,1},{1,0},{2,3},{3,2},{4,5},{5,4},{6,7},{7,6},{8,9},{9,8},{10,11... | collective-permute-start | bytes 1769480 | tf_op jit(solution)/shard_map/ppermute | solution.py:432
  419.6 25.5 %collective-permute-start.96 = (bf16[1,1,144,1152]{3,2,1,0:T(8,128)(2,1)S(1)}, bf16[1,1,144,1152]{3,2,1,0:T(8,128)(2,1)S(1)}, u32[]{:S(2)}, u32[]{:S(2)}) collective-permute-start(bf16[1,1,144,1152]{3,2,1,0:T(8,128)(2,1)S(1)} %get-tuple-element.295), channel_id=1, source_target_pairs={{4,0},{8,4},{12,8},{14,12},{10,14},{6,10},{2,6},{0,2},{5,1},{9,5},... | collective-permute-start | bytes 995336 | tf_op jit(solution)/shard_map/ppermute | solution.py:480
  427.2 25.2 %collective-permute-start.67 = (bf16[1,1,72,2304]{3,2,1,0:T(8,128)(2,1)S(1)}, bf16[1,1,72,2304]{3,2,1,0:T(8,128)(2,1)S(1)}, u32[]{:S(2)}, u32[]{:S(2)}) collective-permute-start(bf16[1,1,72,2304]{3,2,1,0:T(8,128)(2,1)S(1)} %get-tuple-element.308), channel_id=1, source_target_pairs={{4,0},{8,4},{12,8},{14,12},{10,14},{6,10},{2,6},{0,2},{5,1},{9,5},... | collective-permute-start | bytes 995336 | tf_op jit(solution)/shard_map/ppermute | solution.py:480
  433.1 26.3 %collective-permute-start.34 = (bf16[1,1,144,1152]{3,2,1,0:T(8,128)(2,1)S(1)}, bf16[1,1,144,1152]{3,2,1,0:T(8,128)(2,1)S(1)}, u32[]{:S(2)}, u32[]{:S(2)}) collective-permute-start(bf16[1,1,144,1152]{3,2,1,0:T(8,128)(2,1)S(1)} %get-tuple-element.321), channel_id=1, source_target_pairs={{4,0},{8,4},{12,8},{14,12},{10,14},{6,10},{2,6},{0,2},{5,1},{9,5},... | collective-permute-start | bytes 995336 | tf_op jit(solution)/shard_map/ppermute | solution.py:480
  450.3 21.1 %collective-permute-start.91 = (bf16[1,1,144,1152]{3,2,1,0:T(8,128)(2,1)S(1)}, bf16[1,1,144,1152]{3,2,1,0:T(8,128)(2,1)S(1)}, u32[]{:S(2)}, u32[]{:S(2)}) collective-permute-start(bf16[1,1,144,1152]{3,2,1,0:T(8,128)(2,1)S(1)} %get-tuple-element.294), channel_id=1, source_target_pairs={{0,4},{4,8},{8,12},{12,14},{14,10},{10,6},{6,2},{2,0},{1,5},{5,9},... | collective-permute-start | bytes 995336 | tf_op jit(solution)/shard_map/ppermute | solution.py:480
  457.4 21.1 %collective-permute-start.62 = (bf16[1,1,72,2304]{3,2,1,0:T(8,128)(2,1)S(1)}, bf16[1,1,72,2304]{3,2,1,0:T(8,128)(2,1)S(1)}, u32[]{:S(2)}, u32[]{:S(2)}) collective-permute-start(bf16[1,1,72,2304]{3,2,1,0:T(8,128)(2,1)S(1)} %get-tuple-element.307), channel_id=1, source_target_pairs={{0,4},{4,8},{8,12},{12,14},{14,10},{10,6},{6,2},{2,0},{1,5},{5,9},... | collective-permute-start | bytes 995336 | tf_op jit(solution)/shard_map/ppermute | solution.py:480
  464.5 21.1 %collective-permute-start.29 = (bf16[1,1,144,1152]{3,2,1,0:T(8,128)(2,1)S(1)}, bf16[1,1,144,1152]{3,2,1,0:T(8,128)(2,1)S(1)}, u32[]{:S(2)}, u32[]{:S(2)}) collective-permute-start(bf16[1,1,144,1152]{3,2,1,0:T(8,128)(2,1)S(1)} %get-tuple-element.320), channel_id=1, source_target_pairs={{0,4},{4,8},{8,12},{12,14},{14,10},{10,6},{6,2},{2,0},{1,5},{5,9},... | collective-permute-start | bytes 995336 | tf_op jit(solution)/shard_map/ppermute | solution.py:480
  551.9 21.1 %collective-permute-start.39 = (bf16[1,1,144,1152]{3,2,1,0:T(8,128)(2,1)S(1)}, bf16[1,1,144,1152]{3,2,1,0:T(8,128)(2,1)S(1)}, u32[]{:S(2)}, u32[]{:S(2)}) collective-permute-start(bf16[1,1,144,1152]{3,2,1,0:T(8,128)(2,1)S(1)} %get-tuple-element.311), channel_id=1, source_target_pairs={{4,0},{8,4},{12,8},{14,12},{10,14},{6,10},{2,6},{0,2},{5,1},{9,5},... | collective-permute-start | bytes 995336 | tf_op jit(solution)/shard_map/ppermute | solution.py:480
  563.9 26.0 %collective-permute-start.103 = (bf16[1,1,144,1152]{3,2,1,0:T(8,128)(2,1)S(1)}, bf16[1,1,144,1152]{3,2,1,0:T(8,128)(2,1)S(1)}, u32[]{:S(2)}, u32[]{:S(2)}) collective-permute-start(bf16[1,1,144,1152]{3,2,1,0:T(8,128)(2,1)S(1)} %get-tuple-element.275), channel_id=1, source_target_pairs={{0,4},{4,8},{8,12},{12,14},{14,10},{10,6},{6,2},{2,0},{1,5},{5,9},... | collective-permute-start | bytes 995336 | tf_op jit(solution)/shard_map/ppermute | solution.py:488
  571.0 21.0 %collective-permute-start.74 = (bf16[1,1,72,2304]{3,2,1,0:T(8,128)(2,1)S(1)}, bf16[1,1,72,2304]{3,2,1,0:T(8,128)(2,1)S(1)}, u32[]{:S(2)}, u32[]{:S(2)}) collective-permute-start(bf16[1,1,72,2304]{3,2,1,0:T(8,128)(2,1)S(1)} %get-tuple-element.279), channel_id=1, source_target_pairs={{0,4},{4,8},{8,12},{12,14},{14,10},{10,6},{6,2},{2,0},{1,5},{5,9},... | collective-permute-start | bytes 995336 | tf_op jit(solution)/shard_map/ppermute | solution.py:488
  589.9 20.9 %collective-permute-start.42 = (bf16[1,1,144,1152]{3,2,1,0:T(8,128)(2,1)S(1)}, bf16[1,1,144,1152]{3,2,1,0:T(8,128)(2,1)S(1)}, u32[]{:S(2)}, u32[]{:S(2)}) collective-permute-start(bf16[1,1,144,1152]{3,2,1,0:T(8,128)(2,1)S(1)} %get-tuple-element.281), channel_id=1, source_target_pairs={{4,0},{8,4},{12,8},{14,12},{10,14},{6,10},{2,6},{0,2},{5,1},{9,5},... | collective-permute-start | bytes 995336 | tf_op jit(solution)/shard_map/ppermute | solution.py:488
  595.9 21.0 %collective-permute-start.43 = (bf16[1,1,144,1152]{3,2,1,0:T(8,128)(2,1)S(1)}, bf16[1,1,144,1152]{3,2,1,0:T(8,128)(2,1)S(1)}, u32[]{:S(2)}, u32[]{:S(2)}) collective-permute-start(bf16[1,1,144,1152]{3,2,1,0:T(8,128)(2,1)S(1)} %collective-permute-done.41), channel_id=1, source_target_pairs={{0,4},{4,8},{8,12},{12,14},{14,10},{10,6},{6,2},{2,0},{1,5},{5,9},... | collective-permute-start | bytes 995336 | tf_op jit(solution)/shard_map/ppermute | solution.py:488
  617.7 20.5 %collective-permute-start.45 = (bf16[1,1,144,1152]{3,2,1,0:T(8,128)(2,1)S(1)}, bf16[1,1,144,1152]{3,2,1,0:T(8,128)(2,1)S(1)}, u32[]{:S(2)}, u32[]{:S(2)}) collective-permute-start(bf16[1,1,144,1152]{3,2,1,0:T(8,128)(2,1)S(1)} %collective-permute-done.43), channel_id=1, source_target_pairs={{0,4},{4,8},{8,12},{12,14},{14,10},{10,6},{6,2},{2,0},{1,5},{5,9},... | collective-permute-start | bytes 995336 | tf_op jit(solution)/shard_map/ppermute | solution.py:488
  639.0 20.5 %collective-permute-start.47 = (bf16[1,1,144,1152]{3,2,1,0:T(8,128)(2,1)S(1)}, bf16[1,1,144,1152]{3,2,1,0:T(8,128)(2,1)S(1)}, u32[]{:S(2)}, u32[]{:S(2)}) collective-permute-start(bf16[1,1,144,1152]{3,2,1,0:T(8,128)(2,1)S(1)} %collective-permute-done.45), channel_id=1, source_target_pairs={{0,4},{4,8},{8,12},{12,14},{14,10},{10,6},{6,2},{2,0},{1,5},{5,9},... | collective-permute-start | bytes 995336 | tf_op jit(solution)/shard_map/ppermute | solution.py:488
  660.4 20.5 %collective-permute-start.49 = (bf16[1,1,144,1152]{3,2,1,0:T(8,128)(2,1)S(1)}, bf16[1,1,144,1152]{3,2,1,0:T(8,128)(2,1)S(1)}, u32[]{:S(2)}, u32[]{:S(2)}) collective-permute-start(bf16[1,1,144,1152]{3,2,1,0:T(8,128)(2,1)S(1)} %collective-permute-done.47), channel_id=1, source_target_pairs={{0,4},{4,8},{8,12},{12,14},{14,10},{10,6},{6,2},{2,0},{1,5},{5,9},... | collective-permute-start | bytes 995336 | tf_op jit(solution)/shard_map/ppermute | solution.py:488
  681.7 20.5 %collective-permute-start.51 = (bf16[1,1,144,1152]{3,2,1,0:T(8,128)(2,1)S(1)}, bf16[1,1,144,1152]{3,2,1,0:T(8,128)(2,1)S(1)}, u32[]{:S(2)}, u32[]{:S(2)}) collective-permute-start(bf16[1,1,144,1152]{3,2,1,0:T(8,128)(2,1)S(1)} %collective-permute-done.49), channel_id=1, source_target_pairs={{0,4},{4,8},{8,12},{12,14},{14,10},{10,6},{6,2},{2,0},{1,5},{5,9},... | collective-permute-start | bytes 995336 | tf_op jit(solution)/shard_map/ppermute | solution.py:488
  695.1 23.6 %collective-permute-start.115 = (bf16[1,1,144,1152]{3,2,1,0:T(8,128)(2,1)S(1)}, bf16[1,1,144,1152]{3,2,1,0:T(8,128)(2,1)S(1)}, u32[]{:S(2)}, u32[]{:S(2)}) collective-permute-start(bf16[1,1,144,1152]{3,2,1,0:T(8,128)(2,1)S(1)} %collective-permute-done.113), channel_id=1, source_target_pairs={{0,4},{4,8},{8,12},{12,14},{14,10},{10,6},{6,2},{2,0},{1,5},{5,9},... | collective-permute-start | bytes 995336 | tf_op jit(solution)/shard_map/ppermute | solution.py:488
  709.8 26.7 %collective-permute-start.116 = (bf16[1,1,144,1152]{3,2,1,0:T(8,128)(2,1)S(1)}, bf16[1,1,144,1152]{3,2,1,0:T(8,128)(2,1)}, u32[]{:S(2)}, u32[]{:S(2)}) collective-permute-start(bf16[1,1,144,1152]{3,2,1,0:T(8,128)(2,1)S(1)} %collective-permute-done.114), channel_id=1, source_target_pairs={{4,0},{8,4},{12,8},{14,12},{10,14},{6,10},{2,6},{0,2},{5,1},{9,5},... | collective-permute-start | bytes 995336 | tf_op jit(solution)/shard_map/ppermute | solution.py:488
  712.7 24.8 %collective-permute-start.87 = (bf16[1,1,72,2304]{3,2,1,0:T(8,128)(2,1)}, bf16[1,1,72,2304]{3,2,1,0:T(8,128)(2,1)}, u32[]{:S(2)}, u32[]{:S(2)}) collective-permute-start(bf16[1,1,72,2304]{3,2,1,0:T(8,128)(2,1)} %collective-permute-done.85), channel_id=1, source_target_pairs={{4,0},{8,4},{12,8},{14,12},{10,14},{6,10},{2,6},{0,2},{5,1},{9,5},... | collective-permute-start | bytes 995336 | tf_op jit(solution)/shard_map/ppermute | solution.py:488
  (135 other events, 1884.2 us)

commit v3 on v2

--- a/solution.py
+++ b/solution.py
@@ -88,7 +88,8 @@
 
 
 def layer_kernel(chunks, index_ref, mod_ref, bqv_ref, bup_ref, bod_ref, x_in,
-                 wqo, wqt, woo, wot, wuo, wut, wdo, wdt, *rest):
+                 *rest):
+    wqs, (woo, wot, wuo, wut, wdo, wdt) = rest[:2], rest[2:8]
     rest = rest[len(rest) - 30:]
     (y_out, ys, xs, h1s, qkvo, qkvt, atts, aos, h2s, preo, pret, acto, actt, mos,
      wq, wo, wu, wd, x, y, h1, qkv, att, attf, ao, h2, pre, act, mo, sems) = rest
@@ -99,7 +100,7 @@
         img = index_ref[0]
         step = wu.shape[2] // chunks
         spots = [(side, slice(place * step, (place + 1) * step)) for side in range(2) for place in range(chunks)]
-        pairs = [(x_in, x), *three_kinds((wqo, wqt), wq), (woo, wo.at[0]), (wot, wo.at[1])]
+        pairs = [(x_in, x), *three_kinds(wqs, wq), (woo, wo.at[0]), (wot, wo.at[1])]
         for side, spot in spots:
             up, down = ((wuo, wdo), (wut, wdt))[side]
             pairs += [(up.at[:, spot], wu.at[side, :, spot]), (down.at[spot, :], wd.at[side, spot, :])]
@@ -116,7 +117,7 @@
         for part in range(6):
             side, kind = part // 3, part % 3
             stream.take()
-            mixed = nn(h1[...], wq[side, kind])
+            mixed = nt(h1[...], wq[side, kind])
             qkv[side, kind] = (mixed + bqv_ref[part : part + 1]).astype(BF)
         pending += [copies.start(qkv.at[0], qkvo.at[img]), copies.start(qkv.at[1], qkvt.at[img])]
 
@@ -189,7 +190,7 @@
     saved = tuple(saved) if saved is not None else ()
     aliases = {14 + i: 1 + i for i in range(len(saved))}
     scratch = [
-        pltpu.VMEM((2, 3, width, half), BF),
+        pltpu.VMEM((2, 3, half, width), BF),
         pltpu.VMEM((2, half, width), BF),
         pltpu.VMEM((2, width, hidden), BF),
         pltpu.VMEM((2, hidden, width), BF),
@@ -310,7 +311,8 @@
     )(index, mods, grad, xs, aos, mos, preo, pret, *weights, *kept)
 
 
-def attn_back_kernel(index_ref, mod_ref, mg_in, xs, aos, qkvo, qkvt, wqo, wqt, woo, wot, *rest):
+def attn_back_kernel(index_ref, mod_ref, mg_in, xs, aos, qkvo, qkvt, *rest):
+    wqs, (woo, wot) = rest[:2], rest[2:4]
     rest = rest[len(rest) - 22:]
     (rg_out, rgs, sums, bqvs, ois, qgo, qgt, wq, wo, mg, rg, x, ao, qkv, oi, qg, da, acc, ng, total, bqv, sems) = rest
 
@@ -320,7 +322,7 @@
         img = index_ref[0]
         stream = Stream(copies, DEPTH, [
             (mg_in, mg), (woo, wo.at[0]), (wot, wo.at[1]), (qkvo.at[img], qkv.at[0]), (qkvt.at[img], qkv.at[1]),
-            *three_kinds((wqo, wqt), wq), (aos.at[img], ao), (xs.at[img], x)])
+            *three_kinds(wqs, wq), (aos.at[img], ao), (xs.at[img], x)])
         half = wo.shape[1]
         size = 2 * half // HEADS
         scale = size ** (-0.5)
@@ -361,7 +363,7 @@
         for part in range(6):
             side, kind = part // 3, part % 3
             stream.take()
-            term = nt(qg[side, kind], wq[side, kind])
+            term = nn(qg[side, kind], wq[side, kind])
             ng[...] = term if part == 0 else ng[...] + term
             bqv[part : part + 1] = jnp.sum(qg[side, kind].astype(F32), axis=0, keepdims=True)
         pending.append(copies.start(bqv, bqvs.at[img]))
@@ -389,7 +391,7 @@
     kept = tuple(kept) if kept is not None else ()
     aliases = {11 + i: 1 + i for i in range(len(kept))}
     scratch = [
-        pltpu.VMEM((2, 3, width, half), BF),
+        pltpu.VMEM((2, 3, half, width), BF),
         pltpu.VMEM((2, half, width), BF),
         pltpu.VMEM((tokens, width), F32),
         pltpu.VMEM((tokens, width), BF),
@@ -454,39 +456,84 @@
     return array
 
 
-def ring_order(peers):
+def ring_pairs(peers):
     order = list(range(0, peers, 2)) + list(range(1, peers, 2))[::-1]
-    place = [order.index(peer) for peer in range(peers)]
     ahead = [(order[i], order[(i + 1) % peers]) for i in range(peers)]
-    return place, ahead, [(b, a) for a, b in ahead]
-
-
-def ring_sum(terms):
+    return ahead, [(b, a) for a, b in ahead]
+
+
+def ring_spots():
     peers = lax.axis_size("dp")
-    place, ahead, behind = ring_order(peers)
-    here = jnp.asarray(place, jnp.int32)[lax.axis_index("dp")]
+    device = lax.axis_index("dp").astype(jnp.uint32)
+    here = jnp.where(device % 2 == 0, device // 2, peers - 1 - device // 2)
+    return [(here + step) & jnp.uint32(peers - 1) for step in range(peers)]
+
+
+def ring_sum(terms, spots, totals, write):
+    peers = len(spots)
     count, width = terms.shape
     part = count // (2 * peers)
     blocks = terms.reshape(2, peers, part, width)
-    total = jnp.zeros((2, peers, part, width), F32)
-    lanes = ((ahead, 1), (behind, -1))
-
-    def block(side, number):
-        return lax.dynamic_slice(blocks, (side, number % peers, 0, 0), (1, 1, part, width))
-
-    moving = [block(side, here) for side in range(2)]
+    lanes = tuple(zip(ring_pairs(peers), (1, -1)))
+    none = jnp.uint32(0)
+
+    def block(side, step):
+        start = (jnp.uint32(side), spots[step % peers], none, none)
+        return lax.dynamic_slice(blocks, start, (1, 1, part, width))[0]
+
+    moving = [block(side, 0) for side in range(2)]
     for step in range(1, peers):
         for side, (pairs, sign) in enumerate(lanes):
             came = lax.ppermute(moving[side], "dp", pairs)
-            mine = block(side, here - sign * step)
+            mine = block(side, -sign * step)
             moving[side] = (came.astype(F32) + mine.astype(F32)).astype(BF)
     for step in range(peers):
         for side, (pairs, sign) in enumerate(lanes):
-            owner = (here - sign * (peers - 1 + step)) % peers
-            total = lax.dynamic_update_slice(total, moving[side].astype(F32), (side, owner, 0, 0))
+            spot = spots[-sign * (peers - 1 + step) % peers]
+            totals = write(totals, side, spot, moving[side].astype(F32))
             if step < peers - 1:
                 moving[side] = lax.ppermute(moving[side], "dp", pairs)
-    return total.reshape(count, width)
+    return totals
+
+
+def put(total, block, spot):
+    none = jnp.uint32(0)
+    return lax.dynamic_update_slice(total, block, (spot, none, none))
+
+
+def put_if(total, block, spot, keep):
+    none = jnp.uint32(0)
+    old = lax.dynamic_slice(total, (spot, none, none), block.shape)
+    return put(total, jnp.where(keep, block, old), spot)
+
+
+def ring_plain(terms, spots):
+    peers = len(spots)
+    count, width = terms.shape
+
+    def write(total, side, spot, block):
+        return put(total, block, spot + jnp.uint32(side * peers))
+
+    total = jnp.zeros((2 * peers, count // (2 * peers), width), F32)
+    return ring_sum(terms, spots, total, write).reshape(count, width)
+
+
+def ring_attn(terms, spots):
+    peers = len(spots)
+    count, width = terms.shape
+    part, quarter = count // (2 * peers), jnp.uint32(peers // 2)
+
+    def write(totals, side, spot, block):
+        qkv, out = totals
+        if side == 0:
+            return put(qkv, block, spot), out
+        early = spot < quarter
+        qkv = put_if(qkv, block, jnp.uint32(peers) + jnp.minimum(spot, quarter - 1), early)
+        return qkv, put_if(out, block, jnp.maximum(spot, quarter) - quarter, ~early)
+
+    totals = (jnp.zeros((3 * peers // 2, part, width), F32), jnp.zeros((peers // 2, part, width), F32))
+    qkv, out = ring_sum(terms, spots, totals, write)
+    return qkv.reshape(3, count // 4, width), out.reshape(count // 4, width)
 
 
 def folded(other, own):
@@ -518,25 +565,20 @@
     def by_core(first_val, later_val):
         return jnp.where(core == 0, first_val, later_val)
 
-    def mine(array, axis):
-        return lax.dynamic_slice_in_dim(array, core * images, images, axis)
-
-    def others(array, axis):
-        return lax.dynamic_slice_in_dim(array, (1 - core) * images, images, axis)
-
     def in_order(own, came, axis):
         return by_core(jnp.concatenate([own, came], axis), jnp.concatenate([came, own], axis))
 
     def whole_images(rows):
-        came = swap(others(rows, 1))
-        return jnp.moveaxis(jnp.concatenate([mine(rows, 1), came], axis=0), 1, 0)
+        for i in range(images):
+            early, later = rows[:, i], rows[:, images + i]
+            yield jnp.concatenate([by_core(early, later), swap(by_core(later, early))], axis=0)
 
     def split_images(rows):
         local = rows.shape[1] // 2
         came = swap(rows[:, local:])
         return jnp.moveaxis(in_order(rows[:, :local], came, 0), 0, 1)[None]
 
-    qkv_own = lax.optimization_barrier(jnp.moveaxis(qkv_weight[0], 1, 0))
+    qkv_own = jnp.transpose(qkv_weight[0], (1, 2, 0))
     w_qkv = (qkv_own, swap(qkv_own))
     w_out = (out_weight[0], swap(out_weight[0]))
     w_up = (up_weight[0], swap(up_weight[0]))
@@ -549,7 +591,8 @@
     mod_local = (
         jnp.dot(silu_b, ada_weight[0], preferred_element_type=F32) + ada_bias[0].astype(F32)[None]
     )
-    modulation = in_order(mine(mod_local, 0), swap(others(mod_local, 0)), 1).reshape(images, 6, width)
+    early, later = mod_local[:images], mod_local[images:]
+    modulation = in_order(by_core(early, later), swap(by_core(later, early)), 1).reshape(images, 6, width)
     slot_no = core * images + jnp.arange(images, dtype=jnp.int32)
     valid = (slot_no < counts[0]).astype(F32)
     mods = jnp.concatenate(
@@ -564,13 +607,13 @@
     bup = pair_bias[:, 2 * half :]
     bod = jnp.concatenate([out_bias, down_bias], axis=0).astype(F32)
 
-    rows_in = whole_images(images_in)
-    cotangent = whole_images(out_cotangent)
+    rows_in = list(whole_images(images_in))
+    cotangent = list(whole_images(out_cotangent))
 
     def turn_index(number, is_active):
         return jnp.stack([jnp.int32(number), is_active.astype(jnp.int32)])
 
-    inputs, saved = [rows_in[i] for i in range(images)], None
+    inputs, saved = list(rows_in), None
     for turn in range(2 * images):
         number, is_early = turn % images, turn < images
         answer = layer_call(
@@ -582,34 +625,40 @@
     ys, xs, h1s, qkvo, qkvt, atts, aos, h2s, preo, pret, acto, actt, mos = saved
     layer_out = split_images(ys)
 
-    inputs, mlp_kept, attn_kept = [cotangent[i] for i in range(images)], None, None
+    inputs, mlp_kept, attn_kept = list(cotangent), None, None
+    spots = ring_spots()
     for turn in range(2 * images):
         number, is_early = turn % images, turn < images
         index = turn_index(number, is_first != is_early)
+        grad = inputs[turn]
+        if attn_kept is not None:
+            grad, attn_kept[1] = lax.optimization_barrier((grad, attn_kept[1]))
         answer = mlp_back_call(
-            index, inputs[turn], mods, (xs, aos, mos, preo, pret), (*w_up, *w_down), mlp_kept, images
+            index, grad, mods, (xs, aos, mos, preo, pret), (*w_up, *w_down), mlp_kept, images
         )
         middle_grad, mlp_kept = answer[0], answer[1:]
+        if turn == 2 * images - 1:
+            mlp_sums, up_sums, down_ins, pre_grads_o, pre_grads_t = mlp_kept
+            down_w = folded(outer(actt, down_ins), outer(acto, down_ins))
+            up_w = folded(outer(h2s, pre_grads_t), outer(h2s, pre_grads_o))
+            middle_grad, down_w = lax.optimization_barrier((middle_grad, down_w))
         answer = attn_back_call(
             index, middle_grad, mods, (xs, aos, qkvo, qkvt), (*w_qkv, *w_out), attn_kept, images
         )
-        attn_kept = answer[1:]
+        attn_kept = list(answer[1:])
         if is_early:
             inputs.append(lax.ppermute(answer[0], "section", [(1, 0)]))
-    mlp_sums, up_sums, down_ins, pre_grads_o, pre_grads_t = mlp_kept
     row_grads, attn_sums, qkv_sums, out_ins, qkv_grads_o, qkv_grads_t = attn_kept
     in_grad = split_images(row_grads)
 
-    down_w = folded(outer(actt, down_ins), outer(acto, down_ins))
-    up_w = folded(outer(h2s, pre_grads_t), outer(h2s, pre_grads_o))
     stacked = 3 * half
     attn_w = folded(
         jnp.concatenate([outers(qkv_grads_t, h1s).reshape(stacked, width), outer(atts[:, 1], out_ins)]),
         jnp.concatenate([outers(qkv_grads_o, h1s).reshape(stacked, width), outer(atts[:, 0], out_ins)]),
     )
-    down_w_sum, up_w_sum, attn_w_sum = ring_sum(down_w), ring_sum(up_w), ring_sum(attn_w)
-    qkv_w_sum = jnp.moveaxis(attn_w_sum[:stacked].reshape(3, half, width), 2, 0)
-    out_w_sum = attn_w_sum[stacked:]
+    down_w_sum, up_w_sum = ring_plain(down_w, spots), ring_plain(up_w, spots)
+    qkv_w_sum, out_w_sum = ring_attn(attn_w, spots)
+    qkv_w_sum = jnp.transpose(qkv_w_sum, (2, 0, 1))
 
     mod_grad = jnp.concatenate([attn_sums[:, :3], mlp_sums[:, :3]], axis=1).astype(BF)
     columns = mod_grad.reshape(images, 2, 3 * width)

time: 752 us -> 723 us (0.961)
  waiting for transfers between devices: 269 us -> 303 us
  local copies, waits for them, and re-layouts: 58.9 us -> 31 us
  between operations: 24 us -> 2.86 us
  starting transfers between devices: 130 us -> 116 us
    ppermute x42, waiting for transfers between devices: 95.6 us -> 129 us  [ring_sum(): came = lax.ppermute(moving[side], 'dp', pairs)]
    ppermute x2, waiting for transfers between devices: 66.4 us -> 48.1 us  [shards(): inputs.append(lax.ppermute(answer[0], 'section', [(1, 0)]))]
    dynamic_update_slice x48, other arithmetic: 23.3 us -> 6.32 us  [put(): return lax.dynamic_update_slice(total, block, (spot, none, none))]
    ppermute x42, waiting for transfers between devices: 83.6 us -> 97.6 us  [ring_sum(): moving[side] = lax.ppermute(moving[side], 'dp', pairs)]
    unnamed x110 -> x109, local copies, waits for them, and re-layouts: 19.6 us -> 13 us
  transfers between devices with their start and end apart: 117 -> 119, of which waited for: 53 -> 72; matrix products, arithmetic and copies ran while one was open for 21% -> 15% of each run, Pallas kernels for 16% -> 14%
where the time goes in v3:
time: 723 us; the launch traced here: 716 us
  waiting for transfers between devices  303 us (42%)
  Pallas kernels  157 us (22%)
  starting transfers between devices  116 us (16%)
  matrix products  60.5 us (8%)
  other arithmetic  46 us (6%)
  local copies, waits for them, and re-layouts  31 us (4%)
    ppermute x42, waiting for transfers between devices, ring_sum(): came = lax.ppermute(moving[side], 'dp', pairs)  129 us
    ppermute x42, waiting for transfers between devices, ring_sum(): moving[side] = lax.ppermute(moving[side], 'dp', pairs)  97.6 us
    pallas_call x4, Pallas kernels, layer_call(): pl.pallas_call(functools.partial(layer_kernel, chunks), out_shape=outs, i...  66.8 us
    pallas_call x4, Pallas kernels, attn_back_call(): pl.pallas_call(attn_back_kernel, out_shape=(sd((tokens, width), BF), sd((...  50.2 us
    ppermute x2, waiting for transfers between devices, shards(): inputs.append(lax.ppermute(answer[0], 'section', [(1, 0)]))  48.1 us
    ppermute x42, starting transfers between devices, ring_sum(): moving[side] = lax.ppermute(moving[side], 'dp', pairs)  44.9 us
    ppermute x42, starting transfers between devices, ring_sum(): came = lax.ppermute(moving[side], 'dp', pairs)  42 us
    pallas_call x4, Pallas kernels, mlp_back_call(): pl.pallas_call(functools.partial(mlp_back_kernel, chunks), out_shape=(sd(...  39.7 us
  transfers between devices with their start and end apart: 119, of which 72 were waited for; matrix products, arithmetic and copies ran while one was open for 15% of the time, Pallas kernels for 14%

profile of v3, /device:TPU:0, one launch (start us, length us, event | category | flops | bytes accessed | tf_op | source)
XLA Modules:
  0.0 715.9 jit_solution(6927491623423837629)
XLA Ops:
  42.3 24.9 %layer.4 = (bf16[256,1152]{1,0:T(8,128)(2,1)}, bf16[2,256,1152]{2,1,0:T(8,128)(2,1)}, bf16[2,256,1152]{2,1,0:T(8,128)(2,1)}, bf16[2,256,1152]{2,1,0:T(8,128)(2,1...) custom-call(s32[2]{0:T(128)} %pad_add_fusion.5.index_ref, ...), custom_call_target="tpu_custom_call" | custom-call | flops 8153726976 | bytes 31850496 | tf_op jit(solution)/shard_map/layer/pallas_call | solution.py:210
  68.5 25.3 %layer.5 = (bf16[256,1152]{1,0:T(8,128)(2,1)}, bf16[2,256,1152]{2,1,0:T(8,128)(2,1)}, bf16[2,256,1152]{2,1,0:T(8,128)(2,1)}, bf16[2,256,1152]{2,1,0:T(8,128)(2,1...) custom-call(s32[2]{0:T(128)} %pad_add_fusion.1.index_ref, ...), custom_call_target="tpu_custom_call", output_to_operand_aliasing={{1}: (14, {}), {2}: (15, {}), {3}: (16, {}), {4}: (17, {}),... | custom-call | flops 8153726976 | bytes 31850496 | tf_op jit(solution)/shard_map/layer/pallas_call | solution.py:210
  96.0 7.9 %layer.6 = (bf16[256,1152]{1,0:T(8,128)(2,1)}, bf16[2,256,1152]{2,1,0:T(8,128)(2,1)}, bf16[2,256,1152]{2,1,0:T(8,128)(2,1)}, bf16[2,256,1152]{2,1,0:T(8,128)(2,1...) custom-call(s32[2]{0:T(128)} %pad_add_fusion.4.index_ref, ...), custom_call_target="tpu_custom_call", output_to_operand_aliasing={{1}: (14, {}), {2}: (15, {}), {3}: (16, {}), {4}: (17, {}),... | custom-call | flops 8153726976 | bytes 31850496 | tf_op jit(solution)/shard_map/layer/pallas_call | solution.py:210
  109.4 8.8 %layer.7 = (bf16[256,1152]{1,0:T(8,128)(2,1)}, bf16[2,256,1152]{2,1,0:T(8,128)(2,1)}, bf16[2,256,1152]{2,1,0:T(8,128)(2,1)}, bf16[2,256,1152]{2,1,0:T(8,128)(2,1...) custom-call(s32[2]{0:T(128)} %pad_add_fusion.2.index_ref, ...), custom_call_target="tpu_custom_call", output_to_operand_aliasing={{1}: (14, {}), {2}: (15, {}), {3}: (16, {}), {4}: (17, {}),... | custom-call | flops 8153726976 | bytes 31850496 | tf_op jit(solution)/shard_map/layer/pallas_call | solution.py:210
  125.6 5.7 mlp_back.5
  131.3 6.3 attn_back.5
  138.9 47.8 %collective-permute-done.14.g_in = bf16[256,1152]{1,0:T(8,128)(2,1)S(1)} collective-permute-done((bf16[256,1152]{1,0:T(8,128)(2,1)}, bf16[256,1152]{1,0:T(8,128)(2,1)S(1)}, u32[]{:S(2)}, u32[]{:S(2)}) %collective-permute-start.14) | collective-permute-done | bytes 589856 | tf_op jit(solution)/shard_map/ppermute | solution.py:650
  187.5 16.3 %mlp_back.6 = (f32[256,1152]{1,0:T(8,128)}, f32[2,8,1152]{2,1,0:T(8,128)}, f32[2,2,2304]{2,1,0:T(2,128)}, bf16[2,256,1152]{2,1,0:T(8,128)(2,1)}, bf16[2,256,2304...) custom-call(s32[2]{0:T(128)} %pad_add_fusion.5.index_ref, ...), custom_call_target="tpu_custom_call", output_to_operand_aliasing={{1}: (12, {}), {2}: (13, {}), {3}: (14, {}), {4}: (15, {}),... | custom-call | flops 5435817984 | bytes 21233664 | tf_op jit(solution)/shard_map/mlp_back/pallas_call | solution.py:299
  203.8 19.5 %attn_back.6 = (bf16[256,1152]{1,0:T(8,128)(2,1)}, bf16[2,256,1152]{2,1,0:T(8,128)(2,1)}, f32[2,8,1152]{2,1,0:T(8,128)}, f32[2,8,576]{2,1,0:T(8,128)}, bf16[2,25...) custom-call(s32[2]{0:T(128)} %pad_add_fusion.5.index_ref, ...), custom_call_target="tpu_custom_call", output_to_operand_aliasing={{1}: (11, {}), {2}: (12, {}), {3}: (13, {}), {4}: (14, {}),... | custom-call | flops 2717908992 | bytes 10616832 | tf_op jit(solution)/shard_map/attn_back/pallas_call | solution.py:410
  224.4 16.4 %mlp_back.7 = (f32[256,1152]{1,0:T(8,128)}, f32[2,8,1152]{2,1,0:T(8,128)}, f32[2,2,2304]{2,1,0:T(2,128)}, bf16[2,256,1152]{2,1,0:T(8,128)(2,1)}, bf16[2,256,2304...) custom-call(s32[2]{0:T(128)} %pad_add_fusion.1.index_ref, ...), custom_call_target="tpu_custom_call", output_to_operand_aliasing={{1}: (12, {}), {2}: (13, {}), {3}: (14, {}), {4}: (15, {}),... | custom-call | flops 5435817984 | bytes 21233664 | tf_op jit(solution)/shard_map/mlp_back/pallas_call | solution.py:299
  240.9 7.8 %fusion.3 = bf16[2304,1152]{1,0:T(8,128)(2,1)} fusion(bf16[2,256,2304]{2,1,0:T(8,128)(2,1)} %get-tuple-element.216, bf16[2,256,1152]{2,1,0:T(8,128)(2,1)} %get-tuple-element.215), kind=kOutput, calls=%fused_computation.9 | convolution fusion | flops 2720563200 | bytes 8847360 | tf_op jit(solution)/shard_map/btk,btd->kd/dot_general | solution.py:545
  256.4 7.1 fusion.5
  272.0 6.5 fusion.2
  281.5 19.7 %attn_back.7 = (bf16[256,1152]{1,0:T(8,128)(2,1)}, bf16[2,256,1152]{2,1,0:T(8,128)(2,1)}, f32[2,8,1152]{2,1,0:T(8,128)}, f32[2,8,576]{2,1,0:T(8,128)}, bf16[2,25...) custom-call(s32[2]{0:T(128)} %pad_add_fusion.1.index_ref, ...), custom_call_target="tpu_custom_call", output_to_operand_aliasing={{1}: (11, {}), {2}: (12, {}), {3}: (13, {}), {4}: (14, {}),... | custom-call | flops 2717908992 | bytes 10616832 | tf_op jit(solution)/shard_map/attn_back/pallas_call | solution.py:410
  313.9 6.0 fusion.4
  319.9 5.8 fusion.18
  370.8 9.3 %convolution_bitcast_fusion = f32[1,1152,3456]{2,1,0:T(8,128)} fusion(bf16[16,1152]{1,0:T(8,128)(2,1)} %collective-permute-done.25, bf16[16,1152]{1,0:T(8,128)(2,1)S(1)} %maximum_select_fusion.12, pred[]{:T(512)S(6)} %eq.27, bf16[16,3456]{1,0:T(8,128)(2,1)S(1)} %collective-permute-done.28, bf16[16,3456]{1,0:T(8,128)(2,1)S(1)} %maximum_select_fusion.4), kind=kOutput, calls=%fused_computation.1 | convolution fusion | flops 256131072 | bytes 16220161 | tf_op jit(solution)/shard_map/sd,sk->dk/dot_general | solution.py:679
  385.2 7.0 collective-permute-done.92
  475.3 7.8 %collective-permute-done.76 = bf16[1,72,2304]{2,1,0:T(8,128)(2,1)S(1)} collective-permute-done((bf16[1,72,2304]{2,1,0:T(8,128)(2,1)S(1)}, bf16[1,72,2304]{2,1,0:T(8,128)(2,1)S(1)}, u32[]{:S(2)}, u32[]{:S(2)}) %collective-permute-start.76) | collective-permute-done | bytes 331808 | tf_op jit(solution)/shard_map/ppermute | solution.py:487
  558.8 5.6 fusion.6
  566.6 8.2 %collective-permute-done.30 = bf16[1,144,1152]{2,1,0:T(8,128)(2,1)S(1)} collective-permute-done((bf16[1,144,1152]{2,1,0:T(8,128)(2,1)S(1)}, bf16[1,144,1152]{2,1,0:T(8,128)(2,1)S(1)}, u32[]{:S(2)}, u32[]{:S(2)}) %collective-permute-start.30) | collective-permute-done | bytes 331808 | tf_op jit(solution)/shard_map/ppermute | solution.py:487
  579.2 9.0 %collective-permute-done.31 = bf16[1,144,1152]{2,1,0:T(8,128)(2,1)S(1)} collective-permute-done((bf16[1,144,1152]{2,1,0:T(8,128)(2,1)S(1)}, bf16[1,144,1152]{2,1,0:T(8,128)(2,1)S(1)}, u32[]{:S(2)}, u32[]{:S(2)}) %collective-permute-start.31) | collective-permute-done | bytes 331808 | tf_op jit(solution)/shard_map/ppermute | solution.py:487
  598.1 7.3 %collective-permute-done.39 = bf16[1,144,1152]{2,1,0:T(8,128)(2,1)S(1)} collective-permute-done((bf16[1,144,1152]{2,1,0:T(8,128)(2,1)S(1)}, bf16[1,144,1152]{2,1,0:T(8,128)(2,1)S(1)}, u32[]{:S(2)}, u32[]{:S(2)}) %collective-permute-start.39) | collective-permute-done | bytes 331808 | tf_op jit(solution)/shard_map/ppermute | solution.py:487
  607.7 8.6 %collective-permute-done.33 = bf16[1,144,1152]{2,1,0:T(8,128)(2,1)S(1)} collective-permute-done((bf16[1,144,1152]{2,1,0:T(8,128)(2,1)S(1)}, bf16[1,144,1152]{2,1,0:T(8,128)(2,1)S(1)}, u32[]{:S(2)}, u32[]{:S(2)}) %collective-permute-start.33) | collective-permute-done | bytes 331808 | tf_op jit(solution)/shard_map/ppermute | solution.py:487
  618.6 7.7 %collective-permute-done.34 = bf16[1,144,1152]{2,1,0:T(8,128)(2,1)S(1)} collective-permute-done((bf16[1,144,1152]{2,1,0:T(8,128)(2,1)S(1)}, bf16[1,144,1152]{2,1,0:T(8,128)(2,1)S(1)}, u32[]{:S(2)}, u32[]{:S(2)}) %collective-permute-start.34) | collective-permute-done | bytes 331808 | tf_op jit(solution)/shard_map/ppermute | solution.py:487
  629.9 6.8 collective-permute-done.35
  640.8 6.4 collective-permute-done.36
  651.3 7.5 %collective-permute-done.44 = bf16[1,144,1152]{2,1,0:T(8,128)(2,1)S(1)} collective-permute-done((bf16[1,144,1152]{2,1,0:T(8,128)(2,1)S(1)}, bf16[1,144,1152]{2,1,0:T(8,128)(2,1)S(1)}, u32[]{:S(2)}, u32[]{:S(2)}) %collective-permute-start.44) | collective-permute-done | bytes 331808 | tf_op jit(solution)/shard_map/ppermute | solution.py:495
  661.2 8.0 %collective-permute-done.46 = bf16[1,144,1152]{2,1,0:T(8,128)(2,1)S(1)} collective-permute-done((bf16[1,144,1152]{2,1,0:T(8,128)(2,1)S(1)}, bf16[1,144,1152]{2,1,0:T(8,128)(2,1)S(1)}, u32[]{:S(2)}, u32[]{:S(2)}) %collective-permute-start.46) | collective-permute-done | bytes 331808 | tf_op jit(solution)/shard_map/ppermute | solution.py:495
  671.7 7.5 %collective-permute-done.48 = bf16[1,144,1152]{2,1,0:T(8,128)(2,1)S(1)} collective-permute-done((bf16[1,144,1152]{2,1,0:T(8,128)(2,1)S(1)}, bf16[1,144,1152]{2,1,0:T(8,128)(2,1)S(1)}, u32[]{:S(2)}, u32[]{:S(2)}) %collective-permute-start.48) | collective-permute-done | bytes 331808 | tf_op jit(solution)/shard_map/ppermute | solution.py:495
  681.6 6.8 collective-permute-done.50
  690.8 5.9 collective-permute-done.52
  (503 shorter events, 362.2 us)
Async XLA Ops:
  10.0 18.1 %collective-permute-start = (f32[2,3456]{1,0:T(2,128)S(1)}, f32[2,3456]{1,0:T(2,128)}, u32[]{:S(2)}, u32[]{:S(2)}) collective-permute-start(f32[2,3456]{1,0:T(2,128)S(1)} %get-tuple-element.363), channel_id=1, source_target_pairs={{0,1},{1,0},{2,3},{3,2},{4,5},{5,4},{6,7},{7,6},{8,9},{9,8},{10,11... | collective-permute-start | bytes 82952 | tf_op jit(solution)/shard_map/ppermute | solution.py:434
  10.7 16.6 %collective-permute-start.1 = (bf16[1,3456]{1,0:T(2,128)(2,1)S(1)}, bf16[1,3456]{1,0:T(2,128)(2,1)S(1)}, u32[]{:S(2)}, u32[]{:S(2)}) collective-permute-start(bf16[1,3456]{1,0:T(2,128)(2,1)S(1)} %broadcast_in_dim.68), channel_id=1, source_target_pairs={{0,1},{1,0},{2,3},{3,2},{4,5},{5,4},{6,7},{7,6},{8,9},{9,8},{10,11... | collective-permute-start | bytes 20744 | tf_op jit(solution)/shard_map/ppermute | solution.py:434
  10.9 30.4 %collective-permute-start.5 = (bf16[1152,2304]{1,0:T(8,128)(2,1)}, bf16[1152,2304]{1,0:T(8,128)(2,1)}, u32[]{:S(2)}, u32[]{:S(2)}) collective-permute-start(bf16[1152,2304]{1,0:T(8,128)(2,1)} %bitcast.270), channel_id=1, source_target_pairs={{0,1},{1,0},{2,3},{3,2},{4,5},{5,4},{6,7},{7,6},{8,9},{9,8},{10,11... | collective-permute-start | bytes 15925256 | tf_op jit(solution)/shard_map/ppermute | solution.py:434
  11.3 30.0 %collective-permute-start.6 = (bf16[2304,1152]{1,0:T(8,128)(2,1)}, bf16[2304,1152]{1,0:T(8,128)(2,1)}, u32[]{:S(2)}, u32[]{:S(2)}) collective-permute-start(bf16[2304,1152]{1,0:T(8,128)(2,1)} %bitcast.279), channel_id=1, source_target_pairs={{0,1},{1,0},{2,3},{3,2},{4,5},{5,4},{6,7},{7,6},{8,9},{9,8},{10,11... | collective-permute-start | bytes 15925256 | tf_op jit(solution)/shard_map/ppermute | solution.py:434
  11.4 29.9 %collective-permute-start.3 = (bf16[3,576,1152]{2,1,0:T(8,128)(2,1)}, bf16[3,576,1152]{2,1,0:T(8,128)(2,1)}, u32[]{:S(2)}, u32[]{:S(2)}) collective-permute-start(bf16[3,576,1152]{2,1,0:T(8,128)(2,1)} %bitcast.288), channel_id=1, source_target_pairs={{0,1},{1,0},{2,3},{3,2},{4,5},{5,4},{6,7},{7,6},{8,9},{9,8},{10,11... | collective-permute-start | bytes 11943944 | tf_op jit(solution)/shard_map/ppermute | solution.py:434
  67.2 28.0 %collective-permute-start.9 = (bf16[256,1152]{1,0:T(8,128)(2,1)}, bf16[256,1152]{1,0:T(8,128)(2,1)S(1)}, u32[]{:S(2)}, u32[]{:S(2)}) collective-permute-start(bf16[256,1152]{1,0:T(8,128)(2,1)} %get-tuple-element.140), channel_id=1, source_target_pairs={{0,16},{1,17},{2,18},{3,19},{4,20},{5,21},{6,22},{7,23},{8,24},{9,... | collective-permute-start | bytes 1769480 | tf_op jit(solution)/shard_map/ppermute | solution.py:624
  93.8 14.8 %collective-permute-start.8 = (bf16[256,1152]{1,0:T(8,128)(2,1)}, bf16[256,1152]{1,0:T(8,128)(2,1)S(1)}, u32[]{:S(2)}, u32[]{:S(2)}) collective-permute-start(bf16[256,1152]{1,0:T(8,128)(2,1)} %get-tuple-element.139), channel_id=1, source_target_pairs={{0,16},{1,17},{2,18},{3,19},{4,20},{5,21},{6,22},{7,23},{8,24},{9,... | collective-permute-start | bytes 1769480 | tf_op jit(solution)/shard_map/ppermute | solution.py:624
  124.3 62.4 %collective-permute-start.14 = (bf16[256,1152]{1,0:T(8,128)(2,1)}, bf16[256,1152]{1,0:T(8,128)(2,1)S(1)}, u32[]{:S(2)}, u32[]{:S(2)}) collective-permute-start(bf16[256,1152]{1,0:T(8,128)(2,1)} %get-tuple-element.191), channel_id=1, source_target_pairs={{16,0},{17,1},{18,2},{19,3},{20,4},{21,5},{22,6},{23,7},{24,8},{25... | collective-permute-start | bytes 1769480 | tf_op jit(solution)/shard_map/ppermute | solution.py:650
  137.6 86.0 %collective-permute-start.13 = (bf16[256,1152]{1,0:T(8,128)(2,1)}, bf16[256,1152]{1,0:T(8,128)(2,1)S(1)}, u32[]{:S(2)}, u32[]{:S(2)}) collective-permute-start(bf16[256,1152]{1,0:T(8,128)(2,1)} %get-tuple-element.190), channel_id=1, source_target_pairs={{16,0},{17,1},{18,2},{19,3},{20,4},{21,5},{22,6},{23,7},{24,8},{25... | collective-permute-start | bytes 1769480 | tf_op jit(solution)/shard_map/ppermute | solution.py:650
  248.6 23.4 %collective-permute-start.15 = (bf16[2304,1152]{1,0:T(8,128)(2,1)}, bf16[2304,1152]{1,0:T(8,128)(2,1)}, u32[]{:S(2)}, u32[]{:S(2)}) collective-permute-start(bf16[2304,1152]{1,0:T(8,128)(2,1)} %fusion.3), channel_id=1, source_target_pairs={{0,1},{1,0},{2,3},{3,2},{4,5},{5,4},{6,7},{7,6},{8,9},{9,8},{10,11... | collective-permute-start | bytes 15925256 | tf_op jit(solution)/shard_map/ppermute | solution.py:434
  263.5 49.9 %collective-permute-start.62 = (bf16[1152,2304]{1,0:T(8,128)(2,1)}, bf16[1152,2304]{1,0:T(8,128)(2,1)}, u32[]{:S(2)}, u32[]{:S(2)}) collective-permute-start(bf16[1152,2304]{1,0:T(8,128)(2,1)} %fusion.5), channel_id=1, source_target_pairs={{0,1},{1,0},{2,3},{3,2},{4,5},{5,4},{6,7},{7,6},{8,9},{9,8},{10,11... | collective-permute-start | bytes 15925256 | tf_op jit(solution)/shard_map/ppermute | solution.py:434
  264.1 106.7 %collective-permute-start.25 = (bf16[16,1152]{1,0:T(8,128)(2,1)S(1)}, bf16[16,1152]{1,0:T(8,128)(2,1)}, u32[]{:S(2)}, u32[]{:S(2)}) collective-permute-start(bf16[16,1152]{1,0:T(8,128)(2,1)S(1)} %maximum_select_fusion.12), channel_id=1, source_target_pairs={{0,8},{2,10},{4,12},{6,14},{8,0},{10,2},{12,4},{14,6},{1,9},{3,11}... | collective-permute-start | bytes 110600 | tf_op jit(solution)/shard_map/ppermute | solution.py:448
  279.5 100.6 %collective-permute-start.91 = (bf16[1,144,1152]{2,1,0:T(8,128)(2,1)}, bf16[1,144,1152]{2,1,0:T(8,128)(2,1)}, u32[]{:S(2)}, u32[]{:S(2)}) collective-permute-start(bf16[1,144,1152]{2,1,0:T(8,128)(2,1)} %get-tuple-element.298), channel_id=1, source_target_pairs={{0,4},{4,8},{8,12},{12,14},{14,10},{10,6},{6,2},{2,0},{1,5},{5,9},... | collective-permute-start | bytes 995336 | tf_op jit(solution)/shard_map/ppermute | solution.py:487
  279.9 105.3 %collective-permute-start.98 = (bf16[1,144,1152]{2,1,0:T(8,128)(2,1)}, bf16[1,144,1152]{2,1,0:T(8,128)(2,1)}, u32[]{:S(2)}, u32[]{:S(2)}) collective-permute-start(bf16[1,144,1152]{2,1,0:T(8,128)(2,1)} %get-tuple-element.297), channel_id=1, source_target_pairs={{4,0},{8,4},{12,8},{14,12},{10,14},{6,10},{2,6},{0,2},{5,1},{9,5},... | collective-permute-start | bytes 995336 | tf_op jit(solution)/shard_map/ppermute | solution.py:487
  304.1 25.5 %collective-permute-start.58 = (f32[5760]{0:T(1024)S(1)}, f32[5760]{0:T(1024)S(1)}, u32[]{:S(2)}, u32[]{:S(2)}) collective-permute-start(f32[5760]{0:T(1024)S(1)} %concatenate.176), channel_id=1, source_target_pairs={{0,1},{1,0},{2,3},{3,2},{4,5},{5,4},{6,7},{7,6},{8,9},{9,8},{10,11... | collective-permute-start | bytes 69128 | tf_op jit(solution)/shard_map/ppermute | solution.py:434
  339.0 42.5 %collective-permute-start.63 = (bf16[1,72,2304]{2,1,0:T(8,128)(2,1)}, bf16[1,72,2304]{2,1,0:T(8,128)(2,1)S(1)}, u32[]{:S(2)}, u32[]{:S(2)}) collective-permute-start(bf16[1,72,2304]{2,1,0:T(8,128)(2,1)} %get-tuple-element.311), channel_id=1, source_target_pairs={{0,4},{4,8},{8,12},{12,14},{14,10},{10,6},{6,2},{2,0},{1,5},{5,9},... | collective-permute-start | bytes 995336 | tf_op jit(solution)/shard_map/ppermute | solution.py:487
  368.9 26.5 %collective-permute-start.70 = (bf16[1,72,2304]{2,1,0:T(8,128)(2,1)}, bf16[1,72,2304]{2,1,0:T(8,128)(2,1)S(1)}, u32[]{:S(2)}, u32[]{:S(2)}) collective-permute-start(bf16[1,72,2304]{2,1,0:T(8,128)(2,1)} %get-tuple-element.310), channel_id=1, source_target_pairs={{4,0},{8,4},{12,8},{14,12},{10,14},{6,10},{2,6},{0,2},{5,1},{9,5},... | collective-permute-start | bytes 995336 | tf_op jit(solution)/shard_map/ppermute | solution.py:487
  370.7 188.0 %collective-permute-start.29 = (bf16[2304,1152]{1,0:T(8,128)(2,1)}, bf16[2304,1152]{1,0:T(8,128)(2,1)}, u32[]{:S(2)}, u32[]{:S(2)}) collective-permute-start(bf16[2304,1152]{1,0:T(8,128)(2,1)} %pad_maximum_fusion), channel_id=1, source_target_pairs={{0,1},{1,0},{2,3},{3,2},{4,5},{5,4},{6,7},{7,6},{8,9},{9,8},{10,11... | collective-permute-start | bytes 15925256 | tf_op jit(solution)/shard_map/ppermute | solution.py:434
  382.5 16.7 %collective-permute-start.64 = (bf16[1,72,2304]{2,1,0:T(8,128)(2,1)S(1)}, bf16[1,72,2304]{2,1,0:T(8,128)(2,1)S(1)}, u32[]{:S(2)}, u32[]{:S(2)}) collective-permute-start(bf16[1,72,2304]{2,1,0:T(8,128)(2,1)S(1)} %fusion.63), channel_id=1, source_target_pairs={{0,4},{4,8},{8,12},{12,14},{14,10},{10,6},{6,2},{2,0},{1,5},{5,9},... | collective-permute-start | bytes 995336 | tf_op jit(solution)/shard_map/ppermute | solution.py:487
  464.7 20.0 %collective-permute-start.105 = (bf16[1,144,1152]{2,1,0:T(8,128)(2,1)S(1)}, bf16[1,144,1152]{2,1,0:T(8,128)(2,1)S(1)}, u32[]{:S(2)}, u32[]{:S(2)}) collective-permute-start(bf16[1,144,1152]{2,1,0:T(8,128)(2,1)S(1)} %get-tuple-element.277), channel_id=1, source_target_pairs={{0,4},{4,8},{8,12},{12,14},{14,10},{10,6},{6,2},{2,0},{1,5},{5,9},... | collective-permute-start | bytes 995336 | tf_op jit(solution)/shard_map/ppermute | solution.py:495
  474.5 15.7 %collective-permute-start.106 = (bf16[1,144,1152]{2,1,0:T(8,128)(2,1)S(1)}, bf16[1,144,1152]{2,1,0:T(8,128)(2,1)S(1)}, u32[]{:S(2)}, u32[]{:S(2)}) collective-permute-start(bf16[1,144,1152]{2,1,0:T(8,128)(2,1)S(1)} %get-tuple-element.275), channel_id=1, source_target_pairs={{4,0},{8,4},{12,8},{14,12},{10,14},{6,10},{2,6},{0,2},{5,1},{9,5},... | collective-permute-start | bytes 995336 | tf_op jit(solution)/shard_map/ppermute | solution.py:495
  486.2 16.3 %collective-permute-start.79 = (bf16[1,72,2304]{2,1,0:T(8,128)(2,1)S(1)}, bf16[1,72,2304]{2,1,0:T(8,128)(2,1)S(1)}, u32[]{:S(2)}, u32[]{:S(2)}) collective-permute-start(bf16[1,72,2304]{2,1,0:T(8,128)(2,1)S(1)} %collective-permute-done.77), channel_id=1, source_target_pairs={{0,4},{4,8},{8,12},{12,14},{14,10},{10,6},{6,2},{2,0},{1,5},{5,9},... | collective-permute-start | bytes 995336 | tf_op jit(solution)/shard_map/ppermute | solution.py:495
  490.2 14.2 %collective-permute-start.108 = (bf16[1,144,1152]{2,1,0:T(8,128)(2,1)S(1)}, bf16[1,144,1152]{2,1,0:T(8,128)(2,1)S(1)}, u32[]{:S(2)}, u32[]{:S(2)}) collective-permute-start(bf16[1,144,1152]{2,1,0:T(8,128)(2,1)S(1)} %collective-permute-done.106), channel_id=1, source_target_pairs={{4,0},{8,4},{12,8},{14,12},{10,14},{6,10},{2,6},{0,2},{5,1},{9,5},... | collective-permute-start | bytes 995336 | tf_op jit(solution)/shard_map/ppermute | solution.py:495
  497.3 14.2 %collective-permute-start.80 = (bf16[1,72,2304]{2,1,0:T(8,128)(2,1)S(1)}, bf16[1,72,2304]{2,1,0:T(8,128)(2,1)S(1)}, u32[]{:S(2)}, u32[]{:S(2)}) collective-permute-start(bf16[1,72,2304]{2,1,0:T(8,128)(2,1)S(1)} %collective-permute-done.78), channel_id=1, source_target_pairs={{4,0},{8,4},{12,8},{14,12},{10,14},{6,10},{2,6},{0,2},{5,1},{9,5},... | collective-permute-start | bytes 995336 | tf_op jit(solution)/shard_map/ppermute | solution.py:495
  547.1 30.8 %collective-permute-start.116 = (bf16[1,144,1152]{2,1,0:T(8,128)(2,1)S(1)}, bf16[1,144,1152]{2,1,0:T(8,128)(2,1)S(1)}, u32[]{:S(2)}, u32[]{:S(2)}) collective-permute-start(bf16[1,144,1152]{2,1,0:T(8,128)(2,1)S(1)} %collective-permute-done.114), channel_id=1, source_target_pairs={{4,0},{8,4},{12,8},{14,12},{10,14},{6,10},{2,6},{0,2},{5,1},{9,5},... | collective-permute-start | bytes 995336 | tf_op jit(solution)/shard_map/ppermute | solution.py:495
  552.3 66.3 %collective-permute-start.117 = (bf16[1,144,1152]{2,1,0:T(8,128)(2,1)S(1)}, bf16[1,144,1152]{2,1,0:T(8,128)(2,1)S(1)}, u32[]{:S(2)}, u32[]{:S(2)}) collective-permute-start(bf16[1,144,1152]{2,1,0:T(8,128)(2,1)S(1)} %collective-permute-done.115), channel_id=1, source_target_pairs={{0,4},{4,8},{8,12},{12,14},{14,10},{10,6},{6,2},{2,0},{1,5},{5,9},... | collective-permute-start | bytes 995336 | tf_op jit(solution)/shard_map/ppermute | solution.py:495
  554.2 21.9 %collective-permute-start.88 = (bf16[1,72,2304]{2,1,0:T(8,128)(2,1)S(1)}, bf16[1,72,2304]{2,1,0:T(8,128)(2,1)S(1)}, u32[]{:S(2)}, u32[]{:S(2)}) collective-permute-start(bf16[1,72,2304]{2,1,0:T(8,128)(2,1)S(1)} %collective-permute-done.86), channel_id=1, source_target_pairs={{4,0},{8,4},{12,8},{14,12},{10,14},{6,10},{2,6},{0,2},{5,1},{9,5},... | collective-permute-start | bytes 995336 | tf_op jit(solution)/shard_map/ppermute | solution.py:495
  574.8 16.2 %collective-permute-start.89 = (bf16[1,72,2304]{2,1,0:T(8,128)(2,1)S(1)}, bf16[1,72,2304]{2,1,0:T(8,128)(2,1)S(1)}, u32[]{:S(2)}, u32[]{:S(2)}) collective-permute-start(bf16[1,72,2304]{2,1,0:T(8,128)(2,1)S(1)} %collective-permute-done.87), channel_id=1, source_target_pairs={{0,4},{4,8},{8,12},{12,14},{14,10},{10,6},{6,2},{2,0},{1,5},{5,9},... | collective-permute-start | bytes 995336 | tf_op jit(solution)/shard_map/ppermute | solution.py:495
  576.1 14.6 %collective-permute-start.38 = (bf16[1,144,1152]{2,1,0:T(8,128)(2,1)S(1)}, bf16[1,144,1152]{2,1,0:T(8,128)(2,1)S(1)}, u32[]{:S(2)}, u32[]{:S(2)}) collective-permute-start(bf16[1,144,1152]{2,1,0:T(8,128)(2,1)S(1)} %get-tuple-element.324), channel_id=1, source_target_pairs={{4,0},{8,4},{12,8},{14,12},{10,14},{6,10},{2,6},{0,2},{5,1},{9,5},... | collective-permute-start | bytes 995336 | tf_op jit(solution)/shard_map/ppermute | solution.py:487
  577.9 52.0 %collective-permute-start.90 = (bf16[1,72,2304]{2,1,0:T(8,128)(2,1)S(1)}, bf16[1,72,2304]{2,1,0:T(8,128)(2,1)S(1)}, u32[]{:S(2)}, u32[]{:S(2)}) collective-permute-start(bf16[1,72,2304]{2,1,0:T(8,128)(2,1)S(1)} %collective-permute-done.88), channel_id=1, source_target_pairs={{4,0},{8,4},{12,8},{14,12},{10,14},{6,10},{2,6},{0,2},{5,1},{9,5},... | collective-permute-start | bytes 995336 | tf_op jit(solution)/shard_map/ppermute | solution.py:495
  588.2 52.6 %collective-permute-start.118 = (bf16[1,144,1152]{2,1,0:T(8,128)(2,1)S(1)}, bf16[1,144,1152]{2,1,0:T(8,128)(2,1)S(1)}, u32[]{:S(2)}, u32[]{:S(2)}) collective-permute-start(bf16[1,144,1152]{2,1,0:T(8,128)(2,1)S(1)} %collective-permute-done.116), channel_id=1, source_target_pairs={{4,0},{8,4},{12,8},{14,12},{10,14},{6,10},{2,6},{0,2},{5,1},{9,5},... | collective-permute-start | bytes 995336 | tf_op jit(solution)/shard_map/ppermute | solution.py:495
  591.0 14.4 %collective-permute-start.39 = (bf16[1,144,1152]{2,1,0:T(8,128)(2,1)S(1)}, bf16[1,144,1152]{2,1,0:T(8,128)(2,1)S(1)}, u32[]{:S(2)}, u32[]{:S(2)}) collective-permute-start(bf16[1,144,1152]{2,1,0:T(8,128)(2,1)S(1)} %get-tuple-element.322), channel_id=1, source_target_pairs={{4,0},{8,4},{12,8},{14,12},{10,14},{6,10},{2,6},{0,2},{5,1},{9,5},... | collective-permute-start | bytes 995336 | tf_op jit(solution)/shard_map/ppermute | solution.py:487
  (139 other events, 1398.0 us)

commit v4 on v2

--- a/solution.py
+++ b/solution.py
@@ -88,7 +88,8 @@
 
 
 def layer_kernel(chunks, index_ref, mod_ref, bqv_ref, bup_ref, bod_ref, x_in,
-                 wqo, wqt, woo, wot, wuo, wut, wdo, wdt, *rest):
+                 *rest):
+    wqs, (woo, wot, wuo, wut, wdo, wdt) = rest[:2], rest[2:8]
     rest = rest[len(rest) - 30:]
     (y_out, ys, xs, h1s, qkvo, qkvt, atts, aos, h2s, preo, pret, acto, actt, mos,
      wq, wo, wu, wd, x, y, h1, qkv, att, attf, ao, h2, pre, act, mo, sems) = rest
@@ -99,7 +100,7 @@
         img = index_ref[0]
         step = wu.shape[2] // chunks
         spots = [(side, slice(place * step, (place + 1) * step)) for side in range(2) for place in range(chunks)]
-        pairs = [(x_in, x), *three_kinds((wqo, wqt), wq), (woo, wo.at[0]), (wot, wo.at[1])]
+        pairs = [(x_in, x), *three_kinds(wqs, wq), (woo, wo.at[0]), (wot, wo.at[1])]
         for side, spot in spots:
             up, down = ((wuo, wdo), (wut, wdt))[side]
             pairs += [(up.at[:, spot], wu.at[side, :, spot]), (down.at[spot, :], wd.at[side, spot, :])]
@@ -116,7 +117,7 @@
         for part in range(6):
             side, kind = part // 3, part % 3
             stream.take()
-            mixed = nn(h1[...], wq[side, kind])
+            mixed = nt(h1[...], wq[side, kind])
             qkv[side, kind] = (mixed + bqv_ref[part : part + 1]).astype(BF)
         pending += [copies.start(qkv.at[0], qkvo.at[img]), copies.start(qkv.at[1], qkvt.at[img])]
 
@@ -160,9 +161,7 @@
             copy.wait()
 
 
-def cost(tokens, weight_count):
-    return pl.CostEstimate(
-        flops=2 * tokens * weight_count, bytes_accessed=2 * weight_count, transcendentals=0)
+SMALL = pl.CostEstimate(flops=1000, bytes_accessed=1000, transcendentals=0)
 
 
 def layer_call(index, x, mods, bqv, bup, bod, weights, saved, images):
@@ -189,7 +188,7 @@
     saved = tuple(saved) if saved is not None else ()
     aliases = {14 + i: 1 + i for i in range(len(saved))}
     scratch = [
-        pltpu.VMEM((2, 3, width, half), BF),
+        pltpu.VMEM((2, 3, half, width), BF),
         pltpu.VMEM((2, half, width), BF),
         pltpu.VMEM((2, width, hidden), BF),
         pltpu.VMEM((2, hidden, width), BF),
@@ -214,7 +213,7 @@
         scratch_shapes=scratch,
         input_output_aliases=aliases,
         compiler_params=pltpu.CompilerParams(vmem_limit_bytes=LIMIT),
-        cost_estimate=cost(tokens, width * (8 * half + 4 * hidden)),
+        cost_estimate=SMALL,
         name="layer",
     )(index, mods, bqv, bup, bod, x, *weights, *saved)
 
@@ -271,7 +270,7 @@
             copy.wait()
 
 
-def mlp_back_call(index, grad, mods, saved, weights, kept, images):
+def mlp_back_call(index, grad, mods, saved, weights, kept, images, deps=()):
     xs, aos, mos, preo, pret = saved
     tokens, width = grad.shape
     hidden = preo.shape[2]
@@ -300,17 +299,18 @@
         out_shape=(
             sd((tokens, width), F32), sd((images, 8, width), F32), sd((images, 2, hidden), F32),
             sd((images, tokens, width), BF), sd((images, tokens, hidden), BF), sd((images, tokens, hidden), BF)),
-        in_specs=[pl.BlockSpec(memory_space=pltpu.SMEM), VM] + [ANY] * (10 + len(kept)),
+        in_specs=[pl.BlockSpec(memory_space=pltpu.SMEM), VM] + [ANY] * (10 + len(kept) + len(deps)),
         out_specs=[ANY] * 6,
         scratch_shapes=scratch,
         input_output_aliases=aliases,
         compiler_params=pltpu.CompilerParams(vmem_limit_bytes=LIMIT),
-        cost_estimate=cost(tokens, 4 * width * hidden),
+        cost_estimate=SMALL,
         name="mlp_back",
-    )(index, mods, grad, xs, aos, mos, preo, pret, *weights, *kept)
-
-
-def attn_back_kernel(index_ref, mod_ref, mg_in, xs, aos, qkvo, qkvt, wqo, wqt, woo, wot, *rest):
+    )(index, mods, grad, xs, aos, mos, preo, pret, *weights, *kept, *deps)
+
+
+def attn_back_kernel(index_ref, mod_ref, mg_in, xs, aos, qkvo, qkvt, *rest):
+    wqs, (woo, wot) = rest[:2], rest[2:4]
     rest = rest[len(rest) - 22:]
     (rg_out, rgs, sums, bqvs, ois, qgo, qgt, wq, wo, mg, rg, x, ao, qkv, oi, qg, da, acc, ng, total, bqv, sems) = rest
 
@@ -320,7 +320,7 @@
         img = index_ref[0]
         stream = Stream(copies, DEPTH, [
             (mg_in, mg), (woo, wo.at[0]), (wot, wo.at[1]), (qkvo.at[img], qkv.at[0]), (qkvt.at[img], qkv.at[1]),
-            *three_kinds((wqo, wqt), wq), (aos.at[img], ao), (xs.at[img], x)])
+            *three_kinds(wqs, wq), (aos.at[img], ao), (xs.at[img], x)])
         half = wo.shape[1]
         size = 2 * half // HEADS
         scale = size ** (-0.5)
@@ -361,7 +361,7 @@
         for part in range(6):
             side, kind = part // 3, part % 3
             stream.take()
-            term = nt(qg[side, kind], wq[side, kind])
+            term = nn(qg[side, kind], wq[side, kind])
             ng[...] = term if part == 0 else ng[...] + term
             bqv[part : part + 1] = jnp.sum(qg[side, kind].astype(F32), axis=0, keepdims=True)
         pending.append(copies.start(bqv, bqvs.at[img]))
@@ -381,7 +381,7 @@
             copy.wait()
 
 
-def attn_back_call(index, grad, mods, saved, weights, kept, images):
+def attn_back_call(index, grad, mods, saved, weights, kept, images, deps=()):
     xs, aos, qkvo, qkvt = saved
     tokens, width = grad.shape
     half = width // 2
@@ -389,7 +389,7 @@
     kept = tuple(kept) if kept is not None else ()
     aliases = {11 + i: 1 + i for i in range(len(kept))}
     scratch = [
-        pltpu.VMEM((2, 3, width, half), BF),
+        pltpu.VMEM((2, 3, half, width), BF),
         pltpu.VMEM((2, half, width), BF),
         pltpu.VMEM((tokens, width), F32),
         pltpu.VMEM((tokens, width), BF),
@@ -411,14 +411,14 @@
             sd((tokens, width), BF), sd((images, tokens, width), BF), sd((images, 8, width), F32),
             sd((images, 8, half), F32), sd((images, tokens, width), BF),
             sd((3, images, tokens, half), BF), sd((3, images, tokens, half), BF)),
-        in_specs=[pl.BlockSpec(memory_space=pltpu.SMEM), VM] + [ANY] * (9 + len(kept)),
+        in_specs=[pl.BlockSpec(memory_space=pltpu.SMEM), VM] + [ANY] * (9 + len(kept) + len(deps)),
         out_specs=[ANY] * 7,
         scratch_shapes=scratch,
         input_output_aliases=aliases,
         compiler_params=pltpu.CompilerParams(vmem_limit_bytes=LIMIT),
-        cost_estimate=cost(tokens, 8 * width * half),
+        cost_estimate=SMALL,
         name="attn_back",
-    )(index, mods, grad, xs, aos, qkvo, qkvt, *weights, *kept)
+    )(index, mods, grad, xs, aos, qkvo, qkvt, *weights, *kept, *deps)
 
 
 def time_embed(timesteps, width_all):
@@ -448,58 +448,186 @@
     return array
 
 
-def add_all(array):
-    for pairs, _ in partners():
-        array = array + lax.ppermute(array, "dp", pairs)
-    return array
-
-
-def ring_order(peers):
+def in_halves(values):
+    high = lax.reduce_precision(values, 8, 7)
+    return [high.astype(BF), (values - high).astype(BF)]
+
+
+def ring_pairs(peers):
     order = list(range(0, peers, 2)) + list(range(1, peers, 2))[::-1]
-    place = [order.index(peer) for peer in range(peers)]
     ahead = [(order[i], order[(i + 1) % peers]) for i in range(peers)]
-    return place, ahead, [(b, a) for a, b in ahead]
-
-
-def ring_sum(terms):
-    peers = lax.axis_size("dp")
-    place, ahead, behind = ring_order(peers)
-    here = jnp.asarray(place, jnp.int32)[lax.axis_index("dp")]
-    count, width = terms.shape
-    part = count // (2 * peers)
-    blocks = terms.reshape(2, peers, part, width)
-    total = jnp.zeros((2, peers, part, width), F32)
-    lanes = ((ahead, 1), (behind, -1))
-
-    def block(side, number):
-        return lax.dynamic_slice(blocks, (side, number % peers, 0, 0), (1, 1, part, width))
-
-    moving = [block(side, here) for side in range(2)]
-    for step in range(1, peers):
-        for side, (pairs, sign) in enumerate(lanes):
-            came = lax.ppermute(moving[side], "dp", pairs)
-            mine = block(side, here - sign * step)
-            moving[side] = (came.astype(F32) + mine.astype(F32)).astype(BF)
-    for step in range(peers):
-        for side, (pairs, sign) in enumerate(lanes):
-            owner = (here - sign * (peers - 1 + step)) % peers
-            total = lax.dynamic_update_slice(total, moving[side].astype(F32), (side, owner, 0, 0))
-            if step < peers - 1:
-                moving[side] = lax.ppermute(moving[side], "dp", pairs)
-    return total.reshape(count, width)
-
-
-def folded(other, own):
-    came = swap(other.astype(BF))
-    return (own + came.astype(F32)).astype(BF)
-
-
-def outer(left, right):
-    return jnp.einsum("btk,btd->kd", left, right, preferred_element_type=F32)
-
-
-def outers(left, right):
-    return jnp.einsum("jbtk,btd->jkd", left, right, preferred_element_type=F32)
+    return ahead, [(b, a) for a, b in ahead]
+
+
+def add_kernel(step, here_ref, blocks, *rest):
+    came, (first, second, mine, sems) = rest[:2], rest[len(rest) - 4:]
+    peers = blocks.shape[1]
+    copies = []
+    for side, sign in enumerate((1, -1)):
+        spot = (here_ref[0] + (-sign * step) % peers) & (peers - 1)
+        copies.append(pltpu.make_async_copy(blocks.at[side, spot], mine.at[side], sems.at[side]))
+        copies[-1].start()
+    for side, out in enumerate((first, second)):
+        copies[side].wait()
+        out[...] = (came[side][...].astype(F32) + mine[side].astype(F32)).astype(BF)
+
+
+def write_kernel(step, peers, split, here_ref, *rest):
+    whole_count = 2 if split else 1
+    came, passed, rows, sems = rest[:2], rest[-4:-2], rest[-2], rest[-1]
+    whole = rest[len(rest) - 4 - whole_count : -4]
+    for side, sign in enumerate((1, -1)):
+        spot = (here_ref[0] + (-sign * step) % peers) & (peers - 1)
+        rows[side] = came[side][...].astype(F32)
+        passed[side][...] = came[side][...]
+
+        def send(target):
+            copy = pltpu.make_async_copy(rows.at[side], target, sems.at[side])
+            copy.start()
+            return copy
+
+        if split and side == 1:
+            quarter = peers // 2
+
+            @pl.when(spot < quarter)
+            def _():
+                send(whole[0].at[peers + spot]).wait()
+
+            @pl.when(spot >= quarter)
+            def _():
+                send(whole[1].at[spot - quarter]).wait()
+        elif split:
+            waiting = send(whole[0].at[spot])
+        else:
+            copy = send(whole[0].at[side * peers + spot])
+            if side == 0:
+                waiting = copy
+            else:
+                copy.wait()
+    waiting.wait()
+
+
+class Ring:
+    def __init__(self, terms, here, split):
+        self.peers, self.here, self.split, self.step = lax.axis_size("dp"), here, split, 0
+        self.count, self.width = terms.shape
+        self.part = self.count // (2 * self.peers)
+        self.blocks = terms.reshape(2, self.peers, self.part, self.width)
+        self.pairs = ring_pairs(self.peers)
+        self.moving = [self.block(side) for side in range(2)]
+        self.totals = ()
+
+    def block(self, side):
+        none = jnp.uint32(0)
+        start = (jnp.uint32(side), self.here[0].astype(jnp.uint32), none, none)
+        return lax.dynamic_slice(self.blocks, start, (1, 1, self.part, self.width))[0, 0]
+
+    def advance(self, deps=()):
+        self.step += 1
+        deps = list(deps)
+        self.moving = [lax.ppermute(array, "dp", pairs) for array, pairs in zip(self.moving, self.pairs)]
+        if self.step < self.peers:
+            self.moving = self.add(deps)
+        if self.step >= self.peers - 1:
+            *self.totals, first, second = self.write(deps if self.step >= self.peers else [])
+            self.moving = [first, second]
+
+    def add(self, deps):
+        part = jax.ShapeDtypeStruct((self.part, self.width), BF)
+        return pl.pallas_call(
+            functools.partial(add_kernel, self.step),
+            out_shape=(part, part),
+            in_specs=[pl.BlockSpec(memory_space=pltpu.SMEM), ANY, VM, VM] + [ANY] * len(deps),
+            out_specs=(VM, VM),
+            scratch_shapes=[pltpu.VMEM((2, self.part, self.width), BF), pltpu.SemaphoreType.DMA((2,))],
+            cost_estimate=SMALL,
+            name="ring_add",
+        )(self.here, self.blocks, *self.moving, *deps)
+
+    def write(self, deps):
+        blocks = (3 * self.peers // 2, self.peers // 2) if self.split else (2 * self.peers,)
+        outs = tuple(jax.ShapeDtypeStruct((count, self.part, self.width), F32) for count in blocks)
+        part = jax.ShapeDtypeStruct((self.part, self.width), BF)
+        return pl.pallas_call(
+            functools.partial(write_kernel, self.step, self.peers, self.split),
+            out_shape=(*outs, part, part),
+            in_specs=[pl.BlockSpec(memory_space=pltpu.SMEM), VM, VM] + [ANY] * (len(self.totals) + len(deps)),
+            out_specs=(ANY,) * len(outs) + (VM, VM),
+            scratch_shapes=[pltpu.VMEM((2, self.part, self.width), F32), pltpu.SemaphoreType.DMA((2,))],
+            input_output_aliases={3 + i: i for i in range(len(self.totals))},
+            cost_estimate=SMALL,
+            name="ring_write",
+        )(self.here, *self.moving, *self.totals, *deps)
+
+
+def flat(block):
+    return block.reshape(-1, block.shape[-1])
+
+
+def product_kernel(has_came, left_ref, right_ref, *rest):
+    total = tn(flat(left_ref[...]), flat(right_ref[...]))
+    if has_came:
+        total = total + rest[0][...].astype(F32)
+    rest[-1][...] = total.astype(BF)
+
+
+def product(left, right, came=(), deps=()):
+    images, tokens, rows = left.shape
+    width = right.shape[2]
+    block = 384 if rows % 384 == 0 else rows
+    out = pl.BlockSpec((block, width), lambda i: (i, 0))
+    return pl.pallas_call(
+        functools.partial(product_kernel, bool(came)),
+        out_shape=jax.ShapeDtypeStruct((rows, width), BF),
+        grid=(rows // block,),
+        in_specs=[
+            pl.BlockSpec((images, tokens, block), lambda i: (0, 0, i)),
+            pl.BlockSpec((images, tokens, width), lambda i: (0, 0, 0)),
+        ] + [out] * len(came) + [ANY] * len(deps),
+        out_specs=out,
+        compiler_params=pltpu.CompilerParams(vmem_limit_bytes=LIMIT),
+        cost_estimate=SMALL,
+        name="product",
+    )(left, right, *came, *deps)
+
+
+def attn_product_kernel(has_came, qg_ref, h_ref, att_ref, oi_ref, *rest):
+    def finish(total):
+        if has_came:
+            total = total + rest[0][...].astype(F32)
+        rest[-1][...] = total.astype(BF)
+
+    step = pl.program_id(0)
+
+    @pl.when(step < 3)
+    def _():
+        finish(tn(flat(qg_ref[...]), flat(h_ref[...])))
+
+    @pl.when(step == 3)
+    def _():
+        finish(tn(flat(att_ref[...]), flat(oi_ref[...])))
+
+
+def attn_product(side, qkv_grads, h1s, atts, out_ins, came=(), deps=()):
+    _, images, tokens, half = qkv_grads.shape
+    width = h1s.shape[2]
+    out = pl.BlockSpec((half, width), lambda i: (i, 0))
+    whole = pl.BlockSpec((images, tokens, width), lambda i: (0, 0, 0))
+    return pl.pallas_call(
+        functools.partial(attn_product_kernel, bool(came)),
+        out_shape=jax.ShapeDtypeStruct((4 * half, width), BF),
+        grid=(4,),
+        in_specs=[
+            pl.BlockSpec((1, images, tokens, half), lambda i: (jnp.minimum(i, 2), 0, 0, 0)),
+            whole,
+            pl.BlockSpec((images, 1, tokens, half), lambda i: (0, side, 0, 0)),
+            whole,
+        ] + [out] * len(came) + [ANY] * len(deps),
+        out_specs=out,
+        compiler_params=pltpu.CompilerParams(vmem_limit_bytes=LIMIT),
+        cost_estimate=SMALL,
+        name="attn_product",
+    )(qkv_grads, h1s, atts, out_ins, *came, *deps)
 
 
 def shards(images_in, timesteps, labels, counts, label_table, ada_weight, ada_bias, qkv_weight,
@@ -518,25 +646,17 @@
     def by_core(first_val, later_val):
         return jnp.where(core == 0, first_val, later_val)
 
-    def mine(array, axis):
-        return lax.dynamic_slice_in_dim(array, core * images, images, axis)
-
-    def others(array, axis):
-        return lax.dynamic_slice_in_dim(array, (1 - core) * images, images, axis)
-
     def in_order(own, came, axis):
         return by_core(jnp.concatenate([own, came], axis), jnp.concatenate([came, own], axis))
 
     def whole_images(rows):
-        came = swap(others(rows, 1))
-        return jnp.moveaxis(jnp.concatenate([mine(rows, 1), came], axis=0), 1, 0)
-
-    def split_images(rows):
-        local = rows.shape[1] // 2
-        came = swap(rows[:, local:])
-        return jnp.moveaxis(in_order(rows[:, :local], came, 0), 0, 1)[None]
-
-    qkv_own = lax.optimization_barrier(jnp.moveaxis(qkv_weight[0], 1, 0))
+        flat = rows.reshape(rows.shape[0], slots * width)
+        early, later = flat[:, : images * width], flat[:, images * width :]
+        own, came = by_core(early, later), swap(by_core(later, early))
+        spans = [slice(i * width, (i + 1) * width) for i in range(images)]
+        return [jnp.concatenate([own[:, span], came[:, span]], axis=0) for span in spans]
+
+    qkv_own = jnp.transpose(qkv_weight[0], (1, 2, 0))
     w_qkv = (qkv_own, swap(qkv_own))
     w_out = (out_weight[0], swap(out_weight[0]))
     w_up = (up_weight[0], swap(up_weight[0]))
@@ -549,7 +669,8 @@
     mod_local = (
         jnp.dot(silu_b, ada_weight[0], preferred_element_type=F32) + ada_bias[0].astype(F32)[None]
     )
-    modulation = in_order(mine(mod_local, 0), swap(others(mod_local, 0)), 1).reshape(images, 6, width)
+    early, later = mod_local[:images], mod_local[images:]
+    modulation = in_order(by_core(early, later), swap(by_core(later, early)), 1).reshape(images, 6, width)
     slot_no = core * images + jnp.arange(images, dtype=jnp.int32)
     valid = (slot_no < counts[0]).astype(F32)
     mods = jnp.concatenate(
@@ -564,13 +685,10 @@
     bup = pair_bias[:, 2 * half :]
     bod = jnp.concatenate([out_bias, down_bias], axis=0).astype(F32)
 
-    rows_in = whole_images(images_in)
-    cotangent = whole_images(out_cotangent)
-
     def turn_index(number, is_active):
         return jnp.stack([jnp.int32(number), is_active.astype(jnp.int32)])
 
-    inputs, saved = [rows_in[i] for i in range(images)], None
+    inputs, cotangent, saved = whole_images(images_in), whole_images(out_cotangent), None
     for turn in range(2 * images):
         number, is_early = turn % images, turn < images
         answer = layer_call(
@@ -580,64 +698,96 @@
         if is_early:
             inputs.append(lax.ppermute(answer[0], "section", [(0, 1)]))
     ys, xs, h1s, qkvo, qkvt, atts, aos, h2s, preo, pret, acto, actt, mos = saved
-    layer_out = split_images(ys)
-
-    inputs, mlp_kept, attn_kept = [cotangent[i] for i in range(images)], None, None
+
+    inputs, mlp_kept, attn_kept = cotangent, None, None
+    peers, device = lax.axis_size("dp"), lax.axis_index("dp")
+    here = jnp.where((device & 1) == 0, device >> 1, peers - 1 - (device >> 1)).astype(jnp.int32).reshape(1)
+    deps = []
     for turn in range(2 * images):
         number, is_early = turn % images, turn < images
         index = turn_index(number, is_first != is_early)
         answer = mlp_back_call(
-            index, inputs[turn], mods, (xs, aos, mos, preo, pret), (*w_up, *w_down), mlp_kept, images
+            index, inputs[turn], mods, (xs, aos, mos, preo, pret), (*w_up, *w_down), mlp_kept, images, deps
         )
-        middle_grad, mlp_kept = answer[0], answer[1:]
+        middle_grad, mlp_kept, deps = answer[0], answer[1:], []
+        if turn == 2 * images - 1:
+            mlp_sums, up_sums, down_ins, pre_grads_o, pre_grads_t = mlp_kept
+            down_t = product(actt, down_ins)
+            up_t = product(h2s, pre_grads_t, deps=[down_t])
+            down_w = product(acto, down_ins, [swap(down_t)], [up_t])
+            rings = [Ring(down_w, here, False)]
+            up_w = product(h2s, pre_grads_o, [swap(up_t)], rings[0].moving)
+            rings.append(Ring(up_w, here, False))
+            rings[0].advance([up_w])
+            deps = [*rings[0].moving, *rings[1].moving]
         answer = attn_back_call(
-            index, middle_grad, mods, (xs, aos, qkvo, qkvt), (*w_qkv, *w_out), attn_kept, images
+            index, middle_grad, mods, (xs, aos, qkvo, qkvt), (*w_qkv, *w_out), attn_kept, images, deps
         )
-        attn_kept = answer[1:]
+        attn_kept = list(answer[1:])
+        deps = [attn_kept[1]]
         if is_early:
             inputs.append(lax.ppermute(answer[0], "section", [(1, 0)]))
-    mlp_sums, up_sums, down_ins, pre_grads_o, pre_grads_t = mlp_kept
     row_grads, attn_sums, qkv_sums, out_ins, qkv_grads_o, qkv_grads_t = attn_kept
-    in_grad = split_images(row_grads)
-
-    down_w = folded(outer(actt, down_ins), outer(acto, down_ins))
-    up_w = folded(outer(h2s, pre_grads_t), outer(h2s, pre_grads_o))
-    stacked = 3 * half
-    attn_w = folded(
-        jnp.concatenate([outers(qkv_grads_t, h1s).reshape(stacked, width), outer(atts[:, 1], out_ins)]),
-        jnp.concatenate([outers(qkv_grads_o, h1s).reshape(stacked, width), outer(atts[:, 0], out_ins)]),
-    )
-    down_w_sum, up_w_sum, attn_w_sum = ring_sum(down_w), ring_sum(up_w), ring_sum(attn_w)
-    qkv_w_sum = jnp.moveaxis(attn_w_sum[:stacked].reshape(3, half, width), 2, 0)
-    out_w_sum = attn_w_sum[stacked:]
-
+
+    for ring in rings:
+        ring.advance([attn_sums])
+    deps = [*rings[0].moving, *rings[1].moving]
+    attn_t = attn_product(1, qkv_grads_t, h1s, atts, out_ins, deps=deps)
+    for ring in rings:
+        ring.advance([attn_t])
+    deps = [*rings[0].moving, *rings[1].moving]
+    attn_w = attn_product(0, qkv_grads_o, h1s, atts, out_ins, [swap(attn_t)], deps)
+    rings.append(Ring(attn_w, here, True))
+    for ring in rings[:2]:
+        ring.advance(rings[2].moving)
+    attn_sums, mlp_sums, qkv_sums, up_sums, row_grads, ys, _ = lax.optimization_barrier(
+        (attn_sums, mlp_sums, qkv_sums, up_sums, row_grads, ys, rings[1].moving))
     mod_grad = jnp.concatenate([attn_sums[:, :3], mlp_sums[:, :3]], axis=1).astype(BF)
-    columns = mod_grad.reshape(images, 2, 3 * width)
-    own_cols = lax.dynamic_index_in_dim(columns, core, 1, keepdims=False)
-    other_cols = lax.dynamic_index_in_dim(columns, 1 - core, 1, keepdims=False)
-    mod_cols = in_order(own_cols, swap(other_cols), 0)
+    columns = mod_grad.reshape(images, 2 * 3 * width)
+    early, later = columns[:, : 3 * width], columns[:, 3 * width :]
+    mod_cols = in_order(by_core(early, later), swap(by_core(later, early)), 0)
+    qkv_total, up_total = jnp.sum(qkv_sums, axis=0), jnp.sum(up_sums, axis=0)
+    own_bias = jnp.concatenate([qkv_total[0], qkv_total[2], up_total[0]])
+    other_bias = jnp.concatenate([qkv_total[3], qkv_total[5], up_total[1]])
+    both_bias = jnp.concatenate([jnp.sum(attn_sums[:, 3], axis=0), jnp.sum(mlp_sums[:, 3], axis=0)])
+    bias = jnp.concatenate([own_bias, both_bias]) + swap(jnp.concatenate([other_bias, both_bias]))
     silu_grad = jnp.einsum("sk,dk->sd", mod_cols, ada_weight[0], preferred_element_type=F32)
     silu_grad = silu_grad + swap(silu_grad)
     silu_grad = silu_grad + lax.ppermute(silu_grad, "section", [(0, 1), (1, 0)])
     cond_grad = silu_back(silu_grad)[0]
-
-    silu_all = gather_all(silu_b)
-    mod_all = gather_all(mod_cols)
-    kept_rows = jnp.concatenate([cond_grad.reshape(1, -1), labels.astype(F32)[None]], axis=1)
-    gathered = gather_all(kept_rows)
-    cond_all = gathered[:, : slots * width].reshape(-1, width)
-    labels_all = gathered[:, slots * width :].reshape(-1)
+    packed = jnp.concatenate(
+        [silu_b.reshape(-1), mod_cols.reshape(-1), *in_halves(cond_grad.reshape(-1)), *in_halves(bias),
+         *in_halves(labels.astype(F32))])
+    packed = gather_all(packed[None])
+    sizes = [slots * width, slots * 3 * width] + [slots * width] * 2 + [bias.shape[0]] * 2 + [slots] * 2
+    ends = [sum(sizes[: i + 1]) for i in range(len(sizes))]
+    parts = [packed[:, end - size : end] for size, end in zip(sizes, ends)]
+    silu_all, mod_all = parts[0].reshape(-1, width), parts[1].reshape(-1, 3 * width)
+    cond_all = (parts[2].astype(F32) + parts[3].astype(F32)).reshape(-1, width)
+    biases = jnp.sum(parts[4].astype(F32) + parts[5].astype(F32), axis=0)
+    labels_all = (parts[6].astype(F32) + parts[7].astype(F32)).reshape(-1)
     ada_w_sum = jnp.einsum("sd,sk->dk", silu_all, mod_all, preferred_element_type=F32)
     ada_b_sum = jnp.sum(mod_all, axis=0, dtype=F32)
-    onehot = (labels_all[None] == jnp.arange(label_table.shape[0], dtype=F32)[:, None]).astype(F32)
+    classes = jnp.arange(label_table.shape[0], dtype=F32)
+    onehot = (labels_all[None] == classes[:, None]).astype(F32)
     table_grad = jnp.dot(onehot, cond_all, precision=lax.Precision.HIGHEST, preferred_element_type=F32)
 
-    qkv_total, up_total = jnp.sum(qkv_sums, axis=0), jnp.sum(up_sums, axis=0)
-    own_bias = jnp.concatenate([qkv_total[0], qkv_total[2], up_total[0]])
-    other_bias = jnp.concatenate([qkv_total[3], qkv_total[5], up_total[1]])
-    both_bias = jnp.concatenate([jnp.sum(attn_sums[:, 3], axis=0), jnp.sum(mlp_sums[:, 3], axis=0)])
-    came_bias = swap(jnp.concatenate([other_bias, both_bias]))
-    biases = add_all(jnp.concatenate([own_bias, both_bias]) + came_bias)
+    def split_images(rows):
+        own, other = jnp.split(rows, 2, axis=1)
+        return jnp.moveaxis(in_order(own, swap(other), 0), 0, 1)[None]
+
+    in_grad, layer_out = split_images(row_grads), split_images(ys)
+    total_steps = 2 * peers - 2
+    while rings[2].step < total_steps:
+        before = rings[2].moving
+        rings[2].advance(rings[1].moving if rings[1].step < total_steps else ())
+        for ring in rings[:2]:
+            if ring.step < total_steps:
+                ring.advance(before)
+    down_w_sum, up_w_sum = (ring.totals[0].reshape(ring.count, ring.width) for ring in rings[:2])
+    qkv_w_sum = rings[2].totals[0].reshape(3, half, width)
+    out_w_sum = rings[2].totals[1].reshape(half, width)
+    qkv_w_sum = jnp.transpose(qkv_w_sum, (2, 0, 1))
     qkv_b_sum = biases[: 2 * half].reshape(2, half)
     up_b_sum = biases[2 * half : 2 * half + hidden]
     out_b_sum = biases[2 * half + hidden : 2 * half + hidden + width]

time: 752 us -> 659 us (0.88)
  Pallas kernels: 155 us -> 339 us
  waiting for transfers between devices: 269 us -> 99.9 us
  matrix products: 57.3 us -> 22.2 us
  other arithmetic: 47.7 us -> 17.4 us
  between operations: 24 us -> 3.52 us
  local copies, waits for them, and re-layouts: 58.9 us -> 46.4 us
  starting transfers between devices: 130 us -> 122 us
    pallas_call x0 -> x51, Pallas kernels: none -> 185 us  [the longest x24 73.5 us: write(): pl.pallas_call(functools.partial(write_kernel, self.step, self.peers, sel...]
    ppermute x87 -> x84, waiting for transfers between devices: 181 us -> 42.5 us  [advance(): lax.ppermute(array, 'dp', pairs)]
    dot_general x8 -> x0, matrix products: 38.3 us -> none  [the longest x6 28.1 us: outer(): return jnp.einsum('btk,btd->kd', left, right, preferred_element_type=F32)]
    dynamic_update_slice x48 -> x0, other arithmetic: 23.3 us -> none  [ring_sum(): lax.dynamic_update_slice(total, moving[side].astype(F32), (side, owner, 0...]
    ppermute x2, waiting for transfers between devices: 66.4 us -> 48.1 us  [shards(): inputs.append(lax.ppermute(answer[0], 'section', [(1, 0)]))]
    ppermute x9 -> x3, waiting for transfers between devices: 16.8 us -> 0.01 us  [gather_all(): came = lax.ppermute(array, 'dp', pairs)]
    ppermute x9 -> x3, starting transfers between devices: 15.5 us -> 3.59 us  [gather_all(): came = lax.ppermute(array, 'dp', pairs)]
    unnamed x110 -> x227, local copies, waits for them, and re-layouts: 19.6 us -> 30.1 us
  transfers between devices with their start and end apart: 117 -> 108, of which waited for: 53 -> 23; matrix products, arithmetic and copies ran while one was open for 21% -> 9% of each run, Pallas kernels for 16% -> 44%
where the time goes in v4:
time: 659 us; the launch traced here: 650 us
  Pallas kernels  339 us (51%)
  starting transfers between devices  122 us (19%)
  waiting for transfers between devices  99.9 us (15%)
  local copies, waits for them, and re-layouts  46.4 us (7%)
  matrix products  22.2 us (3%)
  other arithmetic  17.4 us (3%)
    ppermute x84, starting transfers between devices, advance(): lax.ppermute(array, 'dp', pairs)  109 us
    pallas_call x24, Pallas kernels, write(): pl.pallas_call(functools.partial(write_kernel, self.step, self.peers, sel...  73.5 us
    pallas_call x4, Pallas kernels, layer_call(): pl.pallas_call(functools.partial(layer_kernel, chunks), out_shape=outs, i...  64.4 us
    pallas_call x21, Pallas kernels, add(): pl.pallas_call(functools.partial(add_kernel, self.step), out_shape=(part,...  63.4 us
    pallas_call x4, Pallas kernels, attn_back_call(): pl.pallas_call(attn_back_kernel, out_shape=(sd((tokens, width), BF), sd((...  49.9 us
    ppermute x2, waiting for transfers between devices, shards(): inputs.append(lax.ppermute(answer[0], 'section', [(1, 0)]))  48.1 us
    ppermute x84, waiting for transfers between devices, advance(): lax.ppermute(array, 'dp', pairs)  42.5 us
    pallas_call x4, Pallas kernels, mlp_back_call(): pl.pallas_call(functools.partial(mlp_back_kernel, chunks), out_shape=(sd(...  39.3 us
  transfers between devices with their start and end apart: 108, of which 23 were waited for; matrix products, arithmetic and copies ran while one was open for 9% of the time, Pallas kernels for 44%

profile of v4, /device:TPU:0, one launch (start us, length us, event | category | flops | bytes accessed | tf_op | source)
XLA Modules:
  0.0 650.3 jit_solution(5279457823912521265)
XLA Ops:
  4.9 4.5 fusion.4
  28.2 24.8 %layer.4 = (bf16[256,1152]{1,0:T(8,128)(2,1)}, bf16[2,256,1152]{2,1,0:T(8,128)(2,1)}, bf16[2,256,1152]{2,1,0:T(8,128)(2,1)}, bf16[2,256,1152]{2,1,0:T(8,128)(2,1...) custom-call(s32[2]{0:T(128)} %get-tuple-element.544.index_ref, ...), custom_call_target="tpu_custom_call" | custom-call | flops 1000 | bytes 1000 | tf_op jit(solution)/shard_map/layer/pallas_call | solution.py:208
  54.4 25.2 %layer.5 = (bf16[256,1152]{1,0:T(8,128)(2,1)}, bf16[2,256,1152]{2,1,0:T(8,128)(2,1)}, bf16[2,256,1152]{2,1,0:T(8,128)(2,1)}, bf16[2,256,1152]{2,1,0:T(8,128)(2,1...) custom-call(s32[2]{0:T(128)} %get-tuple-element.543.index_ref, ...), custom_call_target="tpu_custom_call", output_to_operand_aliasing={{1}: (14, {}), {2}: (15, {}), {3}: (16, {}), {4}: (17, {}),... | custom-call | flops 1000 | bytes 1000 | tf_op jit(solution)/shard_map/layer/pallas_call | solution.py:208
  84.0 5.7 layer.6
  89.7 4.7 collective-permute-done.8.x_in
  95.2 8.8 %layer.7 = (bf16[256,1152]{1,0:T(8,128)(2,1)}, bf16[2,256,1152]{2,1,0:T(8,128)(2,1)}, bf16[2,256,1152]{2,1,0:T(8,128)(2,1)}, bf16[2,256,1152]{2,1,0:T(8,128)(2,1...) custom-call(s32[2]{0:T(128)} %pad_add_fusion.index_ref, ...), custom_call_target="tpu_custom_call", output_to_operand_aliasing={{1}: (14, {}), {2}: (15, {}), {3}: (16, {}), {4}: (17, {}),... | custom-call | flops 1000 | bytes 1000 | tf_op jit(solution)/shard_map/layer/pallas_call | solution.py:208
  105.3 4.7 attn_back.4
  111.3 5.7 mlp_back.5
  117.1 6.3 attn_back.5
  124.7 47.8 %collective-permute-done.11.g_in = bf16[256,1152]{1,0:T(8,128)(2,1)S(1)} collective-permute-done((bf16[256,1152]{1,0:T(8,128)(2,1)}, bf16[256,1152]{1,0:T(8,128)(2,1)S(1)}, u32[]{:S(2)}, u32[]{:S(2)}) %collective-permute-start.11) | collective-permute-done | bytes 589856 | tf_op jit(solution)/shard_map/ppermute | solution.py:729
  173.3 16.3 %mlp_back.6 = (f32[256,1152]{1,0:T(8,128)}, f32[2,8,1152]{2,1,0:T(8,128)}, f32[2,2,2304]{2,1,0:T(2,128)}, bf16[2,256,1152]{2,1,0:T(8,128)(2,1)}, bf16[2,256,2304...) custom-call(s32[2]{0:T(128)} %get-tuple-element.544.index_ref, ...), custom_call_target="tpu_custom_call", output_to_operand_aliasing={{1}: (12, {}), {2}: (13, {}), {3}: (14, {}), {4}: (15, {}),... | custom-call | flops 1000 | bytes 1000 | tf_op jit(solution)/shard_map/mlp_back/pallas_call | solution.py:297
  189.6 19.5 %attn_back.6 = (bf16[256,1152]{1,0:T(8,128)(2,1)}, bf16[2,256,1152]{2,1,0:T(8,128)(2,1)}, f32[2,8,1152]{2,1,0:T(8,128)}, f32[2,8,576]{2,1,0:T(8,128)}, bf16[2,25...) custom-call(s32[2]{0:T(128)} %get-tuple-element.544.index_ref, ...), custom_call_target="tpu_custom_call", output_to_operand_aliasing={{1}: (11, {}), {2}: (12, {}), {3}: (13, {}), {4}: (14, {}),... | custom-call | flops 1000 | bytes 1000 | tf_op jit(solution)/shard_map/attn_back/pallas_call | solution.py:408
  210.2 16.0 %mlp_back.7 = (f32[256,1152]{1,0:T(8,128)}, f32[2,8,1152]{2,1,0:T(8,128)}, f32[2,2,2304]{2,1,0:T(2,128)}, bf16[2,256,1152]{2,1,0:T(8,128)(2,1)}, bf16[2,256,2304...) custom-call(s32[2]{0:T(128)} %get-tuple-element.543.index_ref, ...), custom_call_target="tpu_custom_call", output_to_operand_aliasing={{1}: (12, {}), {2}: (13, {}), {3}: (14, {}), {4}: (15, {}),... | custom-call | flops 1000 | bytes 1000 | tf_op jit(solution)/shard_map/mlp_back/pallas_call | solution.py:297
  226.3 7.9 %product.4.rest_0_ = bf16[2304,1152]{1,0:T(8,128)(2,1)} custom-call(bf16[2,256,2304]{2,1,0:T(8,128)(2,1)} %get-tuple-element.329.left_ref, bf16[2,256,1152]{2,1,0:T(8,128)(2,1)} %get-tuple-element.328.right_ref), custom_call_target="tpu_custom_call" | custom-call | flops 1000 | bytes 1000 | tf_op jit(solution)/shard_map/product/pallas_call | solution.py:579
  234.2 6.6 %product.5.rest_1_ = bf16[1152,2304]{1,0:T(8,128)(2,1)} custom-call(bf16[2,256,1152]{2,1,0:T(8,128)(2,1)} %get-tuple-element.330.left_ref, bf16[2,256,2304]{2,1,0:T(8,128)(2,1)} %get-tuple-element.331.right_ref, bf16[2304,1152]{1,0:T(8,128)(2,1)} %product.4.rest_0_), custom_call_target="tpu_custom_call" | custom-call | flops 1000 | bytes 1000 | tf_op jit(solution)/shard_map/product/pallas_call | solution.py:579
  243.3 9.0 %product.6 = bf16[2304,1152]{1,0:T(8,128)(2,1)} custom-call(bf16[2,256,2304]{2,1,0:T(8,128)(2,1)} %get-tuple-element.327.left_ref, bf16[2,256,1152]{2,1,0:T(8,128)(2,1)} %get-tuple-element.328.right_ref, bf16[2304,1152]{1,0:T(8,128)(2,1)} %collective-permute-done.12.rest_0_, bf16[1152,2304]{1,0:T(8,128)(2,1)} %product.5.rest_1_), custom_call_target="tpu_custom_call" | custom-call | flops 1000 | bytes 1000 | tf_op jit(solution)/shard_map/product/pallas_call | solution.py:579
  253.4 3.2 collective-permute-start.13
  257.1 8.6 %product.7.rest_2_ = bf16[1152,2304]{1,0:T(8,128)(2,1)} custom-call(bf16[2,256,1152]{2,1,0:T(8,128)(2,1)} %get-tuple-element.330.left_ref, bf16[2,256,2304]{2,1,0:T(8,128)(2,1)} %get-tuple-element.332.right_ref, bf16[1152,2304]{1,0:T(8,128)(2,1)} %collective-permute-done.15.rest_0_, bf16[144,1152]{1,0:T(8,128)(2,1)} %copy-done.8, bf16[144,1152]{1,0:T(8,128)(2,1)} %copy-done.7), custom_call_target="tpu_custom_call" | custom-call | flops 1000 | bytes 1000 | tf_op jit(solution)/shard_map/product/pallas_call | solution.py:579
  274.8 19.4 %attn_back.7 = (bf16[256,1152]{1,0:T(8,128)(2,1)}, bf16[2,256,1152]{2,1,0:T(8,128)(2,1)}, f32[2,8,1152]{2,1,0:T(8,128)}, f32[2,8,576]{2,1,0:T(8,128)}, bf16[2,25...) custom-call(s32[2]{0:T(128)} %get-tuple-element.543.index_ref, ...), custom_call_target="tpu_custom_call", output_to_operand_aliasing={{1}: (11, {}), {2}: (12, {}), {3}: (13, {}), {4}: (14, {}),... | custom-call | flops 1000 | bytes 1000 | tf_op jit(solution)/shard_map/attn_back/pallas_call | solution.py:408
  302.6 7.7 %attn_product.2.rest_2_ = bf16[2304,1152]{1,0:T(8,128)(2,1)} custom-call(bf16[3,2,256,576]{3,2,1,0:T(8,128)(2,1)} %get-tuple-element.343.qg_ref, bf16[2,256,1152]{2,1,0:T(8,128)(2,1)} %get-tuple-element.344.h_ref, bf16[2,2,256,576]{3,2,1,0:T(8,128)(2,1)} %get-tuple-element.345.att_ref, bf16[2,256,1152]{2,1,0:T(8,128)(2,1)} %get-tuple-element.346.oi_ref, ...), custom_call_target="tpu_custom_call" | custom-call | flops 1000 | bytes 1000 | tf_op jit(solution)/shard_map/attn_product/pallas_call | solution.py:616
  314.5 6.6 %collective-permute-done.25.rest_0_ = bf16[144,1152]{1,0:T(8,128)(2,1)S(1)} collective-permute-done((bf16[144,1152]{1,0:T(8,128)(2,1)S(1)}, bf16[144,1152]{1,0:T(8,128)(2,1)S(1)}, u32[]{:S(2)}, u32[]{:S(2)}) %collective-permute-start.25) | collective-permute-done | bytes 331808 | tf_op jit(solution)/shard_map/ppermute | solution.py:528
  335.4 8.7 %attn_product.3 = bf16[2304,1152]{1,0:T(8,128)(2,1)} custom-call(bf16[3,2,256,576]{3,2,1,0:T(8,128)(2,1)} %get-tuple-element.351.qg_ref, bf16[2,256,1152]{2,1,0:T(8,128)(2,1)} %get-tuple-element.344.h_ref, bf16[2,2,256,576]{3,2,1,0:T(8,128)(2,1)} %get-tuple-element.345.att_ref, bf16[2,256,1152]{2,1,0:T(8,128)(2,1)} %get-tuple-element.346.oi_ref, ...), custom_call_target="tpu_custom_call" | custom-call | flops 1000 | bytes 1000 | tf_op jit(solution)/shard_map/attn_product/pallas_call | solution.py:616
  400.1 5.4 fusion
  451.8 3.2 collective-permute-done.51.rest_1_
  478.6 7.0 %collective-permute-done.60.rest_0_ = bf16[72,2304]{1,0:T(8,128)(2,1)S(1)} collective-permute-done((bf16[72,2304]{1,0:T(8,128)(2,1)}, bf16[72,2304]{1,0:T(8,128)(2,1)S(1)}, u32[]{:S(2)}, u32[]{:S(2)}) %collective-permute-start.60) | collective-permute-done | bytes 331808 | tf_op jit(solution)/shard_map/ppermute | solution.py:528
  514.1 10.5 %collective-permute-done.63.rest_1_ = bf16[144,1152]{1,0:T(8,128)(2,1)} collective-permute-done((bf16[144,1152]{1,0:T(8,128)(2,1)S(1)}, bf16[144,1152]{1,0:T(8,128)(2,1)}, u32[]{:S(2)}, u32[]{:S(2)}) %collective-permute-start.63) | collective-permute-done | bytes 331808 | tf_op jit(solution)/shard_map/ppermute | solution.py:528
  542.6 5.7 collective-permute-start.102
  563.9 5.6 collective-permute-start.103
  573.6 3.3 collective-permute-start.77
  615.8 8.1 %convolution_bitcast_fusion = f32[1,1152,3456]{2,1,0:T(8,128)} fusion(bf16[32,1152]{1,0:T(8,128)(2,1)S(1)} %reshape.116, bf16[32,3456]{1,0:T(8,128)(2,1)S(1)} %reshape.117), kind=kOutput, calls=%fused_computation.1 | convolution fusion | flops 254803968 | bytes 16220160 | tf_op jit(solution)/shard_map/sd,sk->dk/dot_general | solution.py:769
  633.3 4.1 fusion.9
  646.7 3.2 ring_write.38
  (567 shorter events, 323.0 us)
Async XLA Ops:
  0.7 27.6 %collective-permute-start.6 = (bf16[1152,2304]{1,0:T(8,128)(2,1)}, bf16[1152,2304]{1,0:T(8,128)(2,1)}, u32[]{:S(2)}, u32[]{:S(2)}) collective-permute-start(bf16[1152,2304]{1,0:T(8,128)(2,1)} %bitcast.90), channel_id=1, source_target_pairs={{0,1},{1,0},{2,3},{3,2},{4,5},{5,4},{6,7},{7,6},{8,9},{9,8},{10,11... | collective-permute-start | bytes 15925256 | tf_op jit(solution)/shard_map/ppermute | solution.py:432
  1.2 27.1 %collective-permute-start.7 = (bf16[2304,1152]{1,0:T(8,128)(2,1)}, bf16[2304,1152]{1,0:T(8,128)(2,1)}, u32[]{:S(2)}, u32[]{:S(2)}) collective-permute-start(bf16[2304,1152]{1,0:T(8,128)(2,1)} %bitcast.99), channel_id=1, source_target_pairs={{0,1},{1,0},{2,3},{3,2},{4,5},{5,4},{6,7},{7,6},{8,9},{9,8},{10,11... | collective-permute-start | bytes 15925256 | tf_op jit(solution)/shard_map/ppermute | solution.py:432
  25.6 55.3 %collective-permute-start.1 = (bf16[128,2304]{1,0:T(8,128)(2,1)}, bf16[128,2304]{1,0:T(8,128)(2,1)}, u32[]{:S(2)}, u32[]{:S(2)}) collective-permute-start(bf16[128,2304]{1,0:T(8,128)(2,1)} %get-tuple-element.515), channel_id=1, source_target_pairs={{0,1},{1,0},{2,3},{3,2},{4,5},{5,4},{6,7},{7,6},{8,9},{9,8},{10,11... | collective-permute-start | bytes 1769480 | tf_op jit(solution)/shard_map/ppermute | solution.py:432
  53.1 30.1 %collective-permute-start.9 = (bf16[256,1152]{1,0:T(8,128)(2,1)}, bf16[256,1152]{1,0:T(8,128)(2,1)S(1)}, u32[]{:S(2)}, u32[]{:S(2)}) collective-permute-start(bf16[256,1152]{1,0:T(8,128)(2,1)} %get-tuple-element.254), channel_id=1, source_target_pairs={{0,16},{1,17},{2,18},{3,19},{4,20},{5,21},{6,22},{7,23},{8,24},{9,... | collective-permute-start | bytes 1769480 | tf_op jit(solution)/shard_map/ppermute | solution.py:699
  110.0 62.4 %collective-permute-start.11 = (bf16[256,1152]{1,0:T(8,128)(2,1)}, bf16[256,1152]{1,0:T(8,128)(2,1)S(1)}, u32[]{:S(2)}, u32[]{:S(2)}) collective-permute-start(bf16[256,1152]{1,0:T(8,128)(2,1)} %get-tuple-element.302), channel_id=1, source_target_pairs={{16,0},{17,1},{18,2},{19,3},{20,4},{21,5},{22,6},{23,7},{24,8},{25... | collective-permute-start | bytes 1769480 | tf_op jit(solution)/shard_map/ppermute | solution.py:729
  123.4 86.0 %collective-permute-start.10 = (bf16[256,1152]{1,0:T(8,128)(2,1)}, bf16[256,1152]{1,0:T(8,128)(2,1)S(1)}, u32[]{:S(2)}, u32[]{:S(2)}) collective-permute-start(bf16[256,1152]{1,0:T(8,128)(2,1)} %get-tuple-element.301), channel_id=1, source_target_pairs={{16,0},{17,1},{18,2},{19,3},{20,4},{21,5},{22,6},{23,7},{24,8},{25... | collective-permute-start | bytes 1769480 | tf_op jit(solution)/shard_map/ppermute | solution.py:729
  266.8 27.5 %collective-permute-start.16 = (bf16[72,2304]{1,0:T(8,128)(2,1)S(1)}, bf16[72,2304]{1,0:T(8,128)(2,1)S(1)}, u32[]{:S(2)}, u32[]{:S(2)}) collective-permute-start(bf16[72,2304]{1,0:T(8,128)(2,1)S(1)} %get-tuple-element.505.rest_12_), channel_id=1, source_target_pairs={{0,4},{4,8},{8,12},{12,14},{14,10},{10,6},{6,2},{2,0},{1,5},{5,9},... | collective-permute-start | bytes 995336 | tf_op jit(solution)/shard_map/ppermute | solution.py:528
  268.8 25.4 %collective-permute-start.17 = (bf16[72,2304]{1,0:T(8,128)(2,1)S(1)}, bf16[72,2304]{1,0:T(8,128)(2,1)S(1)}, u32[]{:S(2)}, u32[]{:S(2)}) collective-permute-start(bf16[72,2304]{1,0:T(8,128)(2,1)S(1)} %get-tuple-element.504.rest_13_), channel_id=1, source_target_pairs={{4,0},{8,4},{12,8},{14,12},{10,14},{6,10},{2,6},{0,2},{5,1},{9,5},... | collective-permute-start | bytes 995336 | tf_op jit(solution)/shard_map/ppermute | solution.py:528
  272.7 25.4 %collective-permute-start.20 = (bf16[144,1152]{1,0:T(8,128)(2,1)}, bf16[144,1152]{1,0:T(8,128)(2,1)S(1)}, u32[]{:S(2)}, u32[]{:S(2)}) collective-permute-start(bf16[144,1152]{1,0:T(8,128)(2,1)} %get-tuple-element.333.rest_10_), channel_id=1, source_target_pairs={{0,4},{4,8},{8,12},{12,14},{14,10},{10,6},{6,2},{2,0},{1,5},{5,9},... | collective-permute-start | bytes 995336 | tf_op jit(solution)/shard_map/ppermute | solution.py:528
  274.8 23.3 %collective-permute-start.21 = (bf16[144,1152]{1,0:T(8,128)(2,1)}, bf16[144,1152]{1,0:T(8,128)(2,1)S(1)}, u32[]{:S(2)}, u32[]{:S(2)}) collective-permute-start(bf16[144,1152]{1,0:T(8,128)(2,1)} %get-tuple-element.334.rest_11_), channel_id=1, source_target_pairs={{4,0},{8,4},{12,8},{14,12},{10,14},{6,10},{2,6},{0,2},{5,1},{9,5},... | collective-permute-start | bytes 995336 | tf_op jit(solution)/shard_map/ppermute | solution.py:528
  310.3 25.1 %collective-permute-start.24 = (bf16[2304,1152]{1,0:T(8,128)(2,1)}, bf16[2304,1152]{1,0:T(8,128)(2,1)}, u32[]{:S(2)}, u32[]{:S(2)}) collective-permute-start(bf16[2304,1152]{1,0:T(8,128)(2,1)} %attn_product.2.rest_2_), channel_id=1, source_target_pairs={{0,1},{1,0},{2,3},{3,2},{4,5},{5,4},{6,7},{7,6},{8,9},{9,8},{10,11... | collective-permute-start | bytes 15925256 | tf_op jit(solution)/shard_map/ppermute | solution.py:432
  326.8 20.1 %collective-permute-start.86 = (bf16[144,1152]{1,0:T(8,128)(2,1)}, bf16[144,1152]{1,0:T(8,128)(2,1)S(1)}, u32[]{:S(2)}, u32[]{:S(2)}) collective-permute-start(bf16[144,1152]{1,0:T(8,128)(2,1)} %get-tuple-element.352.rest_1_), channel_id=1, source_target_pairs={{0,4},{4,8},{8,12},{12,14},{14,10},{10,6},{6,2},{2,0},{1,5},{5,9},... | collective-permute-start | bytes 995336 | tf_op jit(solution)/shard_map/ppermute | solution.py:528
  333.3 19.7 %collective-permute-start.22 = (bf16[72,2304]{1,0:T(8,128)(2,1)}, bf16[72,2304]{1,0:T(8,128)(2,1)S(1)}, u32[]{:S(2)}, u32[]{:S(2)}) collective-permute-start(bf16[72,2304]{1,0:T(8,128)(2,1)} %get-tuple-element.349.rest_3_), channel_id=1, source_target_pairs={{0,4},{4,8},{8,12},{12,14},{14,10},{10,6},{6,2},{2,0},{1,5},{5,9},... | collective-permute-start | bytes 995336 | tf_op jit(solution)/shard_map/ppermute | solution.py:528
  345.2 22.5 %collective-permute-start.36 = (bf16[144,1152]{1,0:T(8,128)(2,1)S(1)}, bf16[144,1152]{1,0:T(8,128)(2,1)S(1)}, u32[]{:S(2)}, u32[]{:S(2)}) collective-permute-start(bf16[144,1152]{1,0:T(8,128)(2,1)S(1)} %get-tuple-element.503.rest_2_), channel_id=1, source_target_pairs={{0,4},{4,8},{8,12},{12,14},{14,10},{10,6},{6,2},{2,0},{1,5},{5,9},... | collective-permute-start | bytes 995336 | tf_op jit(solution)/shard_map/ppermute | solution.py:528
  346.9 22.7 %collective-permute-start.37 = (bf16[144,1152]{1,0:T(8,128)(2,1)S(1)}, bf16[144,1152]{1,0:T(8,128)(2,1)S(1)}, u32[]{:S(2)}, u32[]{:S(2)}) collective-permute-start(bf16[144,1152]{1,0:T(8,128)(2,1)S(1)} %get-tuple-element.502.rest_3_), channel_id=1, source_target_pairs={{4,0},{8,4},{12,8},{14,12},{10,14},{6,10},{2,6},{0,2},{5,1},{9,5},... | collective-permute-start | bytes 995336 | tf_op jit(solution)/shard_map/ppermute | solution.py:528
  385.2 20.3 %collective-permute-start.93 = (bf16[144,1152]{1,0:T(8,128)(2,1)}, bf16[144,1152]{1,0:T(8,128)(2,1)S(1)}, u32[]{:S(2)}, u32[]{:S(2)}) collective-permute-start(bf16[144,1152]{1,0:T(8,128)(2,1)} %get-tuple-element.441), channel_id=1, source_target_pairs={{4,0},{8,4},{12,8},{14,12},{10,14},{6,10},{2,6},{0,2},{5,1},{9,5},... | collective-permute-start | bytes 995336 | tf_op jit(solution)/shard_map/ppermute | solution.py:528
  389.7 22.6 %collective-permute-start.42 = (bf16[144,1152]{1,0:T(8,128)(2,1)}, bf16[144,1152]{1,0:T(8,128)(2,1)S(1)}, u32[]{:S(2)}, u32[]{:S(2)}) collective-permute-start(bf16[144,1152]{1,0:T(8,128)(2,1)} %get-tuple-element.366.rest_2_), channel_id=1, source_target_pairs={{0,4},{4,8},{8,12},{12,14},{14,10},{10,6},{6,2},{2,0},{1,5},{5,9},... | collective-permute-start | bytes 995336 | tf_op jit(solution)/shard_map/ppermute | solution.py:528
  391.4 21.1 %collective-permute-start.43 = (bf16[144,1152]{1,0:T(8,128)(2,1)}, bf16[144,1152]{1,0:T(8,128)(2,1)S(1)}, u32[]{:S(2)}, u32[]{:S(2)}) collective-permute-start(bf16[144,1152]{1,0:T(8,128)(2,1)} %get-tuple-element.367.rest_3_), channel_id=1, source_target_pairs={{4,0},{8,4},{12,8},{14,12},{10,14},{6,10},{2,6},{0,2},{5,1},{9,5},... | collective-permute-start | bytes 995336 | tf_op jit(solution)/shard_map/ppermute | solution.py:528
  431.8 28.9 %collective-permute-start.96 = (bf16[144,1152]{1,0:T(8,128)(2,1)}, bf16[144,1152]{1,0:T(8,128)(2,1)S(1)}, u32[]{:S(2)}, u32[]{:S(2)}) collective-permute-start(bf16[144,1152]{1,0:T(8,128)(2,1)} %get-tuple-element.447), channel_id=1, source_target_pairs={{0,4},{4,8},{8,12},{12,14},{14,10},{10,6},{6,2},{2,0},{1,5},{5,9},... | collective-permute-start | bytes 995336 | tf_op jit(solution)/shard_map/ppermute | solution.py:528
  434.1 26.8 %collective-permute-start.97 = (bf16[144,1152]{1,0:T(8,128)(2,1)}, bf16[144,1152]{1,0:T(8,128)(2,1)S(1)}, u32[]{:S(2)}, u32[]{:S(2)}) collective-permute-start(bf16[144,1152]{1,0:T(8,128)(2,1)} %get-tuple-element.448), channel_id=1, source_target_pairs={{4,0},{8,4},{12,8},{14,12},{10,14},{6,10},{2,6},{0,2},{5,1},{9,5},... | collective-permute-start | bytes 995336 | tf_op jit(solution)/shard_map/ppermute | solution.py:528
  441.2 35.3 %collective-permute-start.33 = (bf16[1,39176]{1,0:T(2,128)(2,1)S(1)}, bf16[1,39176]{1,0:T(2,128)(2,1)S(1)}, u32[]{:S(2)}, u32[]{:S(2)}) collective-permute-start(bf16[1,39176]{1,0:T(2,128)(2,1)S(1)} %broadcast_in_dim.59), channel_id=1, source_target_pairs={{0,2},{2,0},{4,6},{6,4},{8,10},{10,8},{12,14},{14,12},{1,3},{3,1},... | collective-permute-start | bytes 235064 | tf_op jit(solution)/shard_map/ppermute | solution.py:446
  467.5 33.9 %collective-permute-start.98 = (bf16[144,1152]{1,0:T(8,128)(2,1)}, bf16[144,1152]{1,0:T(8,128)(2,1)S(1)}, u32[]{:S(2)}, u32[]{:S(2)}) collective-permute-start(bf16[144,1152]{1,0:T(8,128)(2,1)} %get-tuple-element.450), channel_id=1, source_target_pairs={{0,4},{4,8},{8,12},{12,14},{14,10},{10,6},{6,2},{2,0},{1,5},{5,9},... | collective-permute-start | bytes 995336 | tf_op jit(solution)/shard_map/ppermute | solution.py:528
  485.6 20.9 %collective-permute-start.34 = (bf16[2,39176]{1,0:T(2,128)(2,1)S(1)}, bf16[2,39176]{1,0:T(2,128)(2,1)S(1)}, u32[]{:S(2)}, u32[]{:S(2)}) collective-permute-start(bf16[2,39176]{1,0:T(2,128)(2,1)S(1)} %broadcast_select_fusion.4), channel_id=1, source_target_pairs={{0,4},{2,6},{4,0},{6,2},{8,12},{10,14},{12,8},{14,10},{1,5},{3,7},... | collective-permute-start | bytes 470120 | tf_op jit(solution)/shard_map/ppermute | solution.py:446
  502.6 27.1 %collective-permute-start.28 = (bf16[2,128,1152]{2,1,0:T(8,128)(2,1)}, bf16[2,128,1152]{2,1,0:T(8,128)(2,1)S(1)}, u32[]{:S(2)}, u32[]{:S(2)}) collective-permute-start(bf16[2,128,1152]{2,1,0:T(8,128)(2,1)} %get-tuple-element.509), channel_id=1, source_target_pairs={{0,1},{1,0},{2,3},{3,2},{4,5},{5,4},{6,7},{7,6},{8,9},{9,8},{10,11... | collective-permute-start | bytes 1769480 | tf_op jit(solution)/shard_map/ppermute | solution.py:432
  506.5 25.0 %collective-permute-start.27 = (bf16[2,128,1152]{2,1,0:T(8,128)(2,1)}, bf16[2,128,1152]{2,1,0:T(8,128)(2,1)S(1)}, u32[]{:S(2)}, u32[]{:S(2)}) collective-permute-start(bf16[2,128,1152]{2,1,0:T(8,128)(2,1)} %get-tuple-element.511), channel_id=1, source_target_pairs={{0,1},{1,0},{2,3},{3,2},{4,5},{5,4},{6,7},{7,6},{8,9},{9,8},{10,11... | collective-permute-start | bytes 1769480 | tf_op jit(solution)/shard_map/ppermute | solution.py:432
  506.6 25.3 %collective-permute-start.100 = (bf16[144,1152]{1,0:T(8,128)(2,1)}, bf16[144,1152]{1,0:T(8,128)(2,1)}, u32[]{:S(2)}, u32[]{:S(2)}) collective-permute-start(bf16[144,1152]{1,0:T(8,128)(2,1)} %get-tuple-element.453), channel_id=1, source_target_pairs={{0,4},{4,8},{8,12},{12,14},{14,10},{10,6},{6,2},{2,0},{1,5},{5,9},... | collective-permute-start | bytes 995336 | tf_op jit(solution)/shard_map/ppermute | solution.py:528
  507.4 26.2 %collective-permute-start.101 = (bf16[144,1152]{1,0:T(8,128)(2,1)}, bf16[144,1152]{1,0:T(8,128)(2,1)}, u32[]{:S(2)}, u32[]{:S(2)}) collective-permute-start(bf16[144,1152]{1,0:T(8,128)(2,1)} %get-tuple-element.454), channel_id=1, source_target_pairs={{4,0},{8,4},{12,8},{14,12},{10,14},{6,10},{2,6},{0,2},{5,1},{9,5},... | collective-permute-start | bytes 995336 | tf_op jit(solution)/shard_map/ppermute | solution.py:528
  524.6 34.4 %collective-permute-start.35 = (bf16[4,39176]{1,0:T(4,128)(2,1)S(1)}, bf16[4,39176]{1,0:T(4,128)(2,1)S(1)}, u32[]{:S(2)}, u32[]{:S(2)}) collective-permute-start(bf16[4,39176]{1,0:T(4,128)(2,1)S(1)} %maximum_select_fusion.3), channel_id=1, source_target_pairs={{0,8},{2,10},{4,12},{6,14},{8,0},{10,2},{12,4},{14,6},{1,9},{3,11}... | collective-permute-start | bytes 940232 | tf_op jit(solution)/shard_map/ppermute | solution.py:446
  531.8 22.1 %collective-permute-start.66 = (bf16[144,1152]{1,0:T(8,128)(2,1)}, bf16[144,1152]{1,0:T(8,128)(2,1)}, u32[]{:S(2)}, u32[]{:S(2)}) collective-permute-start(bf16[144,1152]{1,0:T(8,128)(2,1)} %get-tuple-element.399.rest_3_), channel_id=1, source_target_pairs={{0,4},{4,8},{8,12},{12,14},{14,10},{10,6},{6,2},{2,0},{1,5},{5,9},... | collective-permute-start | bytes 995336 | tf_op jit(solution)/shard_map/ppermute | solution.py:528
  533.5 21.8 %collective-permute-start.67 = (bf16[144,1152]{1,0:T(8,128)(2,1)}, bf16[144,1152]{1,0:T(8,128)(2,1)}, u32[]{:S(2)}, u32[]{:S(2)}) collective-permute-start(bf16[144,1152]{1,0:T(8,128)(2,1)} %get-tuple-element.400.rest_4_), channel_id=1, source_target_pairs={{4,0},{8,4},{12,8},{14,12},{10,14},{6,10},{2,6},{0,2},{5,1},{9,5},... | collective-permute-start | bytes 995336 | tf_op jit(solution)/shard_map/ppermute | solution.py:528
  542.6 38.0 %collective-permute-start.102 = (bf16[144,1152]{1,0:T(8,128)(2,1)}, bf16[144,1152]{1,0:T(8,128)(2,1)S(1)}, u32[]{:S(2)}, u32[]{:S(2)}) collective-permute-start(bf16[144,1152]{1,0:T(8,128)(2,1)} %get-tuple-element.456), channel_id=1, source_target_pairs={{0,4},{4,8},{8,12},{12,14},{14,10},{10,6},{6,2},{2,0},{1,5},{5,9},... | collective-permute-start | bytes 995336 | tf_op jit(solution)/shard_map/ppermute | solution.py:528
  604.3 27.6 %collective-permute-start.106 = (bf16[144,1152]{1,0:T(8,128)(2,1)}, bf16[144,1152]{1,0:T(8,128)(2,1)S(1)}, u32[]{:S(2)}, u32[]{:S(2)}) collective-permute-start(bf16[144,1152]{1,0:T(8,128)(2,1)} %get-tuple-element.462), channel_id=1, source_target_pairs={{0,4},{4,8},{8,12},{12,14},{14,10},{10,6},{6,2},{2,0},{1,5},{5,9},... | collective-permute-start | bytes 995336 | tf_op jit(solution)/shard_map/ppermute | solution.py:528
  (187 other events, 1368.5 us)

commit v5 on v4

--- a/solution.py
+++ b/solution.py
@@ -11,6 +11,7 @@
 eps_norm = 1e-06
 BF, F32 = jnp.bfloat16, jnp.float32
 ANY = pl.BlockSpec(memory_space=pl.ANY)
+HBM = pl.BlockSpec(memory_space=pltpu.HBM)
 VM = pl.BlockSpec(memory_space=pltpu.VMEM)
 LIMIT = 60 * 1024 * 1024
 DEPTH = 4
@@ -142,18 +143,22 @@
         normed, _ = norm_parts(x[...].astype(F32) + mods[2:3] * ao[...])
         h2[...] = (normed * (1.0 + mods[4:5]) + mods[3:4]).astype(BF)
         pending.append(copies.start(h2, h2s.at[img]))
+        stream.take()
+        values = nn(h2[...], wu[0, :, spots[0][1]])
         for number, (side, spot) in enumerate(spots):
-            stream.take()
-            values = nn(h2[...], wu[side, :, spot]) + bup_ref[side : side + 1, spot]
+            stream.take(2 if number + 1 < len(spots) else 1)
+            if number + 1 < len(spots):
+                later = nn(h2[...], wu[spots[number + 1][0], :, spots[number + 1][1]])
+            values = values + bup_ref[side : side + 1, spot]
             pre[side, :, spot] = values.astype(BF)
             inner = jnp.tanh(values * (ROOT + ROOT * CUBE * values * values))
             act[side, :, spot] = (0.5 * values * (1.0 + inner)).astype(BF)
-            stream.take()
             term = nn(act[side, :, spot], wd[side, spot, :])
             mo[...] = term + (bod_ref[1:2] if number == 0 else mo[...])
             pre_out, act_out = ((preo, acto), (pret, actt))[side]
             pending += [copies.start(pre.at[side, :, spot], pre_out.at[img, :, spot]),
                         copies.start(act.at[side, :, spot], act_out.at[img, :, spot])]
+            values = later
         pending.append(copies.start(mo, mos.at[img]))
         y[...] = (mods[6:7] * (x[...].astype(F32) + mods[2:3] * ao[...] + mods[5:6] * mo[...])).astype(BF)
         pending += [copies.start(y, y_out), copies.start(y, ys.at[img])]
@@ -161,6 +166,7 @@
             copy.wait()
 
 
+TOKEN = jax.ShapeDtypeStruct((8, 128), F32)
 SMALL = pl.CostEstimate(flops=1000, bytes_accessed=1000, transcendentals=0)
 
 
@@ -228,31 +234,35 @@
         img = index_ref[0]
         step = pre.shape[2] // chunks
         spots = [(side, slice(place * step, (place + 1) * step)) for side in range(2) for place in range(chunks)]
-        pairs = [(g_in, g)]
+        pairs, ups = [(g_in, g)], []
         for side, spot in spots:
             pre_in, up, down = ((preo, wuo, wdo), (pret, wut, wdt))[side]
-            pairs += [(down.at[spot, :], wd.at[side, spot, :]), (pre_in.at[img, :, spot], pre.at[side, :, spot]),
-                      (up.at[:, spot], wu.at[side, :, spot])]
+            pairs += [(down.at[spot, :], wd.at[side, spot, :]), *ups]
+            ups = [(pre_in.at[img, :, spot], pre.at[side, :, spot]), (up.at[:, spot], wu.at[side, :, spot])]
+        pairs += ups
         stream = Stream(copies, DEPTH, pairs + [(mos.at[img], mo), (xs.at[img], x), (aos.at[img], ao)])
         mods = mod_ref[img]
         stream.take()
         mg[...] = g[...].astype(F32) * mods[6:7]
         di[...] = (mg[...] * mods[5:6]).astype(BF)
         pending = [copies.start(di, dis.at[img])]
+        stream.take()
+        grad = nt(di[...], wd[0, spots[0][1], :])
         for number, (side, spot) in enumerate(spots):
-            stream.take(2)
+            stream.take(3 if number + 1 < len(spots) else 2)
+            if number + 1 < len(spots):
+                later = nt(di[...], wd[spots[number + 1][0], spots[number + 1][1], :])
             values = pre[side, :, spot].astype(F32)
-            grad = nt(di[...], wd[side, spot, :])
             square = values * values
             inner = jnp.tanh(values * (ROOT + ROOT * CUBE * square))
             slope = 0.5 * (1.0 + inner) + 0.5 * values * (1.0 - inner * inner) * (ROOT + 3.0 * ROOT * CUBE * square)
             graded = (grad * slope).astype(BF)
             pg[side, :, spot] = graded
             bu[side : side + 1, spot] = jnp.sum(graded.astype(F32), axis=0, keepdims=True)
-            stream.take()
             term = nt(pg[side, :, spot], wu[side, :, spot])
             ng[...] = term if number == 0 else ng[...] + term
             pending.append(copies.start(pg.at[side, :, spot], (pgo, pgt)[side].at[img, :, spot]))
+            grad = later
         pending.append(copies.start(bu, bus.at[img]))
         stream.take()
         total[2:3] = jnp.sum(mg[...] * mo[...], axis=0, keepdims=True)
@@ -299,7 +309,7 @@
         out_shape=(
             sd((tokens, width), F32), sd((images, 8, width), F32), sd((images, 2, hidden), F32),
             sd((images, tokens, width), BF), sd((images, tokens, hidden), BF), sd((images, tokens, hidden), BF)),
-        in_specs=[pl.BlockSpec(memory_space=pltpu.SMEM), VM] + [ANY] * (10 + len(kept) + len(deps)),
+        in_specs=[pl.BlockSpec(memory_space=pltpu.SMEM), VM] + [ANY] * (10 + len(kept)) + [HBM] * len(deps),
         out_specs=[ANY] * 6,
         scratch_shapes=scratch,
         input_output_aliases=aliases,
@@ -411,7 +421,7 @@
             sd((tokens, width), BF), sd((images, tokens, width), BF), sd((images, 8, width), F32),
             sd((images, 8, half), F32), sd((images, tokens, width), BF),
             sd((3, images, tokens, half), BF), sd((3, images, tokens, half), BF)),
-        in_specs=[pl.BlockSpec(memory_space=pltpu.SMEM), VM] + [ANY] * (9 + len(kept) + len(deps)),
+        in_specs=[pl.BlockSpec(memory_space=pltpu.SMEM), VM] + [ANY] * (9 + len(kept)) + [HBM] * len(deps),
         out_specs=[ANY] * 7,
         scratch_shapes=scratch,
         input_output_aliases=aliases,
@@ -460,51 +470,59 @@
 
 
 def add_kernel(step, here_ref, blocks, *rest):
-    came, (first, second, mine, sems) = rest[:2], rest[len(rest) - 4:]
+    came, (first, second, _, mine, theirs, sems) = rest[:2], rest[len(rest) - 6:]
     peers = blocks.shape[1]
     copies = []
     for side, sign in enumerate((1, -1)):
         spot = (here_ref[0] + (-sign * step) % peers) & (peers - 1)
         copies.append(pltpu.make_async_copy(blocks.at[side, spot], mine.at[side], sems.at[side]))
-        copies[-1].start()
+        copies.append(pltpu.make_async_copy(came[side], theirs.at[side], sems.at[2 + side]))
+    for copy in copies:
+        copy.start()
     for side, out in enumerate((first, second)):
-        copies[side].wait()
-        out[...] = (came[side][...].astype(F32) + mine[side].astype(F32)).astype(BF)
-
-
-def write_kernel(step, peers, split, here_ref, *rest):
-    whole_count = 2 if split else 1
-    came, passed, rows, sems = rest[:2], rest[-4:-2], rest[-2], rest[-1]
-    whole = rest[len(rest) - 4 - whole_count : -4]
-    for side, sign in enumerate((1, -1)):
-        spot = (here_ref[0] + (-sign * step) % peers) & (peers - 1)
-        rows[side] = came[side][...].astype(F32)
-        passed[side][...] = came[side][...]
-
-        def send(target):
-            copy = pltpu.make_async_copy(rows.at[side], target, sems.at[side])
-            copy.start()
-            return copy
-
-        if split and side == 1:
-            quarter = peers // 2
-
-            @pl.when(spot < quarter)
-            def _():
-                send(whole[0].at[peers + spot]).wait()
-
-            @pl.when(spot >= quarter)
-            def _():
-                send(whole[1].at[spot - quarter]).wait()
-        elif split:
-            waiting = send(whole[0].at[spot])
-        else:
-            copy = send(whole[0].at[side * peers + spot])
-            if side == 0:
-                waiting = copy
+        copies[2 * side].wait()
+        copies[2 * side + 1].wait()
+        out[...] = (theirs[side].astype(F32) + mine[side].astype(F32)).astype(BF)
+
+
+def write_kernel(steps, peers, split, passes, here_ref, *rest):
+    count, passed_count, whole_count = 2 * len(steps), 2 if passes else 0, 2 if split else 1
+    came, (blocks, rows, sems) = rest[:count], rest[-3:]
+    outs = rest[len(rest) - 4 - passed_count - whole_count : -4]
+    whole, passed = outs[:whole_count], outs[whole_count:]
+    quarter = peers // 2
+    arrivals = [pltpu.make_async_copy(came[i], blocks.at[i], sems.at[0, i]) for i in range(count)]
+    for copy in arrivals:
+        copy.start()
+
+    def targets(number):
+        step, side = steps[number // 2], number % 2
+        spot = (here_ref[0] + (-(1 - 2 * side) * step) % peers) & (peers - 1)
+        if not split:
+            return [(None, whole[0].at[side * peers + spot])]
+        if side == 0:
+            return [(None, whole[0].at[spot])]
+        return [
+            (spot < quarter, whole[0].at[peers + jnp.minimum(spot, quarter - 1)]),
+            (spot >= quarter, whole[1].at[jnp.maximum(spot - quarter, 0)]),
+        ]
+
+    def each(number, act):
+        for test, target in targets(number):
+            copy = pltpu.make_async_copy(rows.at[number], target, sems.at[1, number])
+            if test is None:
+                act(copy)
             else:
-                copy.wait()
-    waiting.wait()
+                pl.when(test)(functools.partial(act, copy))
+
+    for number in range(count):
+        arrivals[number].wait()
+        rows[number] = blocks[number].astype(F32)
+        each(number, lambda copy: copy.start())
+        if passes and number >= count - 2:
+            passed[number - count][...] = blocks[number]
+    for number in range(count):
+        each(number, lambda copy: copy.wait())
 
 
 class Ring:
@@ -515,7 +533,7 @@
         self.blocks = terms.reshape(2, self.peers, self.part, self.width)
         self.pairs = ring_pairs(self.peers)
         self.moving = [self.block(side) for side in range(2)]
-        self.totals = ()
+        self.totals, self.kept, self.token = (), [], terms
 
     def block(self, side):
         none = jnp.uint32(0)
@@ -527,37 +545,48 @@
         deps = list(deps)
         self.moving = [lax.ppermute(array, "dp", pairs) for array, pairs in zip(self.moving, self.pairs)]
         if self.step < self.peers:
-            self.moving = self.add(deps)
+            *self.moving, self.token = self.add(deps)
         if self.step >= self.peers - 1:
-            *self.totals, first, second = self.write(deps if self.step >= self.peers else [])
-            self.moving = [first, second]
+            self.kept.append((self.step, self.moving))
+            last = self.step == 2 * self.peers - 2
+            if last or len(self.kept) == max(5, self.peers // 4):
+                self.write(deps if self.step >= self.peers else [], not last)
 
     def add(self, deps):
         part = jax.ShapeDtypeStruct((self.part, self.width), BF)
+        scratch = pltpu.VMEM((2, self.part, self.width), BF)
         return pl.pallas_call(
             functools.partial(add_kernel, self.step),
-            out_shape=(part, part),
-            in_specs=[pl.BlockSpec(memory_space=pltpu.SMEM), ANY, VM, VM] + [ANY] * len(deps),
-            out_specs=(VM, VM),
-            scratch_shapes=[pltpu.VMEM((2, self.part, self.width), BF), pltpu.SemaphoreType.DMA((2,))],
+            out_shape=(part, part, TOKEN),
+            in_specs=[pl.BlockSpec(memory_space=pltpu.SMEM)] + [HBM] * (3 + len(deps)),
+            out_specs=(VM, VM, HBM),
+            scratch_shapes=[scratch, scratch, pltpu.SemaphoreType.DMA((4,))],
             cost_estimate=SMALL,
             name="ring_add",
         )(self.here, self.blocks, *self.moving, *deps)
 
-    def write(self, deps):
+    def write(self, deps, passes):
+        steps = tuple(step for step, _ in self.kept)
+        came = [array for _, moving in self.kept for array in moving]
         blocks = (3 * self.peers // 2, self.peers // 2) if self.split else (2 * self.peers,)
         outs = tuple(jax.ShapeDtypeStruct((count, self.part, self.width), F32) for count in blocks)
         part = jax.ShapeDtypeStruct((self.part, self.width), BF)
-        return pl.pallas_call(
-            functools.partial(write_kernel, self.step, self.peers, self.split),
-            out_shape=(*outs, part, part),
-            in_specs=[pl.BlockSpec(memory_space=pltpu.SMEM), VM, VM] + [ANY] * (len(self.totals) + len(deps)),
-            out_specs=(ANY,) * len(outs) + (VM, VM),
-            scratch_shapes=[pltpu.VMEM((2, self.part, self.width), F32), pltpu.SemaphoreType.DMA((2,))],
-            input_output_aliases={3 + i: i for i in range(len(self.totals))},
+        scratch = (len(came), self.part, self.width)
+        answer = pl.pallas_call(
+            functools.partial(write_kernel, steps, self.peers, self.split, passes),
+            out_shape=(*outs, *((part, part) if passes else ()), TOKEN),
+            in_specs=[pl.BlockSpec(memory_space=pltpu.SMEM)] + [HBM] * (len(came) + len(self.totals) + len(deps)),
+            out_specs=(HBM,) * len(outs) + ((VM, VM) if passes else ()) + (HBM,),
+            scratch_shapes=[
+                pltpu.VMEM(scratch, BF), pltpu.VMEM(scratch, F32), pltpu.SemaphoreType.DMA((2, len(came)))],
+            input_output_aliases={1 + len(came) + i: i for i in range(len(self.totals))},
+            compiler_params=pltpu.CompilerParams(vmem_limit_bytes=LIMIT // 2),
             cost_estimate=SMALL,
             name="ring_write",
-        )(self.here, *self.moving, *self.totals, *deps)
+        )(self.here, *came, *self.totals, *deps)
+        self.totals, self.kept, self.token = answer[: len(outs)], [], answer[-1]
+        if passes:
+            self.moving = list(answer[len(outs) : -1])
 
 
 def flat(block):
@@ -583,7 +612,7 @@
         in_specs=[
             pl.BlockSpec((images, tokens, block), lambda i: (0, 0, i)),
             pl.BlockSpec((images, tokens, width), lambda i: (0, 0, 0)),
-        ] + [out] * len(came) + [ANY] * len(deps),
+        ] + [out] * len(came) + [HBM] * len(deps),
         out_specs=out,
         compiler_params=pltpu.CompilerParams(vmem_limit_bytes=LIMIT),
         cost_estimate=SMALL,
@@ -622,7 +651,7 @@
             whole,
             pl.BlockSpec((images, 1, tokens, half), lambda i: (0, side, 0, 0)),
             whole,
-        ] + [out] * len(came) + [ANY] * len(deps),
+        ] + [out] * len(came) + [HBM] * len(deps),
         out_specs=out,
         compiler_params=pltpu.CompilerParams(vmem_limit_bytes=LIMIT),
         cost_estimate=SMALL,
@@ -716,10 +745,10 @@
             up_t = product(h2s, pre_grads_t, deps=[down_t])
             down_w = product(acto, down_ins, [swap(down_t)], [up_t])
             rings = [Ring(down_w, here, False)]
-            up_w = product(h2s, pre_grads_o, [swap(up_t)], rings[0].moving)
+            up_w = product(h2s, pre_grads_o, [swap(up_t)], [rings[0].token])
             rings.append(Ring(up_w, here, False))
             rings[0].advance([up_w])
-            deps = [*rings[0].moving, *rings[1].moving]
+            deps = [rings[0].token, rings[1].token]
         answer = attn_back_call(
             index, middle_grad, mods, (xs, aos, qkvo, qkvt), (*w_qkv, *w_out), attn_kept, images, deps
         )
@@ -731,15 +760,15 @@
 
     for ring in rings:
         ring.advance([attn_sums])
-    deps = [*rings[0].moving, *rings[1].moving]
+    deps = [rings[0].token, rings[1].token]
     attn_t = attn_product(1, qkv_grads_t, h1s, atts, out_ins, deps=deps)
     for ring in rings:
         ring.advance([attn_t])
-    deps = [*rings[0].moving, *rings[1].moving]
+    deps = [rings[0].token, rings[1].token]
     attn_w = attn_product(0, qkv_grads_o, h1s, atts, out_ins, [swap(attn_t)], deps)
     rings.append(Ring(attn_w, here, True))
     for ring in rings[:2]:
-        ring.advance(rings[2].moving)
+        ring.advance([attn_w])
     attn_sums, mlp_sums, qkv_sums, up_sums, row_grads, ys, _ = lax.optimization_barrier(
         (attn_sums, mlp_sums, qkv_sums, up_sums, row_grads, ys, rings[1].moving))
     mod_grad = jnp.concatenate([attn_sums[:, :3], mlp_sums[:, :3]], axis=1).astype(BF)
@@ -778,9 +807,12 @@
 
     in_grad, layer_out = split_images(row_grads), split_images(ys)
     total_steps = 2 * peers - 2
+    earlier, leading = [], []
     while rings[2].step < total_steps:
-        before = rings[2].moving
-        rings[2].advance(rings[1].moving if rings[1].step < total_steps else ())
+        before, earlier = earlier, [rings[2].token]
+        ahead = [ring.token for ring in rings[:2]]
+        rings[2].advance(leading)
+        leading = ahead
         for ring in rings[:2]:
             if ring.step < total_steps:
                 ring.advance(before)

time: 659 us -> 645 us (0.979)
  Pallas kernels: 339 us -> 268 us
  waiting for transfers between devices: 99.9 us -> 152 us
    pallas_call x24 -> x6, Pallas kernels: 73.5 us -> 20.5 us  [write(): pl.pallas_call(functools.partial(write_kernel, steps, self.peers, self.sp...]
    ppermute x84, waiting for transfers between devices: 42.5 us -> 86.1 us  [advance(): lax.ppermute(array, 'dp', pairs)]
    pallas_call x21, Pallas kernels: 63.4 us -> 45.6 us  [add(): pl.pallas_call(functools.partial(add_kernel, self.step), out_shape=(part,...]
    ppermute x3, waiting for transfers between devices: 0.01 us -> 8.52 us  [gather_all(): came = lax.ppermute(array, 'dp', pairs)]
    unnamed x227 -> x169, local copies, waits for them, and re-layouts: 30.1 us -> 22.9 us
  transfers between devices with their start and end apart: 108 -> 108, of which waited for: 23 -> 36; matrix products, arithmetic and copies ran while one was open for 9% -> 12% of each run, Pallas kernels for 44% -> 34%
where the time goes in v5:
time: 645 us; the launch traced here: 637 us
  Pallas kernels  268 us (42%)
  waiting for transfers between devices  152 us (24%)
  starting transfers between devices  119 us (18%)
  local copies, waits for them, and re-layouts  47.5 us (7%)
  other arithmetic  23.8 us (4%)
  matrix products  23.1 us (4%)
    ppermute x84, starting transfers between devices, advance(): lax.ppermute(array, 'dp', pairs)  108 us
    ppermute x84, waiting for transfers between devices, advance(): lax.ppermute(array, 'dp', pairs)  86.1 us
    pallas_call x4, Pallas kernels, layer_call(): pl.pallas_call(functools.partial(layer_kernel, chunks), out_shape=outs, i...  65 us
    pallas_call x4, Pallas kernels, attn_back_call(): pl.pallas_call(attn_back_kernel, out_shape=(sd((tokens, width), BF), sd((...  50 us
    ppermute x2, waiting for transfers between devices, shards(): inputs.append(lax.ppermute(answer[0], 'section', [(1, 0)]))  48.3 us
    pallas_call x21, Pallas kernels, add(): pl.pallas_call(functools.partial(add_kernel, self.step), out_shape=(part,...  45.6 us
    pallas_call x4, Pallas kernels, mlp_back_call(): pl.pallas_call(functools.partial(mlp_back_kernel, chunks), out_shape=(sd(...  38.9 us
    pallas_call x4, Pallas kernels, product(): pl.pallas_call(functools.partial(product_kernel, bool(came)), out_shape=j...  32.1 us
  transfers between devices with their start and end apart: 108, of which 36 were waited for; matrix products, arithmetic and copies ran while one was open for 12% of the time, Pallas kernels for 34%

profile of v5, /device:TPU:0, one launch (start us, length us, event | category | flops | bytes accessed | tf_op | source)
XLA Modules:
  0.0 637.2 jit_solution(10937901710365265204)
XLA Ops:
  4.9 4.5 fusion.4
  28.3 24.9 %layer.4 = (bf16[256,1152]{1,0:T(8,128)(2,1)}, bf16[2,256,1152]{2,1,0:T(8,128)(2,1)}, bf16[2,256,1152]{2,1,0:T(8,128)(2,1)}, bf16[2,256,1152]{2,1,0:T(8,128)(2,1...) custom-call(s32[2]{0:T(128)} %get-tuple-element.470.index_ref, ...), custom_call_target="tpu_custom_call" | custom-call | flops 1000 | bytes 1000 | tf_op jit(solution)/shard_map/layer/pallas_call | solution.py:214
  54.5 25.3 %layer.5 = (bf16[256,1152]{1,0:T(8,128)(2,1)}, bf16[2,256,1152]{2,1,0:T(8,128)(2,1)}, bf16[2,256,1152]{2,1,0:T(8,128)(2,1)}, bf16[2,256,1152]{2,1,0:T(8,128)(2,1...) custom-call(s32[2]{0:T(128)} %get-tuple-element.469.index_ref, ...), custom_call_target="tpu_custom_call", output_to_operand_aliasing={{1}: (14, {}), {2}: (15, {}), {3}: (16, {}), {4}: (17, {}),... | custom-call | flops 1000 | bytes 1000 | tf_op jit(solution)/shard_map/layer/pallas_call | solution.py:214
  84.2 5.9 layer.6
  95.4 8.9 %layer.7 = (bf16[256,1152]{1,0:T(8,128)(2,1)}, bf16[2,256,1152]{2,1,0:T(8,128)(2,1)}, bf16[2,256,1152]{2,1,0:T(8,128)(2,1)}, bf16[2,256,1152]{2,1,0:T(8,128)(2,1...) custom-call(s32[2]{0:T(128)} %pad_add_fusion.index_ref, ...), custom_call_target="tpu_custom_call", output_to_operand_aliasing={{1}: (14, {}), {2}: (15, {}), {3}: (16, {}), {4}: (17, {}),... | custom-call | flops 1000 | bytes 1000 | tf_op jit(solution)/shard_map/layer/pallas_call | solution.py:214
  105.7 4.7 attn_back.4
  111.7 5.4 mlp_back.5
  117.2 6.3 attn_back.5
  124.8 47.9 %collective-permute-done.11.g_in = bf16[256,1152]{1,0:T(8,128)(2,1)S(1)} collective-permute-done((bf16[256,1152]{1,0:T(8,128)(2,1)}, bf16[256,1152]{1,0:T(8,128)(2,1)S(1)}, u32[]{:S(2)}, u32[]{:S(2)}) %collective-permute-start.11) | collective-permute-done | bytes 589856 | tf_op jit(solution)/shard_map/ppermute | solution.py:758
  173.5 16.2 %mlp_back.6 = (f32[256,1152]{1,0:T(8,128)}, f32[2,8,1152]{2,1,0:T(8,128)}, f32[2,2,2304]{2,1,0:T(2,128)}, bf16[2,256,1152]{2,1,0:T(8,128)(2,1)}, bf16[2,256,2304...) custom-call(s32[2]{0:T(128)} %get-tuple-element.470.index_ref, ...), custom_call_target="tpu_custom_call", output_to_operand_aliasing={{1}: (12, {}), {2}: (13, {}), {3}: (14, {}), {4}: (15, {}),... | custom-call | flops 1000 | bytes 1000 | tf_op jit(solution)/shard_map/mlp_back/pallas_call | solution.py:307
  189.7 19.5 %attn_back.6 = (bf16[256,1152]{1,0:T(8,128)(2,1)}, bf16[2,256,1152]{2,1,0:T(8,128)(2,1)}, f32[2,8,1152]{2,1,0:T(8,128)}, f32[2,8,576]{2,1,0:T(8,128)}, bf16[2,25...) custom-call(s32[2]{0:T(128)} %get-tuple-element.470.index_ref, ...), custom_call_target="tpu_custom_call", output_to_operand_aliasing={{1}: (11, {}), {2}: (12, {}), {3}: (13, {}), {4}: (14, {}),... | custom-call | flops 1000 | bytes 1000 | tf_op jit(solution)/shard_map/attn_back/pallas_call | solution.py:418
  210.4 15.9 %mlp_back.7 = (f32[256,1152]{1,0:T(8,128)}, f32[2,8,1152]{2,1,0:T(8,128)}, f32[2,2,2304]{2,1,0:T(2,128)}, bf16[2,256,1152]{2,1,0:T(8,128)(2,1)}, bf16[2,256,2304...) custom-call(s32[2]{0:T(128)} %get-tuple-element.469.index_ref, ...), custom_call_target="tpu_custom_call", output_to_operand_aliasing={{1}: (12, {}), {2}: (13, {}), {3}: (14, {}), {4}: (15, {}),... | custom-call | flops 1000 | bytes 1000 | tf_op jit(solution)/shard_map/mlp_back/pallas_call | solution.py:307
  226.3 7.9 %product.4.rest_0_ = bf16[2304,1152]{1,0:T(8,128)(2,1)} custom-call(bf16[2,256,2304]{2,1,0:T(8,128)(2,1)} %get-tuple-element.292.left_ref, bf16[2,256,1152]{2,1,0:T(8,128)(2,1)} %get-tuple-element.291.right_ref), custom_call_target="tpu_custom_call" | custom-call | flops 1000 | bytes 1000 | tf_op jit(solution)/shard_map/product/pallas_call | solution.py:608
  234.2 6.6 %product.5.rest_1_ = bf16[1152,2304]{1,0:T(8,128)(2,1)} custom-call(bf16[2,256,1152]{2,1,0:T(8,128)(2,1)} %get-tuple-element.293.left_ref, bf16[2,256,2304]{2,1,0:T(8,128)(2,1)} %get-tuple-element.294.right_ref, bf16[2304,1152]{1,0:T(8,128)(2,1)} %product.4.rest_0_), custom_call_target="tpu_custom_call" | custom-call | flops 1000 | bytes 1000 | tf_op jit(solution)/shard_map/product/pallas_call | solution.py:608
  243.3 9.0 %product.6.rest_1_ = bf16[2304,1152]{1,0:T(8,128)(2,1)} custom-call(bf16[2,256,2304]{2,1,0:T(8,128)(2,1)} %get-tuple-element.290.left_ref, bf16[2,256,1152]{2,1,0:T(8,128)(2,1)} %get-tuple-element.291.right_ref, bf16[2304,1152]{1,0:T(8,128)(2,1)} %collective-permute-done.12.rest_0_, bf16[1152,2304]{1,0:T(8,128)(2,1)} %product.5.rest_1_), custom_call_target="tpu_custom_call" | custom-call | flops 1000 | bytes 1000 | tf_op jit(solution)/shard_map/product/pallas_call | solution.py:608
  257.1 8.5 %product.7.rest_2_.rest_11_ = bf16[1152,2304]{1,0:T(8,128)(2,1)} custom-call(bf16[2,256,1152]{2,1,0:T(8,128)(2,1)} %get-tuple-element.293.left_ref, bf16[2,256,2304]{2,1,0:T(8,128)(2,1)} %get-tuple-element.295.right_ref, bf16[1152,2304]{1,0:T(8,128)(2,1)} %collective-permute-done.15.rest_0_, bf16[2304,1152]{1,0:T(8,128)(2,1)} %product.6.rest_1_), custom_call_target="tpu_custom_call" | custom-call | flops 1000 | bytes 1000 | tf_op jit(solution)/shard_map/product/pallas_call | solution.py:608
  273.9 19.4 %attn_back.7 = (bf16[256,1152]{1,0:T(8,128)(2,1)}, bf16[2,256,1152]{2,1,0:T(8,128)(2,1)}, f32[2,8,1152]{2,1,0:T(8,128)}, f32[2,8,576]{2,1,0:T(8,128)}, bf16[2,25...) custom-call(s32[2]{0:T(128)} %get-tuple-element.469.index_ref, ...), custom_call_target="tpu_custom_call", output_to_operand_aliasing={{1}: (11, {}), {2}: (12, {}), {3}: (13, {}), {4}: (14, {}),... | custom-call | flops 1000 | bytes 1000 | tf_op jit(solution)/shard_map/attn_back/pallas_call | solution.py:418
  300.0 7.7 %attn_product.2.rest_2_ = bf16[2304,1152]{1,0:T(8,128)(2,1)} custom-call(bf16[3,2,256,576]{3,2,1,0:T(8,128)(2,1)} %get-tuple-element.305.qg_ref, bf16[2,256,1152]{2,1,0:T(8,128)(2,1)} %get-tuple-element.306.h_ref, bf16[2,2,256,576]{3,2,1,0:T(8,128)(2,1)} %get-tuple-element.307.att_ref, bf16[2,256,1152]{2,1,0:T(8,128)(2,1)} %get-tuple-element.308.oi_ref, ...), custom_call_target="tpu_custom_call" | custom-call | flops 1000 | bytes 1000 | tf_op jit(solution)/shard_map/attn_product/pallas_call | solution.py:645
  311.9 6.6 %collective-permute-done.18.rest_0_ = bf16[72,2304]{1,0:T(8,128)(2,1)S(1)} collective-permute-done((bf16[72,2304]{1,0:T(8,128)(2,1)S(1)}, bf16[72,2304]{1,0:T(8,128)(2,1)S(1)}, u32[]{:S(2)}, u32[]{:S(2)}) %collective-permute-start.18) | collective-permute-done | bytes 331808 | tf_op jit(solution)/shard_map/ppermute | solution.py:546
  332.4 8.6 %attn_product.3.rest_2_ = bf16[2304,1152]{1,0:T(8,128)(2,1)} custom-call(bf16[3,2,256,576]{3,2,1,0:T(8,128)(2,1)} %get-tuple-element.315.qg_ref, bf16[2,256,1152]{2,1,0:T(8,128)(2,1)} %get-tuple-element.306.h_ref, bf16[2,2,256,576]{3,2,1,0:T(8,128)(2,1)} %get-tuple-element.307.att_ref, bf16[2,256,1152]{2,1,0:T(8,128)(2,1)} %get-tuple-element.308.oi_ref, ...), custom_call_target="tpu_custom_call" | custom-call | flops 1000 | bytes 1000 | tf_op jit(solution)/shard_map/attn_product/pallas_call | solution.py:645
  369.1 5.4 fusion
  377.5 5.9 collective-permute-done.38.rest_0_
  418.7 4.9 collective-permute-done.48.rest_0_
  434.8 4.7 collective-permute-done.54.rest_0_
  473.1 5.5 collective-permute-done.64.rest_0_
  481.6 7.2 %collective-permute-done.65.rest_1_ = bf16[144,1152]{1,0:T(8,128)(2,1)} collective-permute-done((bf16[144,1152]{1,0:T(8,128)(2,1)}, bf16[144,1152]{1,0:T(8,128)(2,1)}, u32[]{:S(2)}, u32[]{:S(2)}) %collective-permute-start.65) | collective-permute-done | bytes 331808 | tf_op jit(solution)/shard_map/ppermute | solution.py:546
  496.6 8.2 %collective-permute-done.35 = bf16[4,39176]{1,0:T(4,128)(2,1)} collective-permute-done((bf16[4,39176]{1,0:T(4,128)(2,1)S(1)}, bf16[4,39176]{1,0:T(4,128)(2,1)}, u32[]{:S(2)}, u32[]{:S(2)}) %collective-permute-start.35) | collective-permute-done | bytes 313440 | tf_op jit(solution)/shard_map/ppermute | solution.py:456
  512.5 4.5 collective-permute-done.79.rest_7_
  569.2 5.1 collective-permute-done.72.rest_8_
  575.5 4.7 ring_write.8
  603.1 9.1 %convolution_bitcast_fusion = f32[1,1152,3456]{2,1,0:T(8,128)} fusion(bf16[32,1152]{1,0:T(8,128)(2,1)} %reshape.115, bf16[32,3456]{1,0:T(8,128)(2,1)S(1)} %reshape.116), kind=kOutput, calls=%fused_computation.1 | convolution fusion | flops 254803968 | bytes 16220160 | tf_op jit(solution)/shard_map/sd,sk->dk/dot_general | solution.py:798
  625.5 4.5 collective-permute-done.107.rest_5_
  (491 shorter events, 304.6 us)
Async XLA Ops:
  0.7 27.6 %collective-permute-start.6 = (bf16[1152,2304]{1,0:T(8,128)(2,1)}, bf16[1152,2304]{1,0:T(8,128)(2,1)}, u32[]{:S(2)}, u32[]{:S(2)}) collective-permute-start(bf16[1152,2304]{1,0:T(8,128)(2,1)} %bitcast.87), channel_id=1, source_target_pairs={{0,1},{1,0},{2,3},{3,2},{4,5},{5,4},{6,7},{7,6},{8,9},{9,8},{10,11... | collective-permute-start | bytes 15925256 | tf_op jit(solution)/shard_map/ppermute | solution.py:442
  1.2 27.1 %collective-permute-start.7 = (bf16[2304,1152]{1,0:T(8,128)(2,1)}, bf16[2304,1152]{1,0:T(8,128)(2,1)}, u32[]{:S(2)}, u32[]{:S(2)}) collective-permute-start(bf16[2304,1152]{1,0:T(8,128)(2,1)} %bitcast.96), channel_id=1, source_target_pairs={{0,1},{1,0},{2,3},{3,2},{4,5},{5,4},{6,7},{7,6},{8,9},{9,8},{10,11... | collective-permute-start | bytes 15925256 | tf_op jit(solution)/shard_map/ppermute | solution.py:442
  25.6 55.5 %collective-permute-start.1 = (bf16[128,2304]{1,0:T(8,128)(2,1)}, bf16[128,2304]{1,0:T(8,128)(2,1)}, u32[]{:S(2)}, u32[]{:S(2)}) collective-permute-start(bf16[128,2304]{1,0:T(8,128)(2,1)} %get-tuple-element.441), channel_id=1, source_target_pairs={{0,1},{1,0},{2,3},{3,2},{4,5},{5,4},{6,7},{7,6},{8,9},{9,8},{10,11... | collective-permute-start | bytes 1769480 | tf_op jit(solution)/shard_map/ppermute | solution.py:442
  53.2 30.2 %collective-permute-start.9 = (bf16[256,1152]{1,0:T(8,128)(2,1)}, bf16[256,1152]{1,0:T(8,128)(2,1)S(1)}, u32[]{:S(2)}, u32[]{:S(2)}) collective-permute-start(bf16[256,1152]{1,0:T(8,128)(2,1)} %get-tuple-element.217), channel_id=1, source_target_pairs={{0,16},{1,17},{2,18},{3,19},{4,20},{5,21},{6,22},{7,23},{8,24},{9,... | collective-permute-start | bytes 1769480 | tf_op jit(solution)/shard_map/ppermute | solution.py:728
  110.4 62.3 %collective-permute-start.11 = (bf16[256,1152]{1,0:T(8,128)(2,1)}, bf16[256,1152]{1,0:T(8,128)(2,1)S(1)}, u32[]{:S(2)}, u32[]{:S(2)}) collective-permute-start(bf16[256,1152]{1,0:T(8,128)(2,1)} %get-tuple-element.265), channel_id=1, source_target_pairs={{16,0},{17,1},{18,2},{19,3},{20,4},{21,5},{22,6},{23,7},{24,8},{25... | collective-permute-start | bytes 1769480 | tf_op jit(solution)/shard_map/ppermute | solution.py:758
  123.5 86.1 %collective-permute-start.10 = (bf16[256,1152]{1,0:T(8,128)(2,1)}, bf16[256,1152]{1,0:T(8,128)(2,1)S(1)}, u32[]{:S(2)}, u32[]{:S(2)}) collective-permute-start(bf16[256,1152]{1,0:T(8,128)(2,1)} %get-tuple-element.264), channel_id=1, source_target_pairs={{16,0},{17,1},{18,2},{19,3},{20,4},{21,5},{22,6},{23,7},{24,8},{25... | collective-permute-start | bytes 1769480 | tf_op jit(solution)/shard_map/ppermute | solution.py:758
  266.7 26.6 %collective-permute-start.16 = (bf16[72,2304]{1,0:T(8,128)(2,1)S(1)}, bf16[72,2304]{1,0:T(8,128)(2,1)S(1)}, u32[]{:S(2)}, u32[]{:S(2)}) collective-permute-start(bf16[72,2304]{1,0:T(8,128)(2,1)S(1)} %get-tuple-element.431), channel_id=1, source_target_pairs={{0,4},{4,8},{8,12},{12,14},{14,10},{10,6},{6,2},{2,0},{1,5},{5,9},... | collective-permute-start | bytes 995336 | tf_op jit(solution)/shard_map/ppermute | solution.py:546
  268.8 24.6 %collective-permute-start.17 = (bf16[72,2304]{1,0:T(8,128)(2,1)S(1)}, bf16[72,2304]{1,0:T(8,128)(2,1)S(1)}, u32[]{:S(2)}, u32[]{:S(2)}) collective-permute-start(bf16[72,2304]{1,0:T(8,128)(2,1)S(1)} %get-tuple-element.430), channel_id=1, source_target_pairs={{4,0},{8,4},{12,8},{14,12},{10,14},{6,10},{2,6},{0,2},{5,1},{9,5},... | collective-permute-start | bytes 995336 | tf_op jit(solution)/shard_map/ppermute | solution.py:546
  271.8 24.6 %collective-permute-start.20 = (bf16[144,1152]{1,0:T(8,128)(2,1)}, bf16[144,1152]{1,0:T(8,128)(2,1)S(1)}, u32[]{:S(2)}, u32[]{:S(2)}) collective-permute-start(bf16[144,1152]{1,0:T(8,128)(2,1)} %get-tuple-element.309), channel_id=1, source_target_pairs={{0,4},{4,8},{8,12},{12,14},{14,10},{10,6},{6,2},{2,0},{1,5},{5,9},... | collective-permute-start | bytes 995336 | tf_op jit(solution)/shard_map/ppermute | solution.py:546
  273.9 22.5 %collective-permute-start.21 = (bf16[144,1152]{1,0:T(8,128)(2,1)}, bf16[144,1152]{1,0:T(8,128)(2,1)S(1)}, u32[]{:S(2)}, u32[]{:S(2)}) collective-permute-start(bf16[144,1152]{1,0:T(8,128)(2,1)} %get-tuple-element.310), channel_id=1, source_target_pairs={{4,0},{8,4},{12,8},{14,12},{10,14},{6,10},{2,6},{0,2},{5,1},{9,5},... | collective-permute-start | bytes 995336 | tf_op jit(solution)/shard_map/ppermute | solution.py:546
  307.7 24.7 %collective-permute-start.24 = (bf16[2304,1152]{1,0:T(8,128)(2,1)}, bf16[2304,1152]{1,0:T(8,128)(2,1)}, u32[]{:S(2)}, u32[]{:S(2)}) collective-permute-start(bf16[2304,1152]{1,0:T(8,128)(2,1)} %attn_product.2.rest_2_), channel_id=1, source_target_pairs={{0,1},{1,0},{2,3},{3,2},{4,5},{5,4},{6,7},{7,6},{8,9},{9,8},{10,11... | collective-permute-start | bytes 15925256 | tf_op jit(solution)/shard_map/ppermute | solution.py:442
  330.3 21.5 %collective-permute-start.40 = (bf16[144,1152]{1,0:T(8,128)(2,1)}, bf16[144,1152]{1,0:T(8,128)(2,1)S(1)}, u32[]{:S(2)}, u32[]{:S(2)}) collective-permute-start(bf16[144,1152]{1,0:T(8,128)(2,1)} %get-tuple-element.330), channel_id=1, source_target_pairs={{0,4},{4,8},{8,12},{12,14},{14,10},{10,6},{6,2},{2,0},{1,5},{5,9},... | collective-permute-start | bytes 995336 | tf_op jit(solution)/shard_map/ppermute | solution.py:546
  332.0 21.5 %collective-permute-start.41 = (bf16[144,1152]{1,0:T(8,128)(2,1)}, bf16[144,1152]{1,0:T(8,128)(2,1)S(1)}, u32[]{:S(2)}, u32[]{:S(2)}) collective-permute-start(bf16[144,1152]{1,0:T(8,128)(2,1)} %get-tuple-element.331), channel_id=1, source_target_pairs={{4,0},{8,4},{12,8},{14,12},{10,14},{6,10},{2,6},{0,2},{5,1},{9,5},... | collective-permute-start | bytes 995336 | tf_op jit(solution)/shard_map/ppermute | solution.py:546
  361.7 28.1 %collective-permute-start.52 = (bf16[72,2304]{1,0:T(8,128)(2,1)}, bf16[72,2304]{1,0:T(8,128)(2,1)S(1)}, u32[]{:S(2)}, u32[]{:S(2)}) collective-permute-start(bf16[72,2304]{1,0:T(8,128)(2,1)} %get-tuple-element.345), channel_id=1, source_target_pairs={{0,4},{4,8},{8,12},{12,14},{14,10},{10,6},{6,2},{2,0},{1,5},{5,9},... | collective-permute-start | bytes 995336 | tf_op jit(solution)/shard_map/ppermute | solution.py:546
  404.4 24.3 %collective-permute-start.56 = (bf16[144,1152]{1,0:T(8,128)(2,1)}, bf16[144,1152]{1,0:T(8,128)(2,1)S(1)}, u32[]{:S(2)}, u32[]{:S(2)}) collective-permute-start(bf16[144,1152]{1,0:T(8,128)(2,1)} %get-tuple-element.350), channel_id=1, source_target_pairs={{0,4},{4,8},{8,12},{12,14},{14,10},{10,6},{6,2},{2,0},{1,5},{5,9},... | collective-permute-start | bytes 995336 | tf_op jit(solution)/shard_map/ppermute | solution.py:546
  414.4 28.0 %collective-permute-start.33 = (bf16[1,39176]{1,0:T(2,128)(2,1)S(1)}, bf16[1,39176]{1,0:T(2,128)(2,1)S(1)}, u32[]{:S(2)}, u32[]{:S(2)}) collective-permute-start(bf16[1,39176]{1,0:T(2,128)(2,1)S(1)} %broadcast_in_dim.59), channel_id=1, source_target_pairs={{0,2},{2,0},{4,6},{6,4},{8,10},{10,8},{12,14},{14,12},{1,3},{3,1},... | collective-permute-start | bytes 235064 | tf_op jit(solution)/shard_map/ppermute | solution.py:456
  423.6 20.3 %collective-permute-start.62 = (bf16[72,2304]{1,0:T(8,128)(2,1)}, bf16[72,2304]{1,0:T(8,128)(2,1)S(1)}, u32[]{:S(2)}, u32[]{:S(2)}) collective-permute-start(bf16[72,2304]{1,0:T(8,128)(2,1)} %get-tuple-element.359), channel_id=1, source_target_pairs={{0,4},{4,8},{8,12},{12,14},{14,10},{10,6},{6,2},{2,0},{1,5},{5,9},... | collective-permute-start | bytes 995336 | tf_op jit(solution)/shard_map/ppermute | solution.py:546
  432.6 29.8 %collective-permute-start.28 = (bf16[2,128,1152]{2,1,0:T(8,128)(2,1)}, bf16[2,128,1152]{2,1,0:T(8,128)(2,1)S(1)}, u32[]{:S(2)}, u32[]{:S(2)}) collective-permute-start(bf16[2,128,1152]{2,1,0:T(8,128)(2,1)} %get-tuple-element.435), channel_id=1, source_target_pairs={{0,1},{1,0},{2,3},{3,2},{4,5},{5,4},{6,7},{7,6},{8,9},{9,8},{10,11... | collective-permute-start | bytes 1769480 | tf_op jit(solution)/shard_map/ppermute | solution.py:442
  439.5 23.3 %collective-permute-start.27 = (bf16[2,128,1152]{2,1,0:T(8,128)(2,1)}, bf16[2,128,1152]{2,1,0:T(8,128)(2,1)}, u32[]{:S(2)}, u32[]{:S(2)}) collective-permute-start(bf16[2,128,1152]{2,1,0:T(8,128)(2,1)} %get-tuple-element.437), channel_id=1, source_target_pairs={{0,1},{1,0},{2,3},{3,2},{4,5},{5,4},{6,7},{7,6},{8,9},{9,8},{10,11... | collective-permute-start | bytes 1769480 | tf_op jit(solution)/shard_map/ppermute | solution.py:442
  463.2 29.4 %collective-permute-start.83 = (bf16[72,2304]{1,0:T(8,128)(2,1)S(1)}, bf16[72,2304]{1,0:T(8,128)(2,1)S(1)}, u32[]{:S(2)}, u32[]{:S(2)}) collective-permute-start(bf16[72,2304]{1,0:T(8,128)(2,1)S(1)} %copy-done.5), channel_id=1, source_target_pairs={{4,0},{8,4},{12,8},{14,12},{10,14},{6,10},{2,6},{0,2},{5,1},{9,5},... | collective-permute-start | bytes 995336 | tf_op jit(solution)/shard_map/ppermute | solution.py:546
  464.5 29.6 %collective-permute-start.76 = (bf16[144,1152]{1,0:T(8,128)(2,1)S(1)}, bf16[144,1152]{1,0:T(8,128)(2,1)}, u32[]{:S(2)}, u32[]{:S(2)}) collective-permute-start(bf16[144,1152]{1,0:T(8,128)(2,1)S(1)} %collective-permute-done.74.rest_2_), channel_id=1, source_target_pairs={{0,4},{4,8},{8,12},{12,14},{14,10},{10,6},{6,2},{2,0},{1,5},{5,9},... | collective-permute-start | bytes 995336 | tf_op jit(solution)/shard_map/ppermute | solution.py:546
  468.8 25.9 %collective-permute-start.77 = (bf16[144,1152]{1,0:T(8,128)(2,1)S(1)}, bf16[144,1152]{1,0:T(8,128)(2,1)}, u32[]{:S(2)}, u32[]{:S(2)}) collective-permute-start(bf16[144,1152]{1,0:T(8,128)(2,1)S(1)} %collective-permute-done.75.rest_3_), channel_id=1, source_target_pairs={{4,0},{8,4},{12,8},{14,12},{10,14},{6,10},{2,6},{0,2},{5,1},{9,5},... | collective-permute-start | bytes 995336 | tf_op jit(solution)/shard_map/ppermute | solution.py:546
  471.4 34.2 %collective-permute-start.84 = (bf16[72,2304]{1,0:T(8,128)(2,1)S(1)}, bf16[72,2304]{1,0:T(8,128)(2,1)S(1)}, u32[]{:S(2)}, u32[]{:S(2)}) collective-permute-start(bf16[72,2304]{1,0:T(8,128)(2,1)S(1)} %collective-permute-done.82.rest_2_), channel_id=1, source_target_pairs={{0,4},{4,8},{8,12},{12,14},{14,10},{10,6},{6,2},{2,0},{1,5},{5,9},... | collective-permute-start | bytes 995336 | tf_op jit(solution)/shard_map/ppermute | solution.py:546
  494.7 22.2 %collective-permute-start.79 = (bf16[144,1152]{1,0:T(8,128)(2,1)}, bf16[144,1152]{1,0:T(8,128)(2,1)}, u32[]{:S(2)}, u32[]{:S(2)}) collective-permute-start(bf16[144,1152]{1,0:T(8,128)(2,1)} %collective-permute-done.77.rest_5_), channel_id=1, source_target_pairs={{4,0},{8,4},{12,8},{14,12},{10,14},{6,10},{2,6},{0,2},{5,1},{9,5},... | collective-permute-start | bytes 995336 | tf_op jit(solution)/shard_map/ppermute | solution.py:546
  509.8 21.5 %collective-permute-start.86 = (bf16[72,2304]{1,0:T(8,128)(2,1)S(1)}, bf16[72,2304]{1,0:T(8,128)(2,1)S(1)}, u32[]{:S(2)}, u32[]{:S(2)}) collective-permute-start(bf16[72,2304]{1,0:T(8,128)(2,1)S(1)} %collective-permute-done.84.rest_4_), channel_id=1, source_target_pairs={{0,4},{4,8},{8,12},{12,14},{14,10},{10,6},{6,2},{2,0},{1,5},{5,9},... | collective-permute-start | bytes 995336 | tf_op jit(solution)/shard_map/ppermute | solution.py:546
  512.4 22.0 %collective-permute-start.87 = (bf16[72,2304]{1,0:T(8,128)(2,1)}, bf16[72,2304]{1,0:T(8,128)(2,1)S(1)}, u32[]{:S(2)}, u32[]{:S(2)}) collective-permute-start(bf16[72,2304]{1,0:T(8,128)(2,1)} %collective-permute-done.85.rest_5_), channel_id=1, source_target_pairs={{4,0},{8,4},{12,8},{14,12},{10,14},{6,10},{2,6},{0,2},{5,1},{9,5},... | collective-permute-start | bytes 995336 | tf_op jit(solution)/shard_map/ppermute | solution.py:546
  537.0 22.0 %collective-permute-start.70 = (bf16[144,1152]{1,0:T(8,128)(2,1)S(1)}, bf16[144,1152]{1,0:T(8,128)(2,1)S(1)}, u32[]{:S(2)}, u32[]{:S(2)}) collective-permute-start(bf16[144,1152]{1,0:T(8,128)(2,1)S(1)} %collective-permute-done.68.rest_4_), channel_id=1, source_target_pairs={{0,4},{4,8},{8,12},{12,14},{14,10},{10,6},{6,2},{2,0},{1,5},{5,9},... | collective-permute-start | bytes 995336 | tf_op jit(solution)/shard_map/ppermute | solution.py:546
  555.6 26.3 %collective-permute-start.102 = (bf16[72,2304]{1,0:T(8,128)(2,1)S(1)}, bf16[72,2304]{1,0:T(8,128)(2,1)S(1)}, u32[]{:S(2)}, u32[]{:S(2)}) collective-permute-start(bf16[72,2304]{1,0:T(8,128)(2,1)S(1)} %get-tuple-element.384), channel_id=1, source_target_pairs={{0,4},{4,8},{8,12},{12,14},{14,10},{10,6},{6,2},{2,0},{1,5},{5,9},... | collective-permute-start | bytes 995336 | tf_op jit(solution)/shard_map/ppermute | solution.py:546
  561.7 32.0 %collective-permute-start.103 = (bf16[72,2304]{1,0:T(8,128)(2,1)S(1)}, bf16[72,2304]{1,0:T(8,128)(2,1)S(1)}, u32[]{:S(2)}, u32[]{:S(2)}) collective-permute-start(bf16[72,2304]{1,0:T(8,128)(2,1)S(1)} %get-tuple-element.385), channel_id=1, source_target_pairs={{4,0},{8,4},{12,8},{14,12},{10,14},{6,10},{2,6},{0,2},{5,1},{9,5},... | collective-permute-start | bytes 995336 | tf_op jit(solution)/shard_map/ppermute | solution.py:546
  565.4 28.4 %collective-permute-start.98 = (bf16[144,1152]{1,0:T(8,128)(2,1)S(1)}, bf16[144,1152]{1,0:T(8,128)(2,1)S(1)}, u32[]{:S(2)}, u32[]{:S(2)}) collective-permute-start(bf16[144,1152]{1,0:T(8,128)(2,1)S(1)} %collective-permute-done.96.rest_0_), channel_id=1, source_target_pairs={{0,4},{4,8},{8,12},{12,14},{14,10},{10,6},{6,2},{2,0},{1,5},{5,9},... | collective-permute-start | bytes 995336 | tf_op jit(solution)/shard_map/ppermute | solution.py:546
  574.3 21.4 %collective-permute-start.99 = (bf16[144,1152]{1,0:T(8,128)(2,1)S(1)}, bf16[144,1152]{1,0:T(8,128)(2,1)S(1)}, u32[]{:S(2)}, u32[]{:S(2)}) collective-permute-start(bf16[144,1152]{1,0:T(8,128)(2,1)S(1)} %collective-permute-done.97.rest_1_), channel_id=1, source_target_pairs={{4,0},{8,4},{12,8},{14,12},{10,14},{6,10},{2,6},{0,2},{5,1},{9,5},... | collective-permute-start | bytes 995336 | tf_op jit(solution)/shard_map/ppermute | solution.py:546
  593.8 20.3 %collective-permute-start.105 = (bf16[72,2304]{1,0:T(8,128)(2,1)S(1)}, bf16[72,2304]{1,0:T(8,128)(2,1)}, u32[]{:S(2)}, u32[]{:S(2)}) collective-permute-start(bf16[72,2304]{1,0:T(8,128)(2,1)S(1)} %collective-permute-done.103.rest_1_), channel_id=1, source_target_pairs={{4,0},{8,4},{12,8},{14,12},{10,14},{6,10},{2,6},{0,2},{5,1},{9,5},... | collective-permute-start | bytes 995336 | tf_op jit(solution)/shard_map/ppermute | solution.py:546
  (158 other events, 1494.2 us)

commit v6 on v5

--- a/solution.py
+++ b/solution.py
@@ -91,9 +91,9 @@
 def layer_kernel(chunks, index_ref, mod_ref, bqv_ref, bup_ref, bod_ref, x_in,
                  *rest):
     wqs, (woo, wot, wuo, wut, wdo, wdt) = rest[:2], rest[2:8]
-    rest = rest[len(rest) - 30:]
+    rest = rest[len(rest) - 32:]
     (y_out, ys, xs, h1s, qkvo, qkvt, atts, aos, h2s, preo, pret, acto, actt, mos,
-     wq, wo, wu, wd, x, y, h1, qkv, att, attf, ao, h2, pre, act, mo, sems) = rest
+     wq, wo, wu, wd, x, y, h1, qkv, att, attf, ao, h2, pre, act, mo, ao_b, mo_b, sems) = rest
 
     @pl.when(index_ref[1] == 1)
     def _():
@@ -139,7 +139,8 @@
         pending.append(copies.start(att, atts.at[img]))
         stream.take(2)
         ao[...] = nn(att[0], wo[0]) + nn(att[1], wo[1]) + bod_ref[0:1]
-        pending.append(copies.start(ao, aos.at[img]))
+        ao_b[...] = ao[...].astype(BF)
+        pending.append(copies.start(ao_b, aos.at[img]))
         normed, _ = norm_parts(x[...].astype(F32) + mods[2:3] * ao[...])
         h2[...] = (normed * (1.0 + mods[4:5]) + mods[3:4]).astype(BF)
         pending.append(copies.start(h2, h2s.at[img]))
@@ -159,7 +160,8 @@
             pending += [copies.start(pre.at[side, :, spot], pre_out.at[img, :, spot]),
                         copies.start(act.at[side, :, spot], act_out.at[img, :, spot])]
             values = later
-        pending.append(copies.start(mo, mos.at[img]))
+        mo_b[...] = mo[...].astype(BF)
+        pending.append(copies.start(mo_b, mos.at[img]))
         y[...] = (mods[6:7] * (x[...].astype(F32) + mods[2:3] * ao[...] + mods[5:6] * mo[...])).astype(BF)
         pending += [copies.start(y, y_out), copies.start(y, ys.at[img])]
         for copy in pending:
@@ -183,13 +185,13 @@
         sd((images, 3, tokens, half), BF),
         sd((images, 3, tokens, half), BF),
         sd((images, 2, tokens, half), BF),
-        sd((images, tokens, width), F32),
+        sd((images, tokens, width), BF),
         sd((images, tokens, width), BF),
         sd((images, tokens, hidden), BF),
         sd((images, tokens, hidden), BF),
         sd((images, tokens, hidden), BF),
         sd((images, tokens, hidden), BF),
-        sd((images, tokens, width), F32),
+        sd((images, tokens, width), BF),
     )
     saved = tuple(saved) if saved is not None else ()
     aliases = {14 + i: 1 + i for i in range(len(saved))}
@@ -209,6 +211,8 @@
         pltpu.VMEM((2, tokens, hidden), BF),
         pltpu.VMEM((2, tokens, hidden), BF),
         pltpu.VMEM((tokens, width), F32),
+        pltpu.VMEM((tokens, width), BF),
+        pltpu.VMEM((tokens, width), BF),
         pltpu.SemaphoreType.DMA((64,)),
     ]
     return pl.pallas_call(
@@ -265,10 +269,10 @@
             grad = later
         pending.append(copies.start(bu, bus.at[img]))
         stream.take()
-        total[2:3] = jnp.sum(mg[...] * mo[...], axis=0, keepdims=True)
+        total[2:3] = jnp.sum(mg[...] * mo[...].astype(F32), axis=0, keepdims=True)
         total[3:4] = jnp.sum(di[...].astype(F32), axis=0, keepdims=True)
         stream.take(2)
-        normed, inverse = norm_parts(x[...].astype(F32) + mods[2:3] * ao[...])
+        normed, inverse = norm_parts(x[...].astype(F32) + mods[2:3] * ao[...].astype(F32))
         total[0:1] = jnp.sum(ng[...], axis=0, keepdims=True)
         total[1:2] = jnp.sum(ng[...] * normed, axis=0, keepdims=True)
         pending.append(copies.start(total, sums.at[img]))
@@ -294,8 +298,8 @@
         pltpu.VMEM((tokens, width), BF),
         pltpu.VMEM((tokens, width), F32),
         pltpu.VMEM((tokens, width), BF),
-        pltpu.VMEM((tokens, width), F32),
-        pltpu.VMEM((tokens, width), F32),
+        pltpu.VMEM((tokens, width), BF),
+        pltpu.VMEM((tokens, width), BF),
         pltpu.VMEM((2, tokens, hidden), BF),
         pltpu.VMEM((tokens, width), BF),
         pltpu.VMEM((2, tokens, hidden), BF),
@@ -376,7 +380,7 @@
             bqv[part : part + 1] = jnp.sum(qg[side, kind].astype(F32), axis=0, keepdims=True)
         pending.append(copies.start(bqv, bqvs.at[img]))
         stream.take()
-        total[2:3] = jnp.sum(mg[...] * ao[...], axis=0, keepdims=True)
+        total[2:3] = jnp.sum(mg[...] * ao[...].astype(F32), axis=0, keepdims=True)
         total[3:4] = jnp.sum(oi[...].astype(F32), axis=0, keepdims=True)
         stream.take()
         normed, inverse = norm_parts(x[...].astype(F32))
@@ -404,7 +408,7 @@
         pltpu.VMEM((tokens, width), F32),
         pltpu.VMEM((tokens, width), BF),
         pltpu.VMEM((tokens, width), BF),
-        pltpu.VMEM((tokens, width), F32),
+        pltpu.VMEM((tokens, width), BF),
         pltpu.VMEM((2, 3, tokens, half), BF),
         pltpu.VMEM((tokens, width), BF),
         pltpu.VMEM((2, 3, tokens, half), BF),
@@ -726,7 +730,12 @@
         saved = answer[1:]
         if is_early:
             inputs.append(lax.ppermute(answer[0], "section", [(0, 1)]))
+    def split_images(rows):
+        own, other = jnp.split(rows, 2, axis=1)
+        return jnp.moveaxis(in_order(own, swap(other), 0), 0, 1)[None]
+
     ys, xs, h1s, qkvo, qkvt, atts, aos, h2s, preo, pret, acto, actt, mos = saved
+    layer_out = split_images(ys)
 
     inputs, mlp_kept, attn_kept = cotangent, None, None
     peers, device = lax.axis_size("dp"), lax.axis_index("dp")
@@ -735,6 +744,7 @@
     for turn in range(2 * images):
         number, is_early = turn % images, turn < images
         index = turn_index(number, is_first != is_early)
+        deps = deps + [layer_out] if turn == images else deps
         answer = mlp_back_call(
             index, inputs[turn], mods, (xs, aos, mos, preo, pret), (*w_up, *w_down), mlp_kept, images, deps
         )
@@ -769,8 +779,8 @@
     rings.append(Ring(attn_w, here, True))
     for ring in rings[:2]:
         ring.advance([attn_w])
-    attn_sums, mlp_sums, qkv_sums, up_sums, row_grads, ys, _ = lax.optimization_barrier(
-        (attn_sums, mlp_sums, qkv_sums, up_sums, row_grads, ys, rings[1].moving))
+    attn_sums, mlp_sums, qkv_sums, up_sums, row_grads, _ = lax.optimization_barrier(
+        (attn_sums, mlp_sums, qkv_sums, up_sums, row_grads, rings[1].moving))
     mod_grad = jnp.concatenate([attn_sums[:, :3], mlp_sums[:, :3]], axis=1).astype(BF)
     columns = mod_grad.reshape(images, 2 * 3 * width)
     early, later = columns[:, : 3 * width], columns[:, 3 * width :]
@@ -801,11 +811,7 @@
     onehot = (labels_all[None] == classes[:, None]).astype(F32)
     table_grad = jnp.dot(onehot, cond_all, precision=lax.Precision.HIGHEST, preferred_element_type=F32)
 
-    def split_images(rows):
-        own, other = jnp.split(rows, 2, axis=1)
-        return jnp.moveaxis(in_order(own, swap(other), 0), 0, 1)[None]
-
-    in_grad, layer_out = split_images(row_grads), split_images(ys)
+    in_grad = split_images(row_grads)
     total_steps = 2 * peers - 2
     earlier, leading = [], []
     while rings[2].step < total_steps:

time: 645 us -> 640 us (level)
  starting transfers between devices: 119 us -> 138 us
  waiting for transfers between devices: 152 us -> 135 us
    ppermute x84, starting transfers between devices: 108 us -> 123 us  [advance(): lax.ppermute(array, 'dp', pairs)]
    ppermute x84, waiting for transfers between devices: 86.1 us -> 73.1 us  [advance(): lax.ppermute(array, 'dp', pairs)]
    unnamed x169 -> x171, local copies, waits for them, and re-layouts: 22.9 us -> 19.9 us
  transfers between devices with their start and end apart: 108 -> 108, of which waited for: 36 -> 34; matrix products, arithmetic and copies ran while one was open for 12% -> 11% of each run, Pallas kernels for 34% -> 35%
where the time goes in v6:
time: 640 us; the launch traced here: 632 us
  Pallas kernels  268 us (42%)
  starting transfers between devices  138 us (22%)
  waiting for transfers between devices  135 us (21%)
  local copies, waits for them, and re-layouts  41.7 us (7%)
  matrix products  23.1 us (4%)
  other arithmetic  22.6 us (4%)
    ppermute x84, starting transfers between devices, advance(): lax.ppermute(array, 'dp', pairs)  123 us
    ppermute x84, waiting for transfers between devices, advance(): lax.ppermute(array, 'dp', pairs)  73.1 us
    pallas_call x4, Pallas kernels, layer_call(): pl.pallas_call(functools.partial(layer_kernel, chunks), out_shape=outs, i...  65.2 us
    ppermute x2, waiting for transfers between devices, shards(): inputs.append(lax.ppermute(answer[0], 'section', [(1, 0)]))  49.8 us
    pallas_call x4, Pallas kernels, attn_back_call(): pl.pallas_call(attn_back_kernel, out_shape=(sd((tokens, width), BF), sd((...  48.5 us
    pallas_call x21, Pallas kernels, add(): pl.pallas_call(functools.partial(add_kernel, self.step), out_shape=(part,...  45.5 us
    pallas_call x4, Pallas kernels, mlp_back_call(): pl.pallas_call(functools.partial(mlp_back_kernel, chunks), out_shape=(sd(...  38.9 us
    pallas_call x4, Pallas kernels, product(): pl.pallas_call(functools.partial(product_kernel, bool(came)), out_shape=j...  32.1 us
  transfers between devices with their start and end apart: 108, of which 34 were waited for; matrix products, arithmetic and copies ran while one was open for 11% of the time, Pallas kernels for 35%

profile of v6, /device:TPU:0, one launch (start us, length us, event | category | flops | bytes accessed | tf_op | source)
XLA Modules:
  0.0 631.8 jit_solution(2714335269696857743)
XLA Ops:
  4.9 4.5 fusion.4
  28.2 24.5 %layer.4 = (bf16[256,1152]{1,0:T(8,128)(2,1)}, bf16[2,256,1152]{2,1,0:T(8,128)(2,1)}, bf16[2,256,1152]{2,1,0:T(8,128)(2,1)}, bf16[2,256,1152]{2,1,0:T(8,128)(2,1...) custom-call(s32[2]{0:T(128)} %get-tuple-element.468.index_ref, ...), custom_call_target="tpu_custom_call" | custom-call | flops 1000 | bytes 1000 | tf_op jit(solution)/shard_map/layer/pallas_call | solution.py:218
  54.1 24.9 %layer.5 = (bf16[256,1152]{1,0:T(8,128)(2,1)}, bf16[2,256,1152]{2,1,0:T(8,128)(2,1)}, bf16[2,256,1152]{2,1,0:T(8,128)(2,1)}, bf16[2,256,1152]{2,1,0:T(8,128)(2,1...) custom-call(s32[2]{0:T(128)} %get-tuple-element.467.index_ref, ...), custom_call_target="tpu_custom_call", output_to_operand_aliasing={{1}: (14, {}), {2}: (15, {}), {3}: (16, {}), {4}: (17, {}),... | custom-call | flops 1000 | bytes 1000 | tf_op jit(solution)/shard_map/layer/pallas_call | solution.py:218
  82.9 6.5 %layer.6 = (bf16[256,1152]{1,0:T(8,128)(2,1)}, bf16[2,256,1152]{2,1,0:T(8,128)(2,1)}, bf16[2,256,1152]{2,1,0:T(8,128)(2,1)}, bf16[2,256,1152]{2,1,0:T(8,128)(2,1...) custom-call(s32[2]{0:T(128)} %pad_add_fusion.4.index_ref, ...), custom_call_target="tpu_custom_call", output_to_operand_aliasing={{1}: (14, {}), {2}: (15, {}), {3}: (16, {}), {4}: (17, {}),... | custom-call | flops 1000 | bytes 1000 | tf_op jit(solution)/shard_map/layer/pallas_call | solution.py:218
  94.6 9.2 %layer.7 = (bf16[256,1152]{1,0:T(8,128)(2,1)}, bf16[2,256,1152]{2,1,0:T(8,128)(2,1)}, bf16[2,256,1152]{2,1,0:T(8,128)(2,1)}, bf16[2,256,1152]{2,1,0:T(8,128)(2,1...) custom-call(s32[2]{0:T(128)} %pad_add_fusion.2.index_ref, ...), custom_call_target="tpu_custom_call", output_to_operand_aliasing={{1}: (14, {}), {2}: (15, {}), {3}: (16, {}), {4}: (17, {}),... | custom-call | flops 1000 | bytes 1000 | tf_op jit(solution)/shard_map/layer/pallas_call | solution.py:218
  111.2 5.5 mlp_back.5
  116.8 7.3 %attn_back.5 = (bf16[256,1152]{1,0:T(8,128)(2,1)}, bf16[2,256,1152]{2,1,0:T(8,128)(2,1)}, f32[2,8,1152]{2,1,0:T(8,128)}, f32[2,8,576]{2,1,0:T(8,128)}, bf16[2,25...) custom-call(s32[2]{0:T(128)} %get-tuple-element.471.index_ref, ...), custom_call_target="tpu_custom_call", output_to_operand_aliasing={{1}: (11, {}), {2}: (12, {}), {3}: (13, {}), {4}: (14, {}),... | custom-call | flops 1000 | bytes 1000 | tf_op jit(solution)/shard_map/attn_back/pallas_call | solution.py:422
  127.5 47.6 %collective-permute-done.12.g_in = bf16[256,1152]{1,0:T(8,128)(2,1)} collective-permute-done((bf16[256,1152]{1,0:T(8,128)(2,1)}, bf16[256,1152]{1,0:T(8,128)(2,1)}, u32[]{:S(2)}, u32[]{:S(2)}) %collective-permute-start.12) | collective-permute-done | bytes 589856 | tf_op jit(solution)/shard_map/ppermute | solution.py:768
  175.1 15.9 %mlp_back.6 = (f32[256,1152]{1,0:T(8,128)}, f32[2,8,1152]{2,1,0:T(8,128)}, f32[2,2,2304]{2,1,0:T(2,128)}, bf16[2,256,1152]{2,1,0:T(8,128)(2,1)}, bf16[2,256,2304...) custom-call(s32[2]{0:T(128)} %get-tuple-element.468.index_ref, ...), custom_call_target="tpu_custom_call", output_to_operand_aliasing={{1}: (12, {}), {2}: (13, {}), {3}: (14, {}), {4}: (15, {}),... | custom-call | flops 1000 | bytes 1000 | tf_op jit(solution)/shard_map/mlp_back/pallas_call | solution.py:311
  191.0 19.6 %attn_back.6 = (bf16[256,1152]{1,0:T(8,128)(2,1)}, bf16[2,256,1152]{2,1,0:T(8,128)(2,1)}, f32[2,8,1152]{2,1,0:T(8,128)}, f32[2,8,576]{2,1,0:T(8,128)}, bf16[2,25...) custom-call(s32[2]{0:T(128)} %get-tuple-element.468.index_ref, ...), custom_call_target="tpu_custom_call", output_to_operand_aliasing={{1}: (11, {}), {2}: (12, {}), {3}: (13, {}), {4}: (14, {}),... | custom-call | flops 1000 | bytes 1000 | tf_op jit(solution)/shard_map/attn_back/pallas_call | solution.py:422
  213.7 16.2 %mlp_back.7 = (f32[256,1152]{1,0:T(8,128)}, f32[2,8,1152]{2,1,0:T(8,128)}, f32[2,2,2304]{2,1,0:T(2,128)}, bf16[2,256,1152]{2,1,0:T(8,128)(2,1)}, bf16[2,256,2304...) custom-call(s32[2]{0:T(128)} %get-tuple-element.467.index_ref, ...), custom_call_target="tpu_custom_call", output_to_operand_aliasing={{1}: (12, {}), {2}: (13, {}), {3}: (14, {}), {4}: (15, {}),... | custom-call | flops 1000 | bytes 1000 | tf_op jit(solution)/shard_map/mlp_back/pallas_call | solution.py:311
  229.8 7.9 %product.4.rest_0_ = bf16[2304,1152]{1,0:T(8,128)(2,1)} custom-call(bf16[2,256,2304]{2,1,0:T(8,128)(2,1)} %get-tuple-element.292.left_ref, bf16[2,256,1152]{2,1,0:T(8,128)(2,1)} %get-tuple-element.291.right_ref), custom_call_target="tpu_custom_call" | custom-call | flops 1000 | bytes 1000 | tf_op jit(solution)/shard_map/product/pallas_call | solution.py:612
  237.7 6.6 %product.5.rest_1_ = bf16[1152,2304]{1,0:T(8,128)(2,1)} custom-call(bf16[2,256,1152]{2,1,0:T(8,128)(2,1)} %get-tuple-element.293.left_ref, bf16[2,256,2304]{2,1,0:T(8,128)(2,1)} %get-tuple-element.294.right_ref, bf16[2304,1152]{1,0:T(8,128)(2,1)} %product.4.rest_0_), custom_call_target="tpu_custom_call" | custom-call | flops 1000 | bytes 1000 | tf_op jit(solution)/shard_map/product/pallas_call | solution.py:612
  246.8 9.0 %product.6.rest_1_ = bf16[2304,1152]{1,0:T(8,128)(2,1)} custom-call(bf16[2,256,2304]{2,1,0:T(8,128)(2,1)} %get-tuple-element.290.left_ref, bf16[2,256,1152]{2,1,0:T(8,128)(2,1)} %get-tuple-element.291.right_ref, bf16[2304,1152]{1,0:T(8,128)(2,1)} %collective-permute-done.13.rest_0_, bf16[1152,2304]{1,0:T(8,128)(2,1)} %product.5.rest_1_), custom_call_target="tpu_custom_call" | custom-call | flops 1000 | bytes 1000 | tf_op jit(solution)/shard_map/product/pallas_call | solution.py:612
  260.2 8.6 %product.7.rest_2_.rest_11_ = bf16[1152,2304]{1,0:T(8,128)(2,1)} custom-call(bf16[2,256,1152]{2,1,0:T(8,128)(2,1)} %get-tuple-element.293.left_ref, bf16[2,256,2304]{2,1,0:T(8,128)(2,1)} %get-tuple-element.295.right_ref, bf16[1152,2304]{1,0:T(8,128)(2,1)} %collective-permute-done.16.rest_0_, bf16[2304,1152]{1,0:T(8,128)(2,1)} %product.6.rest_1_), custom_call_target="tpu_custom_call" | custom-call | flops 1000 | bytes 1000 | tf_op jit(solution)/shard_map/product/pallas_call | solution.py:612
  277.0 19.5 %attn_back.7 = (bf16[256,1152]{1,0:T(8,128)(2,1)}, bf16[2,256,1152]{2,1,0:T(8,128)(2,1)}, f32[2,8,1152]{2,1,0:T(8,128)}, f32[2,8,576]{2,1,0:T(8,128)}, bf16[2,25...) custom-call(s32[2]{0:T(128)} %get-tuple-element.467.index_ref, ...), custom_call_target="tpu_custom_call", output_to_operand_aliasing={{1}: (11, {}), {2}: (12, {}), {3}: (13, {}), {4}: (14, {}),... | custom-call | flops 1000 | bytes 1000 | tf_op jit(solution)/shard_map/attn_back/pallas_call | solution.py:422
  303.2 7.7 %attn_product.2.rest_2_ = bf16[2304,1152]{1,0:T(8,128)(2,1)} custom-call(bf16[3,2,256,576]{3,2,1,0:T(8,128)(2,1)} %get-tuple-element.304.qg_ref, bf16[2,256,1152]{2,1,0:T(8,128)(2,1)} %get-tuple-element.305.h_ref, bf16[2,2,256,576]{3,2,1,0:T(8,128)(2,1)} %get-tuple-element.306.att_ref, bf16[2,256,1152]{2,1,0:T(8,128)(2,1)} %get-tuple-element.307.oi_ref, ...), custom_call_target="tpu_custom_call" | custom-call | flops 1000 | bytes 1000 | tf_op jit(solution)/shard_map/attn_product/pallas_call | solution.py:649
  315.1 6.5 %collective-permute-done.19.rest_0_ = bf16[72,2304]{1,0:T(8,128)(2,1)S(1)} collective-permute-done((bf16[72,2304]{1,0:T(8,128)(2,1)S(1)}, bf16[72,2304]{1,0:T(8,128)(2,1)S(1)}, u32[]{:S(2)}, u32[]{:S(2)}) %collective-permute-start.19) | collective-permute-done | bytes 331808 | tf_op jit(solution)/shard_map/ppermute | solution.py:550
  335.5 8.6 %attn_product.3.rest_2_ = bf16[2304,1152]{1,0:T(8,128)(2,1)} custom-call(bf16[3,2,256,576]{3,2,1,0:T(8,128)(2,1)} %get-tuple-element.314.qg_ref, bf16[2,256,1152]{2,1,0:T(8,128)(2,1)} %get-tuple-element.305.h_ref, bf16[2,2,256,576]{3,2,1,0:T(8,128)(2,1)} %get-tuple-element.306.att_ref, bf16[2,256,1152]{2,1,0:T(8,128)(2,1)} %get-tuple-element.307.oi_ref, ...), custom_call_target="tpu_custom_call" | custom-call | flops 1000 | bytes 1000 | tf_op jit(solution)/shard_map/attn_product/pallas_call | solution.py:649
  371.5 5.4 fusion
  397.7 6.9 %collective-permute-done.42.rest_0_ = bf16[144,1152]{1,0:T(8,128)(2,1)S(1)} collective-permute-done((bf16[144,1152]{1,0:T(8,128)(2,1)}, bf16[144,1152]{1,0:T(8,128)(2,1)S(1)}, u32[]{:S(2)}, u32[]{:S(2)}) %collective-permute-start.42) | collective-permute-done | bytes 331808 | tf_op jit(solution)/shard_map/ppermute | solution.py:550
  415.4 7.2 %collective-permute-done.48.rest_0_ = bf16[144,1152]{1,0:T(8,128)(2,1)S(1)} collective-permute-done((bf16[144,1152]{1,0:T(8,128)(2,1)}, bf16[144,1152]{1,0:T(8,128)(2,1)S(1)}, u32[]{:S(2)}, u32[]{:S(2)}) %collective-permute-start.48) | collective-permute-done | bytes 331808 | tf_op jit(solution)/shard_map/ppermute | solution.py:550
  473.6 4.7 collective-permute-done.64.rest_0_
  480.7 6.3 collective-permute-done.65.rest_1_
  493.4 5.0 collective-permute-start.85
  512.8 5.0 collective-permute-start.80
  523.8 7.1 %collective-permute-start.81 = (bf16[144,1152]{1,0:T(8,128)(2,1)S(1)}, bf16[144,1152]{1,0:T(8,128)(2,1)S(1)}, u32[]{:S(2)}, u32[]{:S(2)}) collective-permute-start(bf16[144,1152]{1,0:T(8,128)(2,1)S(1)} %copy-done.9), channel_id=1, source_target_pairs={{4,0},{8,4},{12,8},{14,12},{10,14},{6,10},{2,6},{0,2},{5,1},{9,5},... | collective-permute-start | bytes 995336 | tf_op jit(solution)/shard_map/ppermute | solution.py:550
  534.6 5.1 collective-permute-start.70
  545.0 4.8 collective-permute-start.96
  567.5 4.8 collective-permute-done.72.rest_8_
  574.8 4.7 ring_write.8
  599.0 9.1 %convolution_bitcast_fusion = f32[1,1152,3456]{2,1,0:T(8,128)} fusion(bf16[32,1152]{1,0:T(8,128)(2,1)} %reshape.115, bf16[32,3456]{1,0:T(8,128)(2,1)S(1)} %reshape.116), kind=kOutput, calls=%fused_computation.1 | convolution fusion | flops 254803968 | bytes 16220160 | tf_op jit(solution)/shard_map/sd,sk->dk/dot_general | solution.py:808
  (493 shorter events, 296.5 us)
Async XLA Ops:
  0.7 27.6 %collective-permute-start.5 = (bf16[1152,2304]{1,0:T(8,128)(2,1)}, bf16[1152,2304]{1,0:T(8,128)(2,1)}, u32[]{:S(2)}, u32[]{:S(2)}) collective-permute-start(bf16[1152,2304]{1,0:T(8,128)(2,1)} %bitcast.87), channel_id=1, source_target_pairs={{0,1},{1,0},{2,3},{3,2},{4,5},{5,4},{6,7},{7,6},{8,9},{9,8},{10,11... | collective-permute-start | bytes 15925256 | tf_op jit(solution)/shard_map/ppermute | solution.py:446
  1.2 27.0 %collective-permute-start.6 = (bf16[2304,1152]{1,0:T(8,128)(2,1)}, bf16[2304,1152]{1,0:T(8,128)(2,1)}, u32[]{:S(2)}, u32[]{:S(2)}) collective-permute-start(bf16[2304,1152]{1,0:T(8,128)(2,1)} %bitcast.96), channel_id=1, source_target_pairs={{0,1},{1,0},{2,3},{3,2},{4,5},{5,4},{6,7},{7,6},{8,9},{9,8},{10,11... | collective-permute-start | bytes 15925256 | tf_op jit(solution)/shard_map/ppermute | solution.py:446
  25.6 55.3 %collective-permute-start.10 = (bf16[128,2304]{1,0:T(8,128)(2,1)}, bf16[128,2304]{1,0:T(8,128)(2,1)}, u32[]{:S(2)}, u32[]{:S(2)}) collective-permute-start(bf16[128,2304]{1,0:T(8,128)(2,1)} %get-tuple-element.435), channel_id=1, source_target_pairs={{0,1},{1,0},{2,3},{3,2},{4,5},{5,4},{6,7},{7,6},{8,9},{9,8},{10,11... | collective-permute-start | bytes 1769480 | tf_op jit(solution)/shard_map/ppermute | solution.py:446
  52.7 29.3 %collective-permute-start.8 = (bf16[256,1152]{1,0:T(8,128)(2,1)}, bf16[256,1152]{1,0:T(8,128)(2,1)S(1)}, u32[]{:S(2)}, u32[]{:S(2)}) collective-permute-start(bf16[256,1152]{1,0:T(8,128)(2,1)} %get-tuple-element.216), channel_id=1, source_target_pairs={{0,16},{1,17},{2,18},{3,19},{4,20},{5,21},{6,22},{7,23},{8,24},{9,... | collective-permute-start | bytes 1769480 | tf_op jit(solution)/shard_map/ppermute | solution.py:732
  110.0 65.1 %collective-permute-start.12 = (bf16[256,1152]{1,0:T(8,128)(2,1)}, bf16[256,1152]{1,0:T(8,128)(2,1)}, u32[]{:S(2)}, u32[]{:S(2)}) collective-permute-start(bf16[256,1152]{1,0:T(8,128)(2,1)} %get-tuple-element.265), channel_id=1, source_target_pairs={{16,0},{17,1},{18,2},{19,3},{20,4},{21,5},{22,6},{23,7},{24,8},{25... | collective-permute-start | bytes 1769480 | tf_op jit(solution)/shard_map/ppermute | solution.py:768
  124.0 88.8 %collective-permute-start.11 = (bf16[256,1152]{1,0:T(8,128)(2,1)}, bf16[256,1152]{1,0:T(8,128)(2,1)S(1)}, u32[]{:S(2)}, u32[]{:S(2)}) collective-permute-start(bf16[256,1152]{1,0:T(8,128)(2,1)} %get-tuple-element.264), channel_id=1, source_target_pairs={{16,0},{17,1},{18,2},{19,3},{20,4},{21,5},{22,6},{23,7},{24,8},{25... | collective-permute-start | bytes 1769480 | tf_op jit(solution)/shard_map/ppermute | solution.py:768
  269.9 26.7 %collective-permute-start.17 = (bf16[72,2304]{1,0:T(8,128)(2,1)S(1)}, bf16[72,2304]{1,0:T(8,128)(2,1)S(1)}, u32[]{:S(2)}, u32[]{:S(2)}) collective-permute-start(bf16[72,2304]{1,0:T(8,128)(2,1)S(1)} %get-tuple-element.429), channel_id=1, source_target_pairs={{0,4},{4,8},{8,12},{12,14},{14,10},{10,6},{6,2},{2,0},{1,5},{5,9},... | collective-permute-start | bytes 995336 | tf_op jit(solution)/shard_map/ppermute | solution.py:550
  271.9 24.7 %collective-permute-start.18 = (bf16[72,2304]{1,0:T(8,128)(2,1)S(1)}, bf16[72,2304]{1,0:T(8,128)(2,1)S(1)}, u32[]{:S(2)}, u32[]{:S(2)}) collective-permute-start(bf16[72,2304]{1,0:T(8,128)(2,1)S(1)} %get-tuple-element.428), channel_id=1, source_target_pairs={{4,0},{8,4},{12,8},{14,12},{10,14},{6,10},{2,6},{0,2},{5,1},{9,5},... | collective-permute-start | bytes 995336 | tf_op jit(solution)/shard_map/ppermute | solution.py:550
  274.9 24.6 %collective-permute-start.21 = (bf16[144,1152]{1,0:T(8,128)(2,1)}, bf16[144,1152]{1,0:T(8,128)(2,1)S(1)}, u32[]{:S(2)}, u32[]{:S(2)}) collective-permute-start(bf16[144,1152]{1,0:T(8,128)(2,1)} %get-tuple-element.308), channel_id=1, source_target_pairs={{0,4},{4,8},{8,12},{12,14},{14,10},{10,6},{6,2},{2,0},{1,5},{5,9},... | collective-permute-start | bytes 995336 | tf_op jit(solution)/shard_map/ppermute | solution.py:550
  276.9 22.7 %collective-permute-start.22 = (bf16[144,1152]{1,0:T(8,128)(2,1)}, bf16[144,1152]{1,0:T(8,128)(2,1)S(1)}, u32[]{:S(2)}, u32[]{:S(2)}) collective-permute-start(bf16[144,1152]{1,0:T(8,128)(2,1)} %get-tuple-element.309), channel_id=1, source_target_pairs={{4,0},{8,4},{12,8},{14,12},{10,14},{6,10},{2,6},{0,2},{5,1},{9,5},... | collective-permute-start | bytes 995336 | tf_op jit(solution)/shard_map/ppermute | solution.py:550
  311.0 24.6 %collective-permute-start.25 = (bf16[2304,1152]{1,0:T(8,128)(2,1)}, bf16[2304,1152]{1,0:T(8,128)(2,1)}, u32[]{:S(2)}, u32[]{:S(2)}) collective-permute-start(bf16[2304,1152]{1,0:T(8,128)(2,1)} %attn_product.2.rest_2_), channel_id=1, source_target_pairs={{0,1},{1,0},{2,3},{3,2},{4,5},{5,4},{6,7},{7,6},{8,9},{9,8},{10,11... | collective-permute-start | bytes 15925256 | tf_op jit(solution)/shard_map/ppermute | solution.py:446
  333.5 21.5 %collective-permute-start.40 = (bf16[144,1152]{1,0:T(8,128)(2,1)}, bf16[144,1152]{1,0:T(8,128)(2,1)S(1)}, u32[]{:S(2)}, u32[]{:S(2)}) collective-permute-start(bf16[144,1152]{1,0:T(8,128)(2,1)} %get-tuple-element.328), channel_id=1, source_target_pairs={{0,4},{4,8},{8,12},{12,14},{14,10},{10,6},{6,2},{2,0},{1,5},{5,9},... | collective-permute-start | bytes 995336 | tf_op jit(solution)/shard_map/ppermute | solution.py:550
  335.1 21.5 %collective-permute-start.41 = (bf16[144,1152]{1,0:T(8,128)(2,1)}, bf16[144,1152]{1,0:T(8,128)(2,1)S(1)}, u32[]{:S(2)}, u32[]{:S(2)}) collective-permute-start(bf16[144,1152]{1,0:T(8,128)(2,1)} %get-tuple-element.329), channel_id=1, source_target_pairs={{4,0},{8,4},{12,8},{14,12},{10,14},{6,10},{2,6},{0,2},{5,1},{9,5},... | collective-permute-start | bytes 995336 | tf_op jit(solution)/shard_map/ppermute | solution.py:550
  347.8 23.3 %collective-permute-start.46 = (bf16[72,2304]{1,0:T(8,128)(2,1)}, bf16[72,2304]{1,0:T(8,128)(2,1)S(1)}, u32[]{:S(2)}, u32[]{:S(2)}) collective-permute-start(bf16[72,2304]{1,0:T(8,128)(2,1)} %get-tuple-element.319), channel_id=1, source_target_pairs={{0,4},{4,8},{8,12},{12,14},{14,10},{10,6},{6,2},{2,0},{1,5},{5,9},... | collective-permute-start | bytes 995336 | tf_op jit(solution)/shard_map/ppermute | solution.py:550
  349.5 27.5 %collective-permute-start.47 = (bf16[72,2304]{1,0:T(8,128)(2,1)}, bf16[72,2304]{1,0:T(8,128)(2,1)S(1)}, u32[]{:S(2)}, u32[]{:S(2)}) collective-permute-start(bf16[72,2304]{1,0:T(8,128)(2,1)} %get-tuple-element.320), channel_id=1, source_target_pairs={{4,0},{8,4},{12,8},{14,12},{10,14},{6,10},{2,6},{0,2},{5,1},{9,5},... | collective-permute-start | bytes 995336 | tf_op jit(solution)/shard_map/ppermute | solution.py:550
  384.4 26.4 %collective-permute-start.50 = (bf16[144,1152]{1,0:T(8,128)(2,1)}, bf16[144,1152]{1,0:T(8,128)(2,1)S(1)}, u32[]{:S(2)}, u32[]{:S(2)}) collective-permute-start(bf16[144,1152]{1,0:T(8,128)(2,1)} %get-tuple-element.340), channel_id=1, source_target_pairs={{0,4},{4,8},{8,12},{12,14},{14,10},{10,6},{6,2},{2,0},{1,5},{5,9},... | collective-permute-start | bytes 995336 | tf_op jit(solution)/shard_map/ppermute | solution.py:550
  404.6 22.4 %collective-permute-start.58 = (bf16[72,2304]{1,0:T(8,128)(2,1)}, bf16[72,2304]{1,0:T(8,128)(2,1)S(1)}, u32[]{:S(2)}, u32[]{:S(2)}) collective-permute-start(bf16[72,2304]{1,0:T(8,128)(2,1)} %get-tuple-element.352), channel_id=1, source_target_pairs={{0,4},{4,8},{8,12},{12,14},{14,10},{10,6},{6,2},{2,0},{1,5},{5,9},... | collective-permute-start | bytes 995336 | tf_op jit(solution)/shard_map/ppermute | solution.py:550
  406.3 21.3 %collective-permute-start.59 = (bf16[72,2304]{1,0:T(8,128)(2,1)}, bf16[72,2304]{1,0:T(8,128)(2,1)S(1)}, u32[]{:S(2)}, u32[]{:S(2)}) collective-permute-start(bf16[72,2304]{1,0:T(8,128)(2,1)} %get-tuple-element.353), channel_id=1, source_target_pairs={{4,0},{8,4},{12,8},{14,12},{10,14},{6,10},{2,6},{0,2},{5,1},{9,5},... | collective-permute-start | bytes 995336 | tf_op jit(solution)/shard_map/ppermute | solution.py:550
  412.1 33.0 %collective-permute-start.33 = (bf16[1,39176]{1,0:T(2,128)(2,1)S(1)}, bf16[1,39176]{1,0:T(2,128)(2,1)S(1)}, u32[]{:S(2)}, u32[]{:S(2)}) collective-permute-start(bf16[1,39176]{1,0:T(2,128)(2,1)S(1)} %broadcast_in_dim.59), channel_id=1, source_target_pairs={{0,2},{2,0},{4,6},{6,4},{8,10},{10,8},{12,14},{14,12},{1,3},{3,1},... | collective-permute-start | bytes 235064 | tf_op jit(solution)/shard_map/ppermute | solution.py:460
  433.6 28.4 %collective-permute-start.28 = (bf16[2,128,1152]{2,1,0:T(8,128)(2,1)}, bf16[2,128,1152]{2,1,0:T(8,128)(2,1)S(1)}, u32[]{:S(2)}, u32[]{:S(2)}) collective-permute-start(bf16[2,128,1152]{2,1,0:T(8,128)(2,1)} %get-tuple-element.433), channel_id=1, source_target_pairs={{0,1},{1,0},{2,3},{3,2},{4,5},{5,4},{6,7},{7,6},{8,9},{9,8},{10,11... | collective-permute-start | bytes 1769480 | tf_op jit(solution)/shard_map/ppermute | solution.py:446
  462.0 31.4 %collective-permute-start.83 = (bf16[72,2304]{1,0:T(8,128)(2,1)S(1)}, bf16[72,2304]{1,0:T(8,128)(2,1)S(1)}, u32[]{:S(2)}, u32[]{:S(2)}) collective-permute-start(bf16[72,2304]{1,0:T(8,128)(2,1)S(1)} %copy-done.5), channel_id=1, source_target_pairs={{4,0},{8,4},{12,8},{14,12},{10,14},{6,10},{2,6},{0,2},{5,1},{9,5},... | collective-permute-start | bytes 995336 | tf_op jit(solution)/shard_map/ppermute | solution.py:550
  464.1 34.3 %collective-permute-start.76 = (bf16[144,1152]{1,0:T(8,128)(2,1)S(1)}, bf16[144,1152]{1,0:T(8,128)(2,1)}, u32[]{:S(2)}, u32[]{:S(2)}) collective-permute-start(bf16[144,1152]{1,0:T(8,128)(2,1)S(1)} %collective-permute-done.74.rest_2_), channel_id=1, source_target_pairs={{0,4},{4,8},{8,12},{12,14},{14,10},{10,6},{6,2},{2,0},{1,5},{5,9},... | collective-permute-start | bytes 995336 | tf_op jit(solution)/shard_map/ppermute | solution.py:550
  469.0 29.4 %collective-permute-start.77 = (bf16[144,1152]{1,0:T(8,128)(2,1)S(1)}, bf16[144,1152]{1,0:T(8,128)(2,1)}, u32[]{:S(2)}, u32[]{:S(2)}) collective-permute-start(bf16[144,1152]{1,0:T(8,128)(2,1)S(1)} %collective-permute-done.75.rest_3_), channel_id=1, source_target_pairs={{4,0},{8,4},{12,8},{14,12},{10,14},{6,10},{2,6},{0,2},{5,1},{9,5},... | collective-permute-start | bytes 995336 | tf_op jit(solution)/shard_map/ppermute | solution.py:550
  471.3 32.9 %collective-permute-start.84 = (bf16[72,2304]{1,0:T(8,128)(2,1)S(1)}, bf16[72,2304]{1,0:T(8,128)(2,1)S(1)}, u32[]{:S(2)}, u32[]{:S(2)}) collective-permute-start(bf16[72,2304]{1,0:T(8,128)(2,1)S(1)} %collective-permute-done.82.rest_2_), channel_id=1, source_target_pairs={{0,4},{4,8},{8,12},{12,14},{14,10},{10,6},{6,2},{2,0},{1,5},{5,9},... | collective-permute-start | bytes 995336 | tf_op jit(solution)/shard_map/ppermute | solution.py:550
  534.6 23.3 %collective-permute-start.70 = (bf16[144,1152]{1,0:T(8,128)(2,1)}, bf16[144,1152]{1,0:T(8,128)(2,1)S(1)}, u32[]{:S(2)}, u32[]{:S(2)}) collective-permute-start(bf16[144,1152]{1,0:T(8,128)(2,1)} %collective-permute-done.68.rest_4_), channel_id=1, source_target_pairs={{0,4},{4,8},{8,12},{12,14},{14,10},{10,6},{6,2},{2,0},{1,5},{5,9},... | collective-permute-start | bytes 995336 | tf_op jit(solution)/shard_map/ppermute | solution.py:550
  554.4 25.6 %collective-permute-start.102 = (bf16[72,2304]{1,0:T(8,128)(2,1)S(1)}, bf16[72,2304]{1,0:T(8,128)(2,1)S(1)}, u32[]{:S(2)}, u32[]{:S(2)}) collective-permute-start(bf16[72,2304]{1,0:T(8,128)(2,1)S(1)} %get-tuple-element.382), channel_id=1, source_target_pairs={{0,4},{4,8},{8,12},{12,14},{14,10},{10,6},{6,2},{2,0},{1,5},{5,9},... | collective-permute-start | bytes 995336 | tf_op jit(solution)/shard_map/ppermute | solution.py:550
  560.5 26.7 %collective-permute-start.103 = (bf16[72,2304]{1,0:T(8,128)(2,1)}, bf16[72,2304]{1,0:T(8,128)(2,1)S(1)}, u32[]{:S(2)}, u32[]{:S(2)}) collective-permute-start(bf16[72,2304]{1,0:T(8,128)(2,1)} %get-tuple-element.383), channel_id=1, source_target_pairs={{4,0},{8,4},{12,8},{14,12},{10,14},{6,10},{2,6},{0,2},{5,1},{9,5},... | collective-permute-start | bytes 995336 | tf_op jit(solution)/shard_map/ppermute | solution.py:550
  563.2 24.1 %collective-permute-start.98 = (bf16[144,1152]{1,0:T(8,128)(2,1)S(1)}, bf16[144,1152]{1,0:T(8,128)(2,1)S(1)}, u32[]{:S(2)}, u32[]{:S(2)}) collective-permute-start(bf16[144,1152]{1,0:T(8,128)(2,1)S(1)} %collective-permute-done.96.rest_0_), channel_id=1, source_target_pairs={{0,4},{4,8},{8,12},{12,14},{14,10},{10,6},{6,2},{2,0},{1,5},{5,9},... | collective-permute-start | bytes 995336 | tf_op jit(solution)/shard_map/ppermute | solution.py:550
  587.3 25.0 %collective-permute-start.105 = (bf16[72,2304]{1,0:T(8,128)(2,1)S(1)}, bf16[72,2304]{1,0:T(8,128)(2,1)}, u32[]{:S(2)}, u32[]{:S(2)}) collective-permute-start(bf16[72,2304]{1,0:T(8,128)(2,1)S(1)} %collective-permute-done.103.rest_1_), channel_id=1, source_target_pairs={{4,0},{8,4},{12,8},{14,12},{10,14},{6,10},{2,6},{0,2},{5,1},{9,5},... | collective-permute-start | bytes 995336 | tf_op jit(solution)/shard_map/ppermute | solution.py:550
  589.5 22.8 %collective-permute-start.100 = (bf16[144,1152]{1,0:T(8,128)(2,1)S(1)}, bf16[144,1152]{1,0:T(8,128)(2,1)}, u32[]{:S(2)}, u32[]{:S(2)}) collective-permute-start(bf16[144,1152]{1,0:T(8,128)(2,1)S(1)} %collective-permute-done.98.rest_2_), channel_id=1, source_target_pairs={{0,4},{4,8},{8,12},{12,14},{14,10},{10,6},{6,2},{2,0},{1,5},{5,9},... | collective-permute-start | bytes 995336 | tf_op jit(solution)/shard_map/ppermute | solution.py:550
  591.7 23.0 %collective-permute-start.92 = (bf16[144,1152]{1,0:T(8,128)(2,1)S(1)}, bf16[144,1152]{1,0:T(8,128)(2,1)S(1)}, u32[]{:S(2)}, u32[]{:S(2)}) collective-permute-start(bf16[144,1152]{1,0:T(8,128)(2,1)S(1)} %collective-permute-done.90.rest_0_), channel_id=1, source_target_pairs={{0,4},{4,8},{8,12},{12,14},{14,10},{10,6},{6,2},{2,0},{1,5},{5,9},... | collective-permute-start | bytes 995336 | tf_op jit(solution)/shard_map/ppermute | solution.py:550
  591.7 23.0 %collective-permute-start.93 = (bf16[144,1152]{1,0:T(8,128)(2,1)S(1)}, bf16[144,1152]{1,0:T(8,128)(2,1)}, u32[]{:S(2)}, u32[]{:S(2)}) collective-permute-start(bf16[144,1152]{1,0:T(8,128)(2,1)S(1)} %collective-permute-done.91.rest_1_), channel_id=1, source_target_pairs={{4,0},{8,4},{12,8},{14,12},{10,14},{6,10},{2,6},{0,2},{5,1},{9,5},... | collective-permute-start | bytes 995336 | tf_op jit(solution)/shard_map/ppermute | solution.py:550
  (159 other events, 1518.1 us)
